TPU v7x, 256 devices: a whole 4x4x8 slice. The times are simulated.
256 devices in a mesh: grp: 2 (over z_hi), dev: 128 (over y, z_lo, x, core).
Axes of the slice: x: 4, y: 4, z: 8 (z_hi: 2, z_lo: 4; z = z_hi * 4 + z_lo), core: 2. Of those that a mesh axis runs over, the one named last changes fastest.
Arguments:
- state: float32 [2, 3, 16777216], P('grp', None, 'dev'), may hold values from -6 to 6
- courant: float32 [16777216], P('dev'), may hold values from 0.25 to 1
- remesh: float32 [128, 128], replicated, may hold values from -0.5 to 0.5
- shell_dest: int32 [32768, 1], P('dev'), may hold values from 0 to 127; in each aligned block of 256 rows (0 to 255, 256 to 511, ...) at most 4 rows name the same one
- shell_row: int32 [32768], P('dev'), may hold values from 0 to 1023
- return_dest: int32 [32768, 1], P('dev'), may hold values from 0 to 127; in each aligned block of 256 rows (0 to 255, 256 to 511, ...) at most 4 rows name the same one
- return_row: int32 [32768], P('dev'), may hold values from 0 to 1023
- return_block: int32 [32768], P('dev'), may hold values from 0 to 15
Outputs:
- fields: float32 [2, 3, 16777216], P('grp', None, 'dev')
Inputs may be any that keep to these rules, and one draw needn't show every extreme that they name: `shell_dest`: among the rows of one device (256 aligned rows) no brick is named more than 4 times, a bound that some block reaches. `return_dest`: among the rows of one brick (256 aligned rows) no owner is named more than 4 times, a bound that some block reaches.
All inputs are finite; a program needn't handle non-finite values.
Results may differ from a plain program's by a relative error of at most 0.00027.
Values sent between devices are 32-bit elements; how exact they have to be, the bound alone decides.
No kernel may reach another device: no remote copies, remote signals or barrier semaphores. Data moves between devices by JAX's collectives and lax.ppermute only.
A program may use at most 64 MiB of HBM per device.

v0:
```python
import jax
import jax.numpy as jnp
import ml_dtypes
import numpy as np
from jax import lax
from jax.experimental import pallas as pl
from jax.experimental.pallas import tpu as pltpu
from jax.sharding import Mesh
from jax.sharding import PartitionSpec as P

NX, NY, NZ = 512, 256, 128
NI, NK = 64, 128
NJ = 16
CY, CZ, CX, CC = 4, 4, 4, 2
BRICKS = 128
CAP = 4
SB = 256
RPB = 1024
TARGETS = CY * CX * CC
GROUP = CZ * CAP
SLOTS = BRICKS * CAP
DEV = ("y", "z", "x", "core")
ALL = ("grp",) + DEV

viscosity = 0.2
coupling = 1.0
f32 = jnp.float32
bf16 = jnp.bfloat16
i32 = jnp.int32
highest = lax.Precision.HIGHEST
NT = (((1,), (1,)), ((), ()))


def sines(length):
    counts = np.arange(length) + 1
    phase = counts[:, None] * counts[None, :] % (2 * (length + 1))
    return np.sin(np.pi * phase / (length + 1))


def eigen(length):
    counts = np.arange(length) + 1.0
    return 4.0 * np.sin(0.5 * np.pi * counts / (length + 1)) ** 2


def halves(table):
    table = table.astype(np.float32)
    high = table.astype(ml_dtypes.bfloat16)
    low = (table - high.astype(np.float32)).astype(ml_dtypes.bfloat16)
    return high, low


def paired(table):
    high, low = halves(table)
    return np.block([[high, low], [high, np.zeros_like(low)]]).astype(ml_dtypes.bfloat16)


def line_table():
    dev = np.arange(BRICKS)
    plane = np.where(dev % 2 == 1, 4 * dev + 3, 4 * dev - 1) + 1
    phase = (np.arange(NX) + 1)[:, None] * plane[None, :] % (2 * (NX + 1))
    return np.sin(np.pi * phase / (NX + 1))


def iota(shape, axis):
    return lax.broadcasted_iota(i32, shape, axis)


def split(value):
    high = value.astype(bf16)
    return high, (value - high.astype(f32)).astype(bf16)


def mm(a, b):
    return jnp.dot(a, b, preferred_element_type=f32)


def lanes_paired(value):
    return jnp.concatenate(split(value), axis=1)


def fold(value):
    half = value.shape[1] // 2
    return value[:, :half] + value[:, half:]


def pick(onehot, value):
    return fold(mm(onehot, lanes_paired(value)))


def times_paired(value, table):
    return fold(mm(lanes_paired(value), table))


def table_times(high, low, value):
    vh, vl = split(value)
    return mm(high, vh) + mm(high, vl) + mm(low, vh)


def exact(a, b, dims=(((1,), (0,)), ((), ()))):
    return lax.dot_general(a, b, dims, precision=highest, preferred_element_type=f32)


def onehot(condition):
    return jnp.where(condition, 1.0, 0.0).astype(bf16)


def ranks(matches):
    size = matches.shape[1]
    before = onehot(iota((size, size), 0) < iota((size, size), 1))
    counts = mm(matches.astype(bf16), before)
    return jnp.sum(matches * counts, axis=0, keepdims=True).astype(i32)


def route_kernel(flags, sd, sr, rd, rr, rb, remesh, sz, place, gather, codes, merged):
    zme = flags[3]
    bricks = iota((BRICKS, SB), 0)
    matches = jnp.where(bricks == sd[...], 1.0, 0.0)
    rank = ranks(matches)
    slot = rank * BRICKS + sd[...]
    place[...] = onehot(iota((SLOTS, SB), 0) == slot)
    tagged = jnp.where(bricks == rank, (sr[...] + 1).astype(f32), 0.0)
    sent = exact(matches, tagged, NT)
    owner = rd[...]
    oc = owner & (CC - 1)
    ox = (owner >> 1) & (CX - 1)
    oz = (owner >> 3) & (CZ - 1)
    oy = owner >> 5
    rank = ranks(jnp.where(bricks == owner, 1.0, 0.0))
    lane = oz * CAP + rank
    slot = ((oy * CX + ox) * CC + oc) * GROUP + lane
    gather[...] = lax.dot_general(
        onehot(iota((SLOTS, SB), 0) == slot),
        onehot(iota((RPB, SB), 0) == rr[...]),
        NT,
        preferred_element_type=f32,
    ).astype(bf16)
    via = ((oy * CZ + zme) * CX + ox) * CC + oc
    code = ((oz - zme) & (CZ - 1)) * NJ + rb[...] + 1
    tagged = jnp.where(bricks == lane + CAP, code.astype(f32), 0.0)
    codes[...] = sent + exact(jnp.where(bricks == via, 1.0, 0.0), tagged, NT)
    both = exact(remesh[...], sz[...])
    high, low = split(both)
    merged[...] = jnp.concatenate(
        [
            jnp.concatenate([high, low], axis=1),
            jnp.concatenate([high, jnp.zeros_like(low)], axis=1),
        ],
        axis=0,
    )


def decode_kernel(flags, codes, spread, cells):
    zme = flags[3]
    turned = codes[...].T
    rows = jnp.concatenate([turned[i : i + 1, :] for i in range(CAP)], axis=1).astype(i32)
    spread[...] = onehot(iota((RPB, SLOTS), 0) == rows - 1)
    target = iota((TARGETS, BRICKS), 0)
    source = ((target >> 3) * CZ + zme) * (CX * CC) + (target & (CX * CC - 1))
    chosen = exact(jnp.where(iota((TARGETS, BRICKS), 1) == source, 1.0, 0.0), codes[...])
    wide = jnp.where(
        iota((BRICKS, SLOTS), 0) == (iota((BRICKS, SLOTS), 1) & (GROUP - 1)) + CAP, 1.0, 0.0
    )
    chosen = exact(chosen, wide)
    own = iota((TARGETS, SLOTS), 0) == (iota((TARGETS, SLOTS), 1) >> 4)
    code = jnp.sum(jnp.where(own, chosen, 0.0), axis=0, keepdims=True).astype(i32)
    cells[...] = onehot(iota((CZ * NJ, SLOTS), 0) == code - 1)


def near_kernel(flags, state, courant, up, down, out, layer):
    @pl.when(flags[0] == 0)
    def _():
        cr = jnp.concatenate([up[768:896, :], courant[...], down[768:896, :]], axis=0)

        def step(field, speed):
            rows = speed.shape[0]
            centre = field[128 : 128 + rows]
            transport = (
                8.0 * (field[192 : 192 + rows] - field[64 : 64 + rows])
                - (field[256 : 256 + rows] - field[:rows])
            ) / 12.0
            place = iota((rows, NK), 0) & (NI - 1)
            above = jnp.where(place == NI - 1, 0.0, pltpu.roll(centre, rows - 1, 0))
            below = jnp.where(place == 0, 0.0, pltpu.roll(centre, 1, 0))
            return centre - speed * transport + viscosity * (above - 2.0 * centre + below)

        for c in range(3):
            field = jnp.concatenate(
                [up[c * 256 : (c + 1) * 256, :], state[c], down[c * 256 : (c + 1) * 256, :]], axis=0
            )
            field = step(field, cr)
            out[c] = step(field, courant[...])
            layer[c] = state[c, pl.ds(NI - 1, NJ, stride=NI), :]


def bucket_kernel(blocks, place, merged, out):
    for c in range(3):
        moved = times_paired(blocks[c], merged[...])
        slots = pick(place[...], moved)
        for rank in range(CAP):
            out[pl.ds(c * CAP + rank, BRICKS, stride=3 * CAP), :] = slots[
                rank * BRICKS : (rank + 1) * BRICKS
            ]


def weights(beta):
    outer = beta * beta - 2.0
    g12 = 1.0 / outer
    g13 = g12 / beta
    g11 = (beta * beta - 1.0) * g13
    return g11, g12, g13


def forward_kernel(flags, received, spread, state, sz, syh, syl, mu, planes, outgoing, kept):
    beta = mu[...] + 2.0
    g11, g12, g13 = weights(beta)
    first = flags[1] == 0
    for c in range(3):
        rows = jnp.concatenate(
            [received[pl.ds(c * CAP + r, BRICKS, stride=3 * CAP), :] for r in range(CAP)], axis=0
        )
        field = pick(spread[...], rows) + times_paired(state[c], sz[...])
        field = jnp.concatenate([field[p * NY : (p + 1) * NY] for p in range(4)], axis=1)
        field = table_times(syh[...], syl[...], field)
        f0, f1, f2, f3 = (field[:, p * NZ : (p + 1) * NZ] for p in range(4))
        for p, plane in enumerate((f0, f1, f2, f3)):
            planes[c, p] = plane
        low = g11 * f0 + g12 * f1 + g13 * f2
        high = f3 + g13 * f0 + g12 * f1 + g11 * f2
        outgoing[c * NY : (c + 1) * NY, :] = jnp.where(first, high, low)
        kept[c * NY : (c + 1) * NY, :] = jnp.where(first, low, high)


def reduce_kernel(outgoing, incoming, kept, mu, out):
    g11, g12, g13 = weights(mu[...] + 2.0)
    ratio = g13 / (mu[...] + 2.0 - 2.0 * g11)
    for c in range(3):
        block = slice(c * NY, (c + 1) * NY)
        share = kept[block, :] + ratio * (outgoing[block, :] + incoming[block, :])
        for i in range(2):
            out[pl.ds(c * 2 + i, BRICKS, stride=6), :] = share[i * BRICKS : (i + 1) * BRICKS]


def line_kernel(flags, received, kh, kl, th, tl, lamx, mu, out):
    shares = jnp.concatenate([received[pl.ds(j, BRICKS, stride=6), :] for j in range(6)], axis=1)
    modes = table_times(kh[...], kl[...], shares)
    factors = []
    for i in range(2):
        row = mu[pl.ds(flags[2] + i * BRICKS, 1), :]
        factors.append((2.0 / (NX + 1)) / (lamx[...] + row))
    modes = modes * jnp.concatenate(factors * 3, axis=1)
    solved = table_times(th[...], tl[...], modes)
    for j in range(6):
        out[pl.ds(j, BRICKS, stride=6), :] = solved[:, j * NZ : (j + 1) * NZ]


def inverse_kernel(
    flags, planes, outgoing, incoming, own, other, advanced, gather, sz, syh, syl, mu, out, send
):
    @pl.when(flags[0] == 0)
    def _():
        out[...] = advanced[...]

    @pl.when(flags[0] != 0)
    def _():
        beta = mu[...] + 2.0
        g11, g12, g13 = weights(beta)
        inv = 1.0 / (beta - 2.0 * g11)
        first = flags[1] == 0
        inside = jnp.where(flags[2] == BRICKS - 1, 0.0, 1.0)
        potentials = []
        for c in range(3):

            def unpacked(ref):
                return jnp.concatenate(
                    [ref[pl.ds(c * 2 + i, BRICKS, stride=6), :] for i in range(2)], axis=0
                )

            block = slice(c * NY, (c + 1) * NY)
            a, b = unpacked(own), unpacked(other)
            before, after = jnp.where(first, a, b), jnp.where(first, b, a)
            middle = (outgoing[block, :] + incoming[block, :] + g13 * (before + after)) * inv
            left = jnp.where(first, before, middle)
            right = jnp.where(first, middle, after)
            f0, f1, f2, f3 = (planes[c, p] for p in range(4))
            u0 = g11 * (f0 + left) + g12 * f1 + g13 * (f2 + right)
            u1 = g12 * (f0 + left + beta * f1 + f2 + right)
            u2 = g13 * (f0 + left) + g12 * f1 + g11 * (f2 + right)
            stack = [u0, u1, u2, right]
            if c:
                stack = [left] + stack + [(beta * right - u2 - f3) * inside]
            field = table_times(syh[...], syl[...], jnp.concatenate(stack, axis=1))
            field = jnp.concatenate(
                [field[:, p * NZ : (p + 1) * NZ] for p in range(len(stack))], axis=0
            )
            potentials.append(times_paired(field, sz[...]))
        rows = iota((RPB, NZ), 0) & (NY - 1)
        lanes = iota((RPB, NZ), 1)

        def dy(field):
            upper = jnp.where(rows == NY - 1, 0.0, pltpu.roll(field, RPB - 1, 0))
            lower = jnp.where(rows == 0, 0.0, pltpu.roll(field, 1, 0))
            return (upper - lower) * 0.5

        def dz(field):
            upper = jnp.where(lanes == NZ - 1, 0.0, pltpu.roll(field, NZ - 1, 1))
            lower = jnp.where(lanes == 0, 0.0, pltpu.roll(field, 1, 1))
            return (upper - lower) * 0.5

        def dx(field):
            return (field[2 * NY : 2 * NY + RPB] - field[:RPB]) * 0.5

        px, py, pz = potentials[0], potentials[1][NY : NY + RPB], potentials[2][NY : NY + RPB]
        velocity = (
            dy(pz) - dz(py),
            dz(px) - dx(potentials[2]),
            dx(potentials[1]) - dy(px),
        )
        for c in range(3):
            out[c] = velocity[c]
            rows_out = pick(gather[...], velocity[c])
            send[:, c * GROUP : (c + 1) * GROUP, :] = rows_out.reshape(TARGETS, GROUP, NZ)


def cell_kernel(received, cells, out):
    for c in range(3):
        rows = received[:, c * GROUP : (c + 1) * GROUP, :].reshape(SLOTS, NZ)
        out[:, c * NJ : (c + 1) * NJ, :] = pick(cells[...], rows).reshape(CZ, NJ, NZ)


def close_kernel(flags, field, layer, remesh, b0, b1, b2, b3, out):
    out[...] = field[...]

    @pl.when(flags[0] == 0)
    def _():
        total = exact((b0[...] + b1[...]) + (b2[...] + b3[...]), remesh[...], NT)
        first = [total[c * NJ : (c + 1) * NJ] for c in range(3)]
        second = [layer[c] for c in range(3)]
        for c in range(3):
            d, e = (c + 1) % 3, (c + 2) % 3
            cross = first[d] * second[e] - first[e] * second[d]
            edge = pl.ds(NI - 1, NJ, stride=NI)
            out[c, edge, :] = field[c, edge, :] + coupling * cross


def call(kernel, outs, flags, *args):
    scalars = [] if flags is None else [flags]
    return pl.pallas_call(
        kernel,
        out_shape=[jax.ShapeDtypeStruct(s, d) for s, d in outs],
        in_specs=[pl.BlockSpec(memory_space=pltpu.SMEM)] * len(scalars)
        + [pl.BlockSpec(memory_space=pltpu.VMEM)] * len(args),
        out_specs=[pl.BlockSpec(memory_space=pltpu.VMEM)] * len(outs),
        name=kernel.__name__,
    )(*scalars, *args)


def place_of(g, y, z, x, c):
    return (((g * CY + y) * CZ + z) * CX + x) * CC + c


def chips():
    return [
        (y, z, x, c) for y in range(CY) for z in range(CZ) for x in range(CX) for c in range(CC)
    ]


def on_device(state, courant, remesh, shell_dest, shell_row, return_dest, return_row, return_block):
    dev = lax.axis_index(DEV)
    flags = jnp.stack(
        [lax.axis_index("grp"), lax.axis_index("core"), dev, lax.axis_index("z")]
    ).astype(i32)
    field = state.reshape(3, RPB, NZ)
    speed = courant.reshape(RPB, NK)
    sy, sz, line = sines(NY), sines(NZ), line_table()
    syh, syl = halves(sy)
    iyh, iyl = halves(sy * (2.0 / (NY + 1)))
    szp, izp = paired(sz), paired(sz * (2.0 / (NZ + 1)))
    kh, kl = halves(line)
    th, tl = np.ascontiguousarray(kh.T), np.ascontiguousarray(kl.T)
    lamx = eigen(NX).astype(np.float32)[:, None]
    mu = (eigen(NY)[:, None] + eigen(NZ)[None, :]).astype(np.float32)

    blocks = field.reshape(3, NJ, NI, NK)[:, :, NI - NI // 4 :, :].reshape(3, SB, NK)
    across = [(place_of(0, *q), place_of(1, *q)) for q in chips()]
    blocks = lax.ppermute(blocks, ALL, across)

    ahead = [(d, (d + 1) % BRICKS) for d in range(BRICKS)]
    last = jnp.concatenate([field[:, 768:, :].reshape(768, NK), speed[896:, :]], axis=0)
    lead = jnp.concatenate([field[:, :256, :].reshape(768, NK), speed[:128, :]], axis=0)
    up = lax.ppermute(last, ALL, ahead)
    down = lax.ppermute(lead, ALL, [(b, a) for a, b in ahead])

    rows = [
        v.reshape(1, SB) for v in (shell_dest, shell_row, return_dest, return_row, return_block)
    ]
    place, gather, codes, merged = call(
        route_kernel,
        [
            ((SLOTS, SB), bf16),
            ((SLOTS, RPB), bf16),
            ((BRICKS, NZ), f32),
            ((2 * NK, 2 * NZ), bf16),
        ],
        flags,
        *rows,
        remesh,
        sz.astype(np.float32),
    )
    codes = lax.all_to_all(codes.reshape(BRICKS, 1, NZ), DEV, 0, 0, tiled=True)
    spread, cells = call(
        decode_kernel,
        [((RPB, SLOTS), bf16), ((CZ * NJ, SLOTS), bf16)],
        flags,
        codes.reshape(BRICKS, NZ),
    )
    advanced, layer = call(
        near_kernel, [((3, RPB, NK), f32), ((3, NJ, NK), f32)], flags, field, speed, up, down
    )

    (bundle,) = call(bucket_kernel, [((3 * SLOTS, NZ), f32)], None, blocks, place, merged)
    bundle = lax.all_to_all(bundle.reshape(BRICKS, 3, CAP, NZ), DEV, 0, 0, tiled=True)
    planes, outgoing, kept = call(
        forward_kernel,
        [((3, 4, NY, NZ), f32), ((3 * NY, NZ), f32), ((3 * NY, NZ), f32)],
        flags,
        bundle.reshape(3 * SLOTS, NZ),
        spread,
        field,
        szp,
        syh,
        syl,
        mu,
    )
    swap = [(0, 1), (1, 0)]
    incoming = lax.ppermute(outgoing, "core", swap)
    (share,) = call(reduce_kernel, [((3 * NY, NZ), f32)], None, outgoing, incoming, kept, mu)
    share = lax.all_to_all(share.reshape(BRICKS, 3, 2, NZ), DEV, 0, 0, tiled=True)
    (solved,) = call(
        line_kernel,
        [((3 * NY, NZ), f32)],
        flags,
        share.reshape(3 * NY, NZ),
        kh,
        kl,
        th,
        tl,
        lamx,
        mu,
    )
    own = lax.all_to_all(solved.reshape(BRICKS, 3, 2, NZ), DEV, 0, 0, tiled=True)
    own = own.reshape(3 * NY, NZ)
    other = lax.ppermute(own, "core", swap)
    result, send = call(
        inverse_kernel,
        [((3, RPB, NZ), f32), ((TARGETS, 3 * GROUP, NZ), f32)],
        flags,
        planes,
        outgoing,
        incoming,
        own,
        other,
        advanced,
        gather,
        izp,
        iyh,
        iyl,
        mu,
    )
    returned = lax.all_to_all(send, ("y", "x", "core"), 0, 0, tiled=True)
    (sums,) = call(cell_kernel, [((CZ, 3 * NJ, NZ), f32)], None, returned, cells)
    parts = []
    for k in range(CZ):
        pairs = [
            (place_of(1, y, z, x, c), place_of(0, y, (z + k) % CZ, x, c)) for y, z, x, c in chips()
        ]
        parts.append(lax.ppermute(sums[k], ALL, pairs))
    (result,) = call(close_kernel, [((3, RPB, NZ), f32)], flags, result, layer, remesh, *parts)
    return result.reshape(1, 3, RPB * NZ)


def solution(mesh):
    fine = Mesh(mesh.devices.reshape(2, CY, CZ, CX, CC), ALL)
    placed = (
        P("grp", None, DEV),
        P(DEV),
        P(),
        P(DEV, None),
        P(DEV),
        P(DEV, None),
        P(DEV),
        P(DEV),
    )
    return jax.shard_map(
        on_device, mesh=fine, in_specs=placed, out_specs=P("grp", None, DEV), check_vma=False
    )
```

profile of v0, /device:TPU:1, one launch (start us, length us, event | category | flops | bytes accessed | tf_op | source)
XLA Modules:
  0.0 180.7 jit_solution(16606592279118059316)
XLA Ops:
  0.0 1.0 slice.60
  1.0 9.7 %collective-permute-start = (f32[3,256,128]{2,1,0:T(8,128)S(1)}, f32[3,256,128]{2,1,0:T(8,128)S(1)}, u32[]{:S(2)}, u32[]{:S(2)}) collective-permute-start(f32[3,256,128]{2,1,0:T(8,128)S(1)} %bitcast.52), channel_id=1, source_target_pairs={{0,128},{1,129},{2,130},{3,131},{4,132},{5,133},{6,134},{7,135},{8... | collective-permute-start | bytes 1179656 | tf_op jit(solution)/shard_map/ppermute | solution.py:385
  11.3 2.9 %route_kernel.1 = (bf16[512,256]{1,0:T(8,128)(2,1)}, bf16[512,1024]{1,0:T(8,128)(2,1)}, f32[128,128]{1,0:T(8,128)}, bf16[256,256]{1,0:T(8,128)(2,1)}) custom-call(s32[4]{0:T(128)} %pad_add_fusion.flags, s32[1,256]{1,0:T(1,128)} %bitcast.55, s32[1,256]{1,0:T(1,128)} %bitcast.56, s32[1,256]{1,0:T(1,128)} %bitcast.57, s32[1,256]{1,0:T(1,128)} %bitcast.58, ...), custom_call_target="tpu_custom_call" | custom-call | tf_op jit(solution)/shard_map/route_kernel/pallas_call | solution.py:347
  14.2 10.6 %all-to-all-start.1 = ((f32[128,1,128]{2,1,0:T(1,128)}), f32[128,1,128]{2,1,0:T(1,128)S(1)}, u32[]{:S(2)}, u32[]{:S(2)}) async-start(f32[128,1,128]{2,1,0:T(1,128)} %bitcast.54), calls=%async_computation.1 | async-start | bytes 131072 | tf_op jit(solution)/shard_map/all_to_all | solution.py:409
  25.6 2.8 %bucket_kernel.1 = f32[1536,128]{1,0:T(8,128)} custom-call(f32[3,256,128]{2,1,0:T(8,128)} %copy-done.7, bf16[512,256]{1,0:T(8,128)(2,1)} %get-tuple-element.18.place, bf16[256,256]{1,0:T(8,128)(2,1)} %get-tuple-element.19.merged), custom_call_target="tpu_custom_call" | custom-call | tf_op jit(solution)/shard_map/bucket_kernel/pallas_call | solution.py:347
  28.4 7.0 %all-to-all-done.1 = f32[128,1,128]{2,1,0:T(1,128)S(1)} async-done(((f32[128,1,128]{2,1,0:T(1,128)}), f32[128,1,128]{2,1,0:T(1,128)S(1)}, u32[]{:S(2)}, u32[]{:S(2)}) %all-to-all-start.1) | async-done | bytes 65568 | tf_op jit(solution)/shard_map/all_to_all | solution.py:409
  35.3 6.7 %all-to-all-start = ((f32[128,3,4,128]{3,2,1,0:T(4,128)}), f32[128,3,4,128]{3,2,1,0:T(4,128)S(1)}, u32[]{:S(2)}, u32[]{:S(2)}) async-start(f32[128,3,4,128]{3,2,1,0:T(4,128)} %bitcast.42), calls=%async_computation | async-start | bytes 1572864 | tf_op jit(solution)/shard_map/all_to_all | solution.py:421
  42.0 2.7 %decode_kernel.1 = (bf16[1024,512]{1,0:T(8,128)(2,1)}, bf16[64,512]{1,0:T(8,128)(2,1)}) custom-call(s32[4]{0:T(128)} %pad_add_fusion.flags, f32[128,128]{1,0:T(8,128)} %bitcast.53), custom_call_target="tpu_custom_call" | custom-call | tf_op jit(solution)/shard_map/decode_kernel/pallas_call | solution.py:347
  44.7 21.1 %all-to-all-done = f32[128,3,4,128]{3,2,1,0:T(4,128)S(1)} async-done(((f32[128,3,4,128]{3,2,1,0:T(4,128)}), f32[128,3,4,128]{3,2,1,0:T(4,128)S(1)}, u32[]{:S(2)}, u32[]{:S(2)}) %all-to-all-start) | async-done | bytes 786464 | tf_op jit(solution)/shard_map/all_to_all | solution.py:421
  66.7 6.0 %forward_kernel.1 = (f32[3,4,256,128]{3,2,1,0:T(8,128)}, f32[768,128]{1,0:T(8,128)}, f32[768,128]{1,0:T(8,128)}) custom-call(s32[4]{0:T(128)} %pad_add_fusion.flags, f32[1536,128]{1,0:T(8,128)} %bitcast.43, bf16[1024,512]{1,0:T(8,128)(2,1)} %get-tuple-element.21.spread, f32[3,1024,128]{2,1,0:T(8,128)} %bitcast.39, bf16[256,256]{1,0:T(8,128)(2,1)} %constant.52.clone.sz, ...), custom_call_target="tpu_custom_call" | custom-call | tf_op jit(solution)/shard_map/forward_kernel/pallas_call | solution.py:347
  72.7 1.3 collective-permute-start.1
  73.9 1.6 collective-permute-done.1.incoming
  76.2 2.1 %reduce_kernel.1 = f32[768,128]{1,0:T(8,128)} custom-call(f32[768,128]{1,0:T(8,128)} %get-tuple-element.23.outgoing, f32[768,128]{1,0:T(8,128)} %copy-done.3, f32[768,128]{1,0:T(8,128)} %get-tuple-element.24.kept, f32[256,128]{1,0:T(8,128)} %constant.55.clone.mu), custom_call_target="tpu_custom_call" | custom-call | tf_op jit(solution)/shard_map/reduce_kernel/pallas_call | solution.py:347
  78.4 22.1 %all_to_all.25 = f32[128,3,2,128]{3,2,1,0:T(2,128)} all-to-all(f32[128,3,2,128]{3,2,1,0:T(2,128)} %bitcast.50), channel_id=1, replica_groups=mesh['grp'=2,'y'=4,'z'=4,'x'=4,'core'=2] {'y','z','x','core'}, dimensions={0} | all-to-all | bytes 786432 | tf_op jit(solution)/shard_map/all_to_all | solution.py:437
  100.4 3.8 %line_kernel.1 = f32[768,128]{1,0:T(8,128)} custom-call(s32[4]{0:T(128)} %pad_add_fusion.flags, f32[768,128]{1,0:T(8,128)} %bitcast.49, bf16[512,128]{1,0:T(8,128)(2,1)} %constant.56.clone.kh, bf16[512,128]{1,0:T(8,128)(2,1)} %constant.57.clone.kl, bf16[128,512]{1,0:T(8,128)(2,1)} %constant.58.clone.th, bf16[128,512]{1,0:T(8,128)(2,1)} %constant.59.clone.tl, ...), custom_call_target="tpu_custom_call" | custom-call | tf_op jit(solution)/shard_map/line_kernel/pallas_call | solution.py:347
  104.3 6.3 %all-to-all-start.3 = ((f32[128,3,2,128]{3,2,1,0:T(2,128)}), f32[128,3,2,128]{3,2,1,0:T(2,128)S(1)}, u32[]{:S(2)}, u32[]{:S(2)}) async-start(f32[128,3,2,128]{3,2,1,0:T(2,128)} %bitcast.48), calls=%async_computation.3 | async-start | bytes 786432 | tf_op jit(solution)/shard_map/all_to_all | solution.py:450
  111.6 3.5 %collective-permute-start.3 = (f32[896,128]{1,0:T(8,128)S(1)}, f32[896,128]{1,0:T(8,128)S(1)}, u32[]{:S(2)}, u32[]{:S(2)}) collective-permute-start(f32[896,128]{1,0:T(8,128)S(1)} %pad_maximum_fusion), channel_id=1, source_target_pairs={{0,1},{1,2},{2,3},{3,4},{4,5},{5,6},{6,7},{7,8},{8,9},{9,10},{10,1... | collective-permute-start | bytes 1376264 | tf_op jit(solution)/shard_map/ppermute | solution.py:390
  115.2 1.9 %collective-permute-start.4 = (f32[896,128]{1,0:T(8,128)S(1)}, f32[896,128]{1,0:T(8,128)S(1)}, u32[]{:S(2)}, u32[]{:S(2)}) collective-permute-start(f32[896,128]{1,0:T(8,128)S(1)} %pad_maximum_fusion.1), channel_id=1, source_target_pairs={{1,0},{2,1},{3,2},{4,3},{5,4},{6,5},{7,6},{8,7},{9,8},{10,9},{11,1... | collective-permute-start | bytes 1376264 | tf_op jit(solution)/shard_map/ppermute | solution.py:391
  117.1 13.9 %all-to-all-done.3 = f32[128,3,2,128]{3,2,1,0:T(2,128)S(1)} async-done(((f32[128,3,2,128]{3,2,1,0:T(2,128)}), f32[128,3,2,128]{3,2,1,0:T(2,128)S(1)}, u32[]{:S(2)}, u32[]{:S(2)}) %all-to-all-start.3) | async-done | bytes 393248 | tf_op jit(solution)/shard_map/all_to_all | solution.py:450
  131.0 1.3 collective-permute-start.2
  133.2 4.9 %near_kernel.1 = (f32[3,1024,128]{2,1,0:T(8,128)}, f32[3,16,128]{2,1,0:T(8,128)}) custom-call(s32[4]{0:T(128)} %pad_add_fusion.flags, f32[3,1024,128]{2,1,0:T(8,128)} %bitcast.40, f32[1024,128]{1,0:T(8,128)} %bitcast.51, f32[896,128]{1,0:T(8,128)} %copy-done.4, f32[896,128]{1,0:T(8,128)} %copy-done.5), custom_call_target="tpu_custom_call" | custom-call | tf_op jit(solution)/shard_map/near_kernel/pallas_call | solution.py:347
  138.8 4.3 %inverse_kernel.1 = (f32[3,1024,128]{2,1,0:T(8,128)}, f32[32,48,128]{2,1,0:T(8,128)}) custom-call(s32[4]{0:T(128)} %pad_add_fusion.flags, f32[3,4,256,128]{3,2,1,0:T(8,128)} %get-tuple-element.22.planes, f32[768,128]{1,0:T(8,128)} %get-tuple-element.23.outgoing, f32[768,128]{1,0:T(8,128)} %copy-done.3, f32[768,128]{1,0:T(8,128)} %bitcast.45, ...), custom_call_target="tpu_custom_call" | custom-call | tf_op jit(solution)/shard_map/inverse_kernel/pallas_call | solution.py:347
  143.1 18.7 %all_to_all.26.received = f32[32,48,128]{2,1,0:T(8,128)} all-to-all(f32[32,48,128]{2,1,0:T(8,128)} %get-tuple-element.29), channel_id=1, replica_groups=mesh['grp'=2,'y'=4,'z'=4,'x'=4,'core'=2] {'y','x','core'}, dimensions={0} | all-to-all | bytes 1572864 | tf_op jit(solution)/shard_map/all_to_all | solution.py:469
  161.8 2.0 %cell_kernel.1 = f32[4,48,128]{2,1,0:T(8,128)} custom-call(f32[32,48,128]{2,1,0:T(8,128)} %all_to_all.26.received, bf16[64,512]{1,0:T(8,128)(2,1)} %get-tuple-element.30.cells), custom_call_target="tpu_custom_call" | custom-call | tf_op jit(solution)/shard_map/cell_kernel/pallas_call | solution.py:347
  164.6 1.3 collective-permute-start.8
  165.9 1.3 collective-permute-start.7
  167.2 1.3 collective-permute-start.6
  168.5 1.3 collective-permute-start.5
  169.8 2.4 %collective-permute-done.8.b3 = f32[48,128]{1,0:T(8,128)S(1)} collective-permute-done((f32[48,128]{1,0:T(8,128)S(1)}, f32[48,128]{1,0:T(8,128)S(1)}, u32[]{:S(2)}, u32[]{:S(2)}) %collective-permute-start.8) | collective-permute-done | bytes 24608 | tf_op jit(solution)/shard_map/ppermute | solution.py:476
  172.6 1.0 collective-permute-done.6.b1
  173.5 3.6 %collective-permute-done.5.b0 = f32[48,128]{1,0:T(8,128)S(1)} collective-permute-done((f32[48,128]{1,0:T(8,128)S(1)}, f32[48,128]{1,0:T(8,128)S(1)}, u32[]{:S(2)}, u32[]{:S(2)}) %collective-permute-start.5) | collective-permute-done | bytes 24608 | tf_op jit(solution)/shard_map/ppermute | solution.py:476
  177.7 3.0 %close_kernel.1 = f32[3,1024,128]{2,1,0:T(8,128)} custom-call(s32[4]{0:T(128)} %pad_add_fusion.flags, f32[3,1024,128]{2,1,0:T(8,128)} %get-tuple-element.27.field, f32[3,16,128]{2,1,0:T(8,128)} %get-tuple-element.28.layer, f32[128,128]{1,0:T(8,128)} %remesh.3, f32[48,128]{1,0:T(8,128)} %copy-done.12, f32[48,128]{1,0:T(8,128)} %copy-done.11, ...), custom_call_target="tpu_custom_call" | custom-call | tf_op jit(solution)/shard_map/close_kernel/pallas_call | solution.py:347
  (37 shorter events, 7.5 us)
Async XLA Ops:
  1.0 23.8 %collective-permute-start = (f32[3,256,128]{2,1,0:T(8,128)S(1)}, f32[3,256,128]{2,1,0:T(8,128)S(1)}, u32[]{:S(2)}, u32[]{:S(2)}) collective-permute-start(f32[3,256,128]{2,1,0:T(8,128)S(1)} %bitcast.52), channel_id=1, source_target_pairs={{0,128},{1,129},{2,130},{3,131},{4,132},{5,133},{6,134},{7,135},{8... | collective-permute-start | bytes 1179656 | tf_op jit(solution)/shard_map/ppermute | solution.py:385
  14.2 21.1 %all-to-all-start.1 = ((f32[128,1,128]{2,1,0:T(1,128)}), f32[128,1,128]{2,1,0:T(1,128)S(1)}, u32[]{:S(2)}, u32[]{:S(2)}) async-start(f32[128,1,128]{2,1,0:T(1,128)} %bitcast.54), calls=%async_computation.1 | async-start | bytes 131072 | tf_op jit(solution)/shard_map/all_to_all | solution.py:409
  24.8 0.7 copy-start.7
  35.3 6.7 %copy-start.8 = (f32[128,1,128]{2,1,0:T(1,128)}, f32[128,1,128]{2,1,0:T(1,128)S(1)}, u32[]{:S(2)}) copy-start(f32[128,1,128]{2,1,0:T(1,128)S(1)} %all-to-all-done.1) | copy-start | bytes 196612
  35.3 30.5 %all-to-all-start = ((f32[128,3,4,128]{3,2,1,0:T(4,128)}), f32[128,3,4,128]{3,2,1,0:T(4,128)S(1)}, u32[]{:S(2)}, u32[]{:S(2)}) async-start(f32[128,3,4,128]{3,2,1,0:T(4,128)} %bitcast.42), calls=%async_computation | async-start | bytes 1572864 | tf_op jit(solution)/shard_map/all_to_all | solution.py:421
  65.8 0.9 copy-start.1
  72.7 2.8 %collective-permute-start.1 = (f32[768,128]{1,0:T(8,128)}, f32[768,128]{1,0:T(8,128)S(1)}, u32[]{:S(2)}, u32[]{:S(2)}) collective-permute-start(f32[768,128]{1,0:T(8,128)} %get-tuple-element.23.outgoing), channel_id=1, source_target_pairs={{0,1},{1,0},{2,3},{3,2},{4,5},{5,4},{6,7},{7,6},{8,9},{9,8},{10,11... | collective-permute-start | bytes 1179656 | tf_op jit(solution)/shard_map/ppermute | solution.py:435
  75.5 0.7 copy-start.3
  100.4 11.0 %copy-start = (f32[1,3,131072]{2,0,1:T(1,128)S(1)}, f32[1,3,131072]{2,0,1:T(1,128)}, u32[]{:S(2)}) copy-start(f32[1,3,131072]{2,0,1:T(1,128)} %param.21) | copy-start | bytes 4718596
  104.3 26.7 %all-to-all-start.3 = ((f32[128,3,2,128]{3,2,1,0:T(2,128)}), f32[128,3,2,128]{3,2,1,0:T(2,128)S(1)}, u32[]{:S(2)}, u32[]{:S(2)}) async-start(f32[128,3,2,128]{3,2,1,0:T(2,128)} %bitcast.48), calls=%async_computation.3 | async-start | bytes 786432 | tf_op jit(solution)/shard_map/all_to_all | solution.py:450
  111.6 20.7 %collective-permute-start.3 = (f32[896,128]{1,0:T(8,128)S(1)}, f32[896,128]{1,0:T(8,128)S(1)}, u32[]{:S(2)}, u32[]{:S(2)}) collective-permute-start(f32[896,128]{1,0:T(8,128)S(1)} %pad_maximum_fusion), channel_id=1, source_target_pairs={{0,1},{1,2},{2,3},{3,4},{4,5},{5,6},{6,7},{7,8},{8,9},{9,10},{10,1... | collective-permute-start | bytes 1376264 | tf_op jit(solution)/shard_map/ppermute | solution.py:390
  115.2 17.1 %collective-permute-start.4 = (f32[896,128]{1,0:T(8,128)S(1)}, f32[896,128]{1,0:T(8,128)S(1)}, u32[]{:S(2)}, u32[]{:S(2)}) collective-permute-start(f32[896,128]{1,0:T(8,128)S(1)} %pad_maximum_fusion.1), channel_id=1, source_target_pairs={{1,0},{2,1},{3,2},{4,3},{5,4},{6,5},{7,6},{8,7},{9,8},{10,9},{11,1... | collective-permute-start | bytes 1376264 | tf_op jit(solution)/shard_map/ppermute | solution.py:391
  131.0 7.1 %copy-start.2 = (f32[128,3,2,128]{3,2,1,0:T(2,128)}, f32[128,3,2,128]{3,2,1,0:T(2,128)S(1)}, u32[]{:S(2)}) copy-start(f32[128,3,2,128]{3,2,1,0:T(2,128)S(1)} %all-to-all-done.3) | copy-start | bytes 1179652
  131.0 7.1 %collective-permute-start.2 = (f32[768,128]{1,0:T(8,128)S(1)}, f32[768,128]{1,0:T(8,128)S(1)}, u32[]{:S(2)}, u32[]{:S(2)}) collective-permute-start(f32[768,128]{1,0:T(8,128)S(1)} %bitcast.44), channel_id=1, source_target_pairs={{0,1},{1,0},{2,3},{3,2},{4,5},{5,4},{6,7},{7,6},{8,9},{9,8},{10,11... | collective-permute-start | bytes 1179656 | tf_op jit(solution)/shard_map/ppermute | solution.py:452
  132.2 0.8 copy-start.4
  132.2 0.9 copy-start.5
  138.1 0.8 copy-start.6
  164.6 7.6 %collective-permute-start.8 = (f32[48,128]{1,0:T(8,128)S(1)}, f32[48,128]{1,0:T(8,128)S(1)}, u32[]{:S(2)}, u32[]{:S(2)}) collective-permute-start(f32[48,128]{1,0:T(8,128)S(1)} %get-tuple-element.35), channel_id=1, source_target_pairs={{128,24},{129,25},{130,26},{131,27},{132,28},{133,29},{134,30},{13... | collective-permute-start | bytes 73736 | tf_op jit(solution)/shard_map/ppermute | solution.py:476
  165.9 6.7 %collective-permute-start.7 = (f32[48,128]{1,0:T(8,128)S(1)}, f32[48,128]{1,0:T(8,128)S(1)}, u32[]{:S(2)}, u32[]{:S(2)}) collective-permute-start(f32[48,128]{1,0:T(8,128)S(1)} %get-tuple-element.36), channel_id=1, source_target_pairs={{128,16},{129,17},{130,18},{131,19},{132,20},{133,21},{134,22},{13... | collective-permute-start | bytes 73736 | tf_op jit(solution)/shard_map/ppermute | solution.py:476
  167.2 6.3 %collective-permute-start.6 = (f32[48,128]{1,0:T(8,128)S(1)}, f32[48,128]{1,0:T(8,128)S(1)}, u32[]{:S(2)}, u32[]{:S(2)}) collective-permute-start(f32[48,128]{1,0:T(8,128)S(1)} %get-tuple-element.37), channel_id=1, source_target_pairs={{128,8},{129,9},{130,10},{131,11},{132,12},{133,13},{134,14},{135,... | collective-permute-start | bytes 73736 | tf_op jit(solution)/shard_map/ppermute | solution.py:476
  168.5 8.6 %collective-permute-start.5 = (f32[48,128]{1,0:T(8,128)S(1)}, f32[48,128]{1,0:T(8,128)S(1)}, u32[]{:S(2)}, u32[]{:S(2)}) collective-permute-start(f32[48,128]{1,0:T(8,128)S(1)} %get-tuple-element.38), channel_id=1, source_target_pairs={{128,0},{129,1},{130,2},{131,3},{132,4},{133,5},{134,6},{135,7},{1... | collective-permute-start | bytes 73736 | tf_op jit(solution)/shard_map/ppermute | solution.py:476
  172.2 4.9 %copy-start.9 = (f32[48,128]{1,0:T(8,128)}, f32[48,128]{1,0:T(8,128)S(1)}, u32[]{:S(2)}) copy-start(f32[48,128]{1,0:T(8,128)S(1)} %collective-permute-done.8.b3) | copy-start | bytes 73732
  172.6 4.6 %copy-start.10 = (f32[48,128]{1,0:T(8,128)}, f32[48,128]{1,0:T(8,128)S(1)}, u32[]{:S(2)}) copy-start(f32[48,128]{1,0:T(8,128)S(1)} %collective-permute-done.7.b2) | copy-start | bytes 73732
  173.5 3.6 %copy-start.11 = (f32[48,128]{1,0:T(8,128)}, f32[48,128]{1,0:T(8,128)S(1)}, u32[]{:S(2)}) copy-start(f32[48,128]{1,0:T(8,128)S(1)} %collective-permute-done.6.b1) | copy-start | bytes 73732
  177.1 0.6 copy-start.12
where the time goes:
time: 182 us; the launch traced here: 181 us
  waiting for transfers between devices  50.8 us (28%)
  starting transfers between devices  46.3 us (25%)
  blocking collectives  40.7 us (22%)
  Pallas kernels  34.5 us (19%)
  local copies, waits for them, and re-layouts  7.43 us (4%)
    pallas_call x10, Pallas kernels, call(): pl.pallas_call(kernel, out_shape=[jax.ShapeDtypeStruct(s, d) for s, d in...  34.5 us
    all_to_all x1, blocking collectives, on_device(): lax.all_to_all(share.reshape(BRICKS, 3, 2, NZ), DEV, 0, 0, tiled=True)  22.1 us
    all_to_all x1, waiting for transfers between devices, on_device(): lax.all_to_all(bundle.reshape(BRICKS, 3, CAP, NZ), DEV, 0, 0, tiled=True)  21.1 us
    all_to_all x1, blocking collectives, on_device(): returned = lax.all_to_all(send, ('y', 'x', 'core'), 0, 0, tiled=True)  18.7 us
    all_to_all x1, waiting for transfers between devices, on_device(): lax.all_to_all(solved.reshape(BRICKS, 3, 2, NZ), DEV, 0, 0, tiled=True)  13.9 us
    all_to_all x1, starting transfers between devices, on_device(): codes = lax.all_to_all(codes.reshape(BRICKS, 1, NZ), DEV, 0, 0, tiled=True)  10.6 us
    ppermute x1, starting transfers between devices, on_device(): blocks = lax.ppermute(blocks, ALL, across)  9.66 us
    ppermute x4, waiting for transfers between devices, on_device(): parts.append(lax.ppermute(sums[k], ALL, pairs))  7.32 us
  transfers between devices with their start and end apart: 12, of which 8 were waited for; matrix products, arithmetic and copies ran while one was open for 1% of the time, Pallas kernels for 7%

commit v1 on v0

--- a/solution.py
+++ b/solution.py
@@ -149,11 +149,10 @@
     )
 
 
-def decode_kernel(flags, codes, spread, cells):
+def decode_kernel(flags, codes, landing, cells):
     zme = flags[3]
     turned = codes[...].T
-    rows = jnp.concatenate([turned[i : i + 1, :] for i in range(CAP)], axis=1).astype(i32)
-    spread[...] = onehot(iota((RPB, SLOTS), 0) == rows - 1)
+    landing[...] = jnp.concatenate([turned[i : i + 1, :] for i in range(CAP)], axis=1).astype(i32)
     target = iota((TARGETS, BRICKS), 0)
     source = ((target >> 3) * CZ + zme) * (CX * CC) + (target & (CX * CC - 1))
     chosen = exact(jnp.where(iota((TARGETS, BRICKS), 1) == source, 1.0, 0.0), codes[...])
@@ -166,7 +165,7 @@
     cells[...] = onehot(iota((CZ * NJ, SLOTS), 0) == code - 1)
 
 
-def near_kernel(flags, state, courant, up, down, out, layer):
+def local_kernel(flags, state, courant, up, down, sz, out, layer):
     @pl.when(flags[0] == 0)
     def _():
         cr = jnp.concatenate([up[768:896, :], courant[...], down[768:896, :]], axis=0)
@@ -191,6 +190,11 @@
             out[c] = step(field, courant[...])
             layer[c] = state[c, pl.ds(NI - 1, NJ, stride=NI), :]
 
+    @pl.when(flags[0] != 0)
+    def _():
+        for c in range(3):
+            out[c] = times_paired(state[c], sz[...])
+
 
 def bucket_kernel(blocks, place, merged, out):
     for c in range(3):
@@ -210,15 +214,16 @@
     return g11, g12, g13
 
 
-def forward_kernel(flags, received, spread, state, sz, syh, syl, mu, planes, outgoing, kept):
+def forward_kernel(flags, received, landing, work, syh, syl, mu, planes, outgoing, kept):
     beta = mu[...] + 2.0
     g11, g12, g13 = weights(beta)
     first = flags[1] == 0
+    spread = onehot(iota((RPB, SLOTS), 0) == landing[...] - 1)
     for c in range(3):
         rows = jnp.concatenate(
             [received[pl.ds(c * CAP + r, BRICKS, stride=3 * CAP), :] for r in range(CAP)], axis=0
         )
-        field = pick(spread[...], rows) + times_paired(state[c], sz[...])
+        field = pick(spread, rows) + work[c]
         field = jnp.concatenate([field[p * NY : (p + 1) * NY] for p in range(4)], axis=1)
         field = table_times(syh[...], syl[...], field)
         f0, f1, f2, f3 = (field[:, p * NZ : (p + 1) * NZ] for p in range(4))
@@ -254,11 +259,30 @@
 
 
 def inverse_kernel(
-    flags, planes, outgoing, incoming, own, other, advanced, gather, sz, syh, syl, mu, out, send
+    flags,
+    planes,
+    outgoing,
+    incoming,
+    own,
+    other,
+    work,
+    gather,
+    sz,
+    syh,
+    syl,
+    mu,
+    out,
+    send,
+    held,
+    rows_held,
+    out_sems,
+    send_sems,
 ):
     @pl.when(flags[0] == 0)
     def _():
-        out[...] = advanced[...]
+        copy = pltpu.make_async_copy(work, out, out_sems.at[0])
+        copy.start()
+        copy.wait()
 
     @pl.when(flags[0] != 0)
     def _():
@@ -315,21 +339,30 @@
             dz(px) - dx(potentials[2]),
             dx(potentials[1]) - dy(px),
         )
+        copies = []
         for c in range(3):
-            out[c] = velocity[c]
+            held[c] = velocity[c]
+            copies.append(pltpu.make_async_copy(held.at[c], out.at[c], out_sems.at[c]))
+            copies[-1].start()
+        for c in range(3):
             rows_out = pick(gather[...], velocity[c])
-            send[:, c * GROUP : (c + 1) * GROUP, :] = rows_out.reshape(TARGETS, GROUP, NZ)
-
-
-def cell_kernel(received, cells, out):
+            rows_held[c] = rows_out.reshape(TARGETS, GROUP, NZ)
+            target = send.at[:, pl.ds(c * GROUP, GROUP), :]
+            copies.append(pltpu.make_async_copy(rows_held.at[c], target, send_sems.at[c]))
+            copies[-1].start()
+        for copy in copies:
+            copy.wait()
+
+
+def cell_kernel(received, cells, *outs):
     for c in range(3):
         rows = received[:, c * GROUP : (c + 1) * GROUP, :].reshape(SLOTS, NZ)
-        out[:, c * NJ : (c + 1) * NJ, :] = pick(cells[...], rows).reshape(CZ, NJ, NZ)
-
-
-def close_kernel(flags, field, layer, remesh, b0, b1, b2, b3, out):
-    out[...] = field[...]
-
+        sums = pick(cells[...], rows)
+        for k in range(CZ):
+            outs[k][c * NJ : (c + 1) * NJ, :] = sums[k * NJ : (k + 1) * NJ]
+
+
+def close_kernel(flags, field, work, layer, remesh, b0, b1, b2, b3, out, slab, sem):
     @pl.when(flags[0] == 0)
     def _():
         total = exact((b0[...] + b1[...]) + (b2[...] + b3[...]), remesh[...], NT)
@@ -338,20 +371,35 @@
         for c in range(3):
             d, e = (c + 1) % 3, (c + 2) % 3
             cross = first[d] * second[e] - first[e] * second[d]
-            edge = pl.ds(NI - 1, NJ, stride=NI)
-            out[c, edge, :] = field[c, edge, :] + coupling * cross
-
-
-def call(kernel, outs, flags, *args):
+            for j in range(NJ):
+                row = c * RPB + (j + 1) * NI
+                slab[c, j, :7, :] = work[c, row - c * RPB - 8 : row - c * RPB - 1, :]
+            slab[c, :, 7, :] = work[c, pl.ds(NI - 1, NJ, stride=NI), :] + coupling * cross
+        copy = pltpu.make_async_copy(slab, out.at[:, :, pl.ds(NI - 8, 8), :], sem)
+        copy.start()
+        copy.wait()
+
+
+def call(kernel, outs, flags, *args, home=pltpu.VMEM, alias=False, scratch=(), free=False):
     scalars = [] if flags is None else [flags]
+    args = [jnp.asarray(a) for a in args]
+    kept = [args.pop(0)] if alias else []
     return pl.pallas_call(
         kernel,
-        out_shape=[jax.ShapeDtypeStruct(s, d) for s, d in outs],
+        out_shape=[(jax.ShapeDtypeStruct if free else home)(s, d) for s, d in outs],
         in_specs=[pl.BlockSpec(memory_space=pltpu.SMEM)] * len(scalars)
+        + [pl.BlockSpec(memory_space=pltpu.HBM)] * len(kept)
         + [pl.BlockSpec(memory_space=pltpu.VMEM)] * len(args),
-        out_specs=[pl.BlockSpec(memory_space=pltpu.VMEM)] * len(outs),
+        out_specs=[pl.BlockSpec(memory_space=home)] * len(outs),
+        scratch_shapes=list(scratch),
+        input_output_aliases={len(scalars): 0} if alias else {},
+        compiler_params=pltpu.CompilerParams(vmem_limit_bytes=24 << 20),
         name=kernel.__name__,
-    )(*scalars, *args)
+    )(
+        *scalars,
+        *kept,
+        *[a if free else pltpu.with_memory_space_constraint(a, pltpu.VMEM) for a in args],
+    )
 
 
 def place_of(g, y, z, x, c):
@@ -405,16 +453,25 @@
         *rows,
         remesh,
         sz.astype(np.float32),
+        free=True,
     )
     codes = lax.all_to_all(codes.reshape(BRICKS, 1, NZ), DEV, 0, 0, tiled=True)
-    spread, cells = call(
+    landing, cells = call(
         decode_kernel,
-        [((RPB, SLOTS), bf16), ((CZ * NJ, SLOTS), bf16)],
+        [((1, SLOTS), i32), ((CZ * NJ, SLOTS), bf16)],
         flags,
         codes.reshape(BRICKS, NZ),
-    )
-    advanced, layer = call(
-        near_kernel, [((3, RPB, NK), f32), ((3, NJ, NK), f32)], flags, field, speed, up, down
+        free=True,
+    )
+    work, layer = call(
+        local_kernel,
+        [((3, RPB, NK), f32), ((3, NJ, NK), f32)],
+        flags,
+        field,
+        speed,
+        up,
+        down,
+        szp,
     )
 
     (bundle,) = call(bucket_kernel, [((3 * SLOTS, NZ), f32)], None, blocks, place, merged)
@@ -424,9 +481,8 @@
         [((3, 4, NY, NZ), f32), ((3 * NY, NZ), f32), ((3 * NY, NZ), f32)],
         flags,
         bundle.reshape(3 * SLOTS, NZ),
-        spread,
-        field,
-        szp,
+        landing,
+        work,
         syh,
         syl,
         mu,
@@ -459,22 +515,41 @@
         incoming,
         own,
         other,
-        advanced,
+        work,
         gather,
         izp,
         iyh,
         iyl,
         mu,
+        home=pltpu.HBM,
+        scratch=[
+            pltpu.VMEM((3, RPB, NZ), f32),
+            pltpu.VMEM((3, TARGETS, GROUP, NZ), f32),
+            pltpu.SemaphoreType.DMA((3,)),
+            pltpu.SemaphoreType.DMA((3,)),
+        ],
     )
     returned = lax.all_to_all(send, ("y", "x", "core"), 0, 0, tiled=True)
-    (sums,) = call(cell_kernel, [((CZ, 3 * NJ, NZ), f32)], None, returned, cells)
+    sums = call(cell_kernel, [((3 * NJ, NZ), f32)] * CZ, None, returned, cells)
     parts = []
     for k in range(CZ):
         pairs = [
             (place_of(1, y, z, x, c), place_of(0, y, (z + k) % CZ, x, c)) for y, z, x, c in chips()
         ]
         parts.append(lax.ppermute(sums[k], ALL, pairs))
-    (result,) = call(close_kernel, [((3, RPB, NZ), f32)], flags, result, layer, remesh, *parts)
+    (result,) = call(
+        close_kernel,
+        [((3, NJ, NI, NZ), f32)],
+        flags,
+        result.reshape(3, NJ, NI, NZ),
+        work,
+        layer,
+        remesh,
+        *parts,
+        home=pltpu.HBM,
+        alias=True,
+        scratch=[pltpu.VMEM((3, NJ, 8, NZ), f32), pltpu.SemaphoreType.DMA],
+    )
     return result.reshape(1, 3, RPB * NZ)
 
 

time: 182 us -> 165 us (0.907)
  blocking collectives: 40.7 us -> 62.1 us
  Pallas kernels: 34.5 us -> 17.5 us
  waiting for transfers between devices: 50.8 us -> 34.3 us
  starting transfers between devices: 46.3 us -> 40.6 us
  local copies, waits for them, and re-layouts: 7.43 us -> 9.32 us
    all_to_all x0 -> x1, blocking collectives: none -> 21.6 us  [on_device(): lax.all_to_all(solved.reshape(BRICKS, 3, 2, NZ), DEV, 0, 0, tiled=True)]
    pallas_call x10, Pallas kernels: 34.5 us -> 17.5 us  [call(): pl.pallas_call(kernel, out_shape=[(jax.ShapeDtypeStruct if free else home...]
    all_to_all x1 -> x0, waiting for transfers between devices: 13.9 us -> none  [on_device(): lax.all_to_all(solved.reshape(BRICKS, 3, 2, NZ), DEV, 0, 0, tiled=True)]
    all_to_all x1, waiting for transfers between devices: 21.1 us -> 9.03 us  [on_device(): lax.all_to_all(bundle.reshape(BRICKS, 3, CAP, NZ), DEV, 0, 0, tiled=True)]
    all_to_all x1 -> x0, starting transfers between devices: 6.26 us -> none  [on_device(): lax.all_to_all(solved.reshape(BRICKS, 3, 2, NZ), DEV, 0, 0, tiled=True)]
    ppermute x1, waiting for transfers between devices: 0.01 us -> 4.33 us  [on_device(): up = lax.ppermute(last, ALL, ahead)]
    ppermute x1, waiting for transfers between devices: 0.01 us -> 3.84 us  [on_device(): down = lax.ppermute(lead, ALL, [(b, a) for a, b in ahead])]
    unnamed x26 -> x56, local copies, waits for them, and re-layouts: 4.67 us -> 7.35 us
  transfers between devices with their start and end apart: 12 -> 11, of which waited for: 8 -> 9; matrix products, arithmetic and copies ran while one was open for 1% -> 1% of each run, Pallas kernels for 7% -> 5%
where the time goes in v1:
time: 165 us
  blocking collectives  62.1 us (38%)
  starting transfers between devices  40.6 us (25%)
  waiting for transfers between devices  34.3 us (21%)
  Pallas kernels  17.5 us (11%)
  local copies, waits for them, and re-layouts  9.32 us (6%)
    all_to_all x1, blocking collectives, on_device(): lax.all_to_all(share.reshape(BRICKS, 3, 2, NZ), DEV, 0, 0, tiled=True)  22.1 us
    all_to_all x1, blocking collectives, on_device(): lax.all_to_all(solved.reshape(BRICKS, 3, 2, NZ), DEV, 0, 0, tiled=True)  21.6 us
    all_to_all x1, blocking collectives, on_device(): returned = lax.all_to_all(send, ('y', 'x', 'core'), 0, 0, tiled=True)  18.4 us
    pallas_call x10, Pallas kernels, call(): pl.pallas_call(kernel, out_shape=[(jax.ShapeDtypeStruct if free else home...  17.5 us
    all_to_all x1, starting transfers between devices, on_device(): codes = lax.all_to_all(codes.reshape(BRICKS, 1, NZ), DEV, 0, 0, tiled=True)  10.6 us
    ppermute x1, starting transfers between devices, on_device(): blocks = lax.ppermute(blocks, ALL, across)  9.66 us
    all_to_all x1, waiting for transfers between devices, on_device(): lax.all_to_all(bundle.reshape(BRICKS, 3, CAP, NZ), DEV, 0, 0, tiled=True)  9.03 us
    all_to_all x1, waiting for transfers between devices, on_device(): codes = lax.all_to_all(codes.reshape(BRICKS, 1, NZ), DEV, 0, 0, tiled=True)  8.09 us
  transfers between devices with their start and end apart: 11, of which 9 were waited for; matrix products, arithmetic and copies ran while one was open for 1% of the time, Pallas kernels for 5%

profile of v1, /device:TPU:1, one launch (start us, length us, event | category | flops | bytes accessed | tf_op | source)
XLA Modules:
  0.0 164.5 jit_solution(2509865969457352461)
XLA Ops:
  0.0 1.0 slice.44
  1.0 9.7 %collective-permute-start = (f32[3,256,128]{2,1,0:T(8,128)S(1)}, f32[3,256,128]{2,1,0:T(8,128)S(1)}, u32[]{:S(2)}, u32[]{:S(2)}) collective-permute-start(f32[3,256,128]{2,1,0:T(8,128)S(1)} %bitcast.49), channel_id=1, source_target_pairs={{0,128},{1,129},{2,130},{3,131},{4,132},{5,133},{6,134},{7,135},{8... | collective-permute-start | bytes 1179656 | tf_op jit(solution)/shard_map/ppermute | solution.py:433
  15.9 2.2 %route_kernel.1 = (bf16[512,256]{1,0:T(8,128)(2,1)S(1)}, bf16[512,1024]{1,0:T(8,128)(2,1)S(1)}, f32[128,128]{1,0:T(8,128)}, bf16[256,256]{1,0:T(8,128)(2,1)S(1)}) custom-call(s32[4]{0:T(128)S(1)} %pad_add_fusion.flags, s32[1,256]{1,0:T(1,128)S(1)} %bitcast.41, s32[1,256]{1,0:T(1,128)S(1)} %bitcast.42, s32[1,256]{1,0:T(1,128)S(1)} %bitcast.43, ...), custom_call_target="tpu_custom_call" | custom-call | tf_op jit(solution)/shard_map/route_kernel/pallas_call | solution.py:387
  19.0 10.6 %all-to-all-start.1 = ((f32[128,1,128]{2,1,0:T(1,128)}), f32[128,1,128]{2,1,0:T(1,128)S(1)}, u32[]{:S(2)}, u32[]{:S(2)}) async-start(f32[128,1,128]{2,1,0:T(1,128)} %bitcast.14), calls=%async_computation.1 | async-start | bytes 131072 | tf_op jit(solution)/shard_map/all_to_all | solution.py:458
  29.6 1.7 %bucket_kernel.1 = f32[1536,128]{1,0:T(8,128)} custom-call(f32[3,256,128]{2,1,0:T(8,128)S(1)} %collective-permute-done.blocks, bf16[512,256]{1,0:T(8,128)(2,1)S(1)} %get-tuple-element.22.place, bf16[256,256]{1,0:T(8,128)(2,1)S(1)} %get-tuple-element.23.merged), custom_call_target="tpu_custom_call" | custom-call | tf_op jit(solution)/shard_map/bucket_kernel/pallas_call | solution.py:387
  31.3 8.1 %all-to-all-done.1 = f32[128,1,128]{2,1,0:T(1,128)S(1)} async-done(((f32[128,1,128]{2,1,0:T(1,128)}), f32[128,1,128]{2,1,0:T(1,128)S(1)}, u32[]{:S(2)}, u32[]{:S(2)}) %all-to-all-start.1) | async-done | bytes 65568 | tf_op jit(solution)/shard_map/all_to_all | solution.py:458
  39.4 7.2 %all-to-all-start = ((f32[128,3,4,128]{3,2,1,0:T(4,128)}), f32[128,3,4,128]{3,2,1,0:T(4,128)}, u32[]{:S(2)}, u32[]{:S(2)}) async-start(f32[128,3,4,128]{3,2,1,0:T(4,128)} %bitcast.11), calls=%async_computation | async-start | bytes 1572864 | tf_op jit(solution)/shard_map/all_to_all | solution.py:478
  47.6 3.7 %collective-permute-start.1 = (f32[896,128]{1,0:T(8,128)S(1)}, f32[896,128]{1,0:T(8,128)S(1)}, u32[]{:S(2)}, u32[]{:S(2)}) collective-permute-start(f32[896,128]{1,0:T(8,128)S(1)} %pad_maximum_fusion), channel_id=1, source_target_pairs={{0,1},{1,2},{2,3},{3,4},{4,5},{5,6},{6,7},{7,8},{8,9},{9,10},{10,1... | collective-permute-start | bytes 1376264 | tf_op jit(solution)/shard_map/ppermute | solution.py:438
  51.4 1.9 %collective-permute-start.2 = (f32[896,128]{1,0:T(8,128)S(1)}, f32[896,128]{1,0:T(8,128)S(1)}, u32[]{:S(2)}, u32[]{:S(2)}) collective-permute-start(f32[896,128]{1,0:T(8,128)S(1)} %pad_maximum_fusion.1), channel_id=1, source_target_pairs={{1,0},{2,1},{3,2},{4,3},{5,4},{6,5},{7,6},{8,7},{9,8},{10,9},{11,1... | collective-permute-start | bytes 1376264 | tf_op jit(solution)/shard_map/ppermute | solution.py:439
  53.3 1.0 decode_kernel.1
  54.9 4.3 %collective-permute-done.1.up = f32[896,128]{1,0:T(8,128)S(1)} collective-permute-done((f32[896,128]{1,0:T(8,128)S(1)}, f32[896,128]{1,0:T(8,128)S(1)}, u32[]{:S(2)}, u32[]{:S(2)}) %collective-permute-start.1) | collective-permute-done | bytes 458784 | tf_op jit(solution)/shard_map/ppermute | solution.py:438
  59.2 3.8 %collective-permute-done.2.down = f32[896,128]{1,0:T(8,128)S(1)} collective-permute-done((f32[896,128]{1,0:T(8,128)S(1)}, f32[896,128]{1,0:T(8,128)S(1)}, u32[]{:S(2)}, u32[]{:S(2)}) %collective-permute-start.2) | collective-permute-done | bytes 458784 | tf_op jit(solution)/shard_map/ppermute | solution.py:439
  63.1 2.5 %local_kernel.1 = (f32[3,1024,128]{2,1,0:T(8,128)S(1)}, f32[3,16,128]{2,1,0:T(8,128)S(1)}) custom-call(s32[4]{0:T(128)S(1)} %pad_add_fusion.flags, f32[3,1024,128]{2,1,0:T(8,128)S(1)} %bitcast.33, f32[1024,128]{1,0:T(8,128)S(1)} %bitcast.39, f32[896,128]{1,0:T(8,128)S(1)} %collective-permute-done.1.up, f32[896,128]{1,0:T(8,128)S(1)} %collective-permute-done.2.down, ...), custom_call_target="tpu_custom_call" | custom-call | tf_op jit(solution)/shard_map/local_kernel/pallas_call | solution.py:387
  66.3 9.0 %all-to-all-done = f32[128,3,4,128]{3,2,1,0:T(4,128)} async-done(((f32[128,3,4,128]{3,2,1,0:T(4,128)}), f32[128,3,4,128]{3,2,1,0:T(4,128)}, u32[]{:S(2)}, u32[]{:S(2)}) %all-to-all-start) | async-done | bytes 786464 | tf_op jit(solution)/shard_map/all_to_all | solution.py:478
  75.3 4.3 %forward_kernel.1 = (f32[3,4,256,128]{3,2,1,0:T(8,128)S(1)}, f32[768,128]{1,0:T(8,128)S(1)}, f32[768,128]{1,0:T(8,128)S(1)}) custom-call(s32[4]{0:T(128)S(1)} %pad_add_fusion.flags, f32[1536,128]{1,0:T(8,128)} %bitcast.12.received, s32[1,512]{1,0:T(1,128)S(1)} %get-tuple-element.25.landing, f32[3,1024,128]{2,1,0:T(8,128)S(1)} %get-tuple-element.26.work, ...), custom_call_target="tpu_custom_call" | custom-call | tf_op jit(solution)/shard_map/forward_kernel/pallas_call | solution.py:387
  79.6 1.3 collective-permute-start.3
  81.0 1.3 collective-permute-done.3.incoming
  82.5 22.1 %all_to_all.25 = f32[128,3,2,128]{3,2,1,0:T(2,128)S(1)} all-to-all(f32[128,3,2,128]{3,2,1,0:T(2,128)S(1)} %bitcast.38), channel_id=1, replica_groups=mesh['grp'=2,'y'=4,'z'=4,'x'=4,'core'=2] {'y','z','x','core'}, dimensions={0} | all-to-all | bytes 786432 | tf_op jit(solution)/shard_map/all_to_all | solution.py:493
  104.7 2.2 %line_kernel.1 = f32[768,128]{1,0:T(8,128)S(1)} custom-call(s32[4]{0:T(128)S(1)} %pad_add_fusion.flags, f32[768,128]{1,0:T(8,128)S(1)} %bitcast.36, bf16[512,128]{1,0:T(8,128)(2,1)S(1)} %copy-done.14, bf16[512,128]{1,0:T(8,128)(2,1)S(1)} %copy-done.13, bf16[128,512]{1,0:T(8,128)(2,1)S(1)} %copy-done.12, bf16[128,512]{1,0:T(8,128)(2,1)S(1)} %copy-done.11, ...), custom_call_target="tpu_custom_call" | custom-call | tf_op jit(solution)/shard_map/line_kernel/pallas_call | solution.py:387
  106.9 21.6 %all_to_all.26 = f32[128,3,2,128]{3,2,1,0:T(2,128)S(1)} all-to-all(f32[128,3,2,128]{3,2,1,0:T(2,128)S(1)} %bitcast.37), channel_id=1, replica_groups=mesh['grp'=2,'y'=4,'z'=4,'x'=4,'core'=2] {'y','z','x','core'}, dimensions={0} | all-to-all | bytes 786432 | tf_op jit(solution)/shard_map/all_to_all | solution.py:506
  128.5 1.1 collective-permute-start.4
  129.6 1.3 collective-permute-done.4.other
  130.9 1.7 %inverse_kernel.1 = (f32[3,1024,128]{2,1,0:T(8,128)}, f32[32,48,128]{2,1,0:T(8,128)}) custom-call(s32[4]{0:T(128)S(1)} %pad_add_fusion.flags, f32[3,4,256,128]{3,2,1,0:T(8,128)S(1)} %get-tuple-element.27.planes, f32[768,128]{1,0:T(8,128)S(1)} %get-tuple-element.28.outgoing, f32[768,128]{1,0:T(8,128)S(1)} %collective-permute-done.3.incoming, ...), custom_call_target="tpu_custom_call" | custom-call | tf_op jit(solution)/shard_map/inverse_kernel/pallas_call | solution.py:387
  132.7 18.4 %all_to_all.27.received = f32[32,48,128]{2,1,0:T(8,128)S(1)} all-to-all(f32[32,48,128]{2,1,0:T(8,128)} %get-tuple-element.33), channel_id=1, replica_groups=mesh['grp'=2,'y'=4,'z'=4,'x'=4,'core'=2] {'y','x','core'}, dimensions={0} | all-to-all | bytes 1572864 | tf_op jit(solution)/shard_map/all_to_all | solution.py:532
  151.4 1.3 collective-permute-start.5
  152.7 1.3 collective-permute-start.6
  154.0 1.3 collective-permute-start.7
  155.3 1.3 collective-permute-start.8
  156.6 3.3 %collective-permute-done.5.b0 = f32[48,128]{1,0:T(8,128)S(1)} collective-permute-done((f32[48,128]{1,0:T(8,128)S(1)}, f32[48,128]{1,0:T(8,128)S(1)}, u32[]{:S(2)}, u32[]{:S(2)}) %collective-permute-start.5) | collective-permute-done | bytes 24608 | tf_op jit(solution)/shard_map/ppermute | solution.py:539
  159.9 1.1 collective-permute-done.7.b2
  161.0 1.9 %collective-permute-done.8.b3 = f32[48,128]{1,0:T(8,128)S(1)} collective-permute-done((f32[48,128]{1,0:T(8,128)S(1)}, f32[48,128]{1,0:T(8,128)S(1)}, u32[]{:S(2)}, u32[]{:S(2)}) %collective-permute-start.8) | collective-permute-done | bytes 24608 | tf_op jit(solution)/shard_map/ppermute | solution.py:539
  162.9 1.5 close_kernel.1
  (65 shorter events, 8.8 us)
Async XLA Ops:
  1.0 28.6 %collective-permute-start = (f32[3,256,128]{2,1,0:T(8,128)S(1)}, f32[3,256,128]{2,1,0:T(8,128)S(1)}, u32[]{:S(2)}, u32[]{:S(2)}) collective-permute-start(f32[3,256,128]{2,1,0:T(8,128)S(1)} %bitcast.49), channel_id=1, source_target_pairs={{0,128},{1,129},{2,130},{3,131},{4,132},{5,133},{6,134},{7,135},{8... | collective-permute-start | bytes 1179656 | tf_op jit(solution)/shard_map/ppermute | solution.py:433
  10.8 0.8 copy-start.5
  11.6 0.8 copy-start.18
  18.1 1.0 copy-start.2
  19.0 20.4 %all-to-all-start.1 = ((f32[128,1,128]{2,1,0:T(1,128)}), f32[128,1,128]{2,1,0:T(1,128)S(1)}, u32[]{:S(2)}, u32[]{:S(2)}) async-start(f32[128,1,128]{2,1,0:T(1,128)} %bitcast.14), calls=%async_computation.1 | async-start | bytes 131072 | tf_op jit(solution)/shard_map/all_to_all | solution.py:458
  29.6 17.9 %copy-start = (f32[1,3,131072]{2,0,1:T(1,128)S(1)}, f32[1,3,131072]{2,0,1:T(1,128)}, u32[]{:S(2)}) copy-start(f32[1,3,131072]{2,0,1:T(1,128)} %param.21) | copy-start | bytes 4718596
  39.4 35.9 %all-to-all-start = ((f32[128,3,4,128]{3,2,1,0:T(4,128)}), f32[128,3,4,128]{3,2,1,0:T(4,128)}, u32[]{:S(2)}, u32[]{:S(2)}) async-start(f32[128,3,4,128]{3,2,1,0:T(4,128)} %bitcast.11), calls=%async_computation | async-start | bytes 1572864 | tf_op jit(solution)/shard_map/all_to_all | solution.py:478
  47.5 15.6 %copy-start.4 = (f32[131072]{0:T(1024)S(1)}, f32[131072]{0:T(1024)}, u32[]{:S(2)}) copy-start(f32[131072]{0:T(1024)} %param.22) | copy-start | bytes 1572868
  47.5 15.6 %copy-start.17 = (bf16[256,256]{1,0:T(8,128)(2,1)S(1)}, bf16[256,256]{1,0:T(8,128)(2,1)}, u32[]{:S(2)}) copy-start(bf16[256,256]{1,0:T(8,128)(2,1)} %constant.52.clone.sz) | copy-start | bytes 393220
  47.6 11.6 %collective-permute-start.1 = (f32[896,128]{1,0:T(8,128)S(1)}, f32[896,128]{1,0:T(8,128)S(1)}, u32[]{:S(2)}, u32[]{:S(2)}) collective-permute-start(f32[896,128]{1,0:T(8,128)S(1)} %pad_maximum_fusion), channel_id=1, source_target_pairs={{0,1},{1,2},{2,3},{3,4},{4,5},{5,6},{6,7},{7,8},{8,9},{9,10},{10,1... | collective-permute-start | bytes 1376264 | tf_op jit(solution)/shard_map/ppermute | solution.py:438
  51.4 11.7 %collective-permute-start.2 = (f32[896,128]{1,0:T(8,128)S(1)}, f32[896,128]{1,0:T(8,128)S(1)}, u32[]{:S(2)}, u32[]{:S(2)}) collective-permute-start(f32[896,128]{1,0:T(8,128)S(1)} %pad_maximum_fusion.1), channel_id=1, source_target_pairs={{1,0},{2,1},{3,2},{4,3},{5,4},{6,5},{7,6},{8,7},{9,8},{10,9},{11,1... | collective-permute-start | bytes 1376264 | tf_op jit(solution)/shard_map/ppermute | solution.py:439
  63.1 12.2 %copy-start.1 = (f32[256,128]{1,0:T(8,128)S(1)}, f32[256,128]{1,0:T(8,128)}, u32[]{:S(2)}) copy-start(f32[256,128]{1,0:T(8,128)} %constant.55.clone.mu) | copy-start | bytes 393220
  63.1 12.2 %copy-start.15 = (bf16[256,256]{1,0:T(8,128)(2,1)S(1)}, bf16[256,256]{1,0:T(8,128)(2,1)}, u32[]{:S(2)}) copy-start(bf16[256,256]{1,0:T(8,128)(2,1)} %constant.54.clone.syl) | copy-start | bytes 393220
  63.1 12.2 %copy-start.16 = (bf16[256,256]{1,0:T(8,128)(2,1)S(1)}, bf16[256,256]{1,0:T(8,128)(2,1)}, u32[]{:S(2)}) copy-start(bf16[256,256]{1,0:T(8,128)(2,1)} %constant.53.clone.syh) | copy-start | bytes 393220
  79.6 25.1 %copy-start.7 = (f32[512,1]{1,0:T(8,128)S(1)}, f32[512,1]{1,0:T(8,128)}, u32[]{:S(2)}) copy-start(f32[512,1]{1,0:T(8,128)} %constant.60.clone.lamx) | copy-start | bytes 6148
  79.6 25.1 %copy-start.11 = (bf16[128,512]{1,0:T(8,128)(2,1)S(1)}, bf16[128,512]{1,0:T(8,128)(2,1)}, u32[]{:S(2)}) copy-start(bf16[128,512]{1,0:T(8,128)(2,1)} %constant.59.clone.tl) | copy-start | bytes 393220
  79.6 25.0 %copy-start.12 = (bf16[128,512]{1,0:T(8,128)(2,1)S(1)}, bf16[128,512]{1,0:T(8,128)(2,1)}, u32[]{:S(2)}) copy-start(bf16[128,512]{1,0:T(8,128)(2,1)} %constant.58.clone.th) | copy-start | bytes 393220
  79.6 25.0 %copy-start.13 = (bf16[512,128]{1,0:T(8,128)(2,1)S(1)}, bf16[512,128]{1,0:T(8,128)(2,1)}, u32[]{:S(2)}) copy-start(bf16[512,128]{1,0:T(8,128)(2,1)} %constant.57.clone.kl) | copy-start | bytes 393220
  79.6 25.0 %copy-start.14 = (bf16[512,128]{1,0:T(8,128)(2,1)S(1)}, bf16[512,128]{1,0:T(8,128)(2,1)}, u32[]{:S(2)}) copy-start(bf16[512,128]{1,0:T(8,128)(2,1)} %constant.56.clone.kh) | copy-start | bytes 393220
  79.6 2.7 %collective-permute-start.3 = (f32[768,128]{1,0:T(8,128)S(1)}, f32[768,128]{1,0:T(8,128)S(1)}, u32[]{:S(2)}, u32[]{:S(2)}) collective-permute-start(f32[768,128]{1,0:T(8,128)S(1)} %get-tuple-element.28.outgoing), channel_id=1, source_target_pairs={{0,1},{1,0},{2,3},{3,2},{4,5},{5,4},{6,7},{7,6},{8,9},{9,8},{10,11... | collective-permute-start | bytes 1179656 | tf_op jit(solution)/shard_map/ppermute | solution.py:491
  82.5 48.5 %copy-start.3 = (bf16[512,1024]{1,0:T(8,128)(2,1)S(1)}, bf16[512,1024]{1,0:T(8,128)(2,1)}, u32[]{:S(2)}) copy-start(bf16[512,1024]{1,0:T(8,128)(2,1)} %copy-done.2) | copy-start | bytes 3145732
  82.5 48.5 %copy-start.8 = (bf16[256,256]{1,0:T(8,128)(2,1)S(1)}, bf16[256,256]{1,0:T(8,128)(2,1)}, u32[]{:S(2)}) copy-start(bf16[256,256]{1,0:T(8,128)(2,1)} %constant.63.clone.syl) | copy-start | bytes 393220
  82.5 48.4 %copy-start.9 = (bf16[256,256]{1,0:T(8,128)(2,1)S(1)}, bf16[256,256]{1,0:T(8,128)(2,1)}, u32[]{:S(2)}) copy-start(bf16[256,256]{1,0:T(8,128)(2,1)} %constant.62.clone.syh) | copy-start | bytes 393220
  82.5 48.4 %copy-start.10 = (bf16[256,256]{1,0:T(8,128)(2,1)S(1)}, bf16[256,256]{1,0:T(8,128)(2,1)}, u32[]{:S(2)}) copy-start(bf16[256,256]{1,0:T(8,128)(2,1)} %constant.61.clone.sz) | copy-start | bytes 393220
  128.5 2.5 %collective-permute-start.4 = (f32[768,128]{1,0:T(8,128)S(1)}, f32[768,128]{1,0:T(8,128)S(1)}, u32[]{:S(2)}, u32[]{:S(2)}) collective-permute-start(f32[768,128]{1,0:T(8,128)S(1)} %bitcast.34), channel_id=1, source_target_pairs={{0,1},{1,0},{2,3},{3,2},{4,5},{5,4},{6,7},{7,6},{8,9},{9,8},{10,11... | collective-permute-start | bytes 1179656 | tf_op jit(solution)/shard_map/ppermute | solution.py:508
  132.7 18.5 %copy-start.20 = (bf16[64,512]{1,0:T(8,128)(2,1)S(1)}, bf16[64,512]{1,0:T(8,128)(2,1)}, u32[]{:S(2)}) copy-start(bf16[64,512]{1,0:T(8,128)(2,1)} %copy-done.19) | copy-start | bytes 196612
  132.7 30.2 %copy-start.6 = (f32[128,128]{1,0:T(8,128)S(1)}, f32[128,128]{1,0:T(8,128)}, u32[]{:S(2)}) copy-start(f32[128,128]{1,0:T(8,128)} %remesh.3) | copy-start | bytes 196612
  132.7 30.2 %copy-start.22 = (f32[3,16,128]{2,1,0:T(8,128)S(1)}, f32[3,16,128]{2,1,0:T(8,128)}, u32[]{:S(2)}) copy-start(f32[3,16,128]{2,1,0:T(8,128)} %copy-done.21) | copy-start | bytes 73732
  151.4 8.5 %collective-permute-start.5 = (f32[48,128]{1,0:T(8,128)S(1)}, f32[48,128]{1,0:T(8,128)S(1)}, u32[]{:S(2)}, u32[]{:S(2)}) collective-permute-start(f32[48,128]{1,0:T(8,128)S(1)} %get-tuple-element.35), channel_id=1, source_target_pairs={{128,0},{129,1},{130,2},{131,3},{132,4},{133,5},{134,6},{135,7},{1... | collective-permute-start | bytes 73736 | tf_op jit(solution)/shard_map/ppermute | solution.py:539
  152.7 7.2 %collective-permute-start.6 = (f32[48,128]{1,0:T(8,128)S(1)}, f32[48,128]{1,0:T(8,128)S(1)}, u32[]{:S(2)}, u32[]{:S(2)}) collective-permute-start(f32[48,128]{1,0:T(8,128)S(1)} %get-tuple-element.36), channel_id=1, source_target_pairs={{128,8},{129,9},{130,10},{131,11},{132,12},{133,13},{134,14},{135,... | collective-permute-start | bytes 73736 | tf_op jit(solution)/shard_map/ppermute | solution.py:539
  154.0 7.0 %collective-permute-start.7 = (f32[48,128]{1,0:T(8,128)S(1)}, f32[48,128]{1,0:T(8,128)S(1)}, u32[]{:S(2)}, u32[]{:S(2)}) collective-permute-start(f32[48,128]{1,0:T(8,128)S(1)} %get-tuple-element.37), channel_id=1, source_target_pairs={{128,16},{129,17},{130,18},{131,19},{132,20},{133,21},{134,22},{13... | collective-permute-start | bytes 73736 | tf_op jit(solution)/shard_map/ppermute | solution.py:539
  155.3 7.6 %collective-permute-start.8 = (f32[48,128]{1,0:T(8,128)S(1)}, f32[48,128]{1,0:T(8,128)S(1)}, u32[]{:S(2)}, u32[]{:S(2)}) collective-permute-start(f32[48,128]{1,0:T(8,128)S(1)} %get-tuple-element.38), channel_id=1, source_target_pairs={{128,24},{129,25},{130,26},{131,27},{132,28},{133,29},{134,30},{13... | collective-permute-start | bytes 73736 | tf_op jit(solution)/shard_map/ppermute | solution.py:539
  (7 other events, 4.6 us)

commit v2 on v1

--- a/solution.py
+++ b/solution.py
@@ -111,8 +111,15 @@
     return jnp.sum(matches * counts, axis=0, keepdims=True).astype(i32)
 
 
-def route_kernel(flags, sd, sr, rd, rr, rb, remesh, sz, place, gather, codes, merged):
-    zme = flags[3]
+def owners(owner):
+    core = owner & (CC - 1)
+    x = (owner >> 1) & (CX - 1)
+    z = (owner >> 3) & (CZ - 1)
+    lane = z * CAP + ranks(jnp.where(iota((BRICKS, SB), 0) == owner, 1.0, 0.0))
+    return owner >> 5, z, x, core, lane
+
+
+def route_kernel(flags, sd, sr, rd, rb, remesh, sz, place, codes, merged):
     bricks = iota((BRICKS, SB), 0)
     matches = jnp.where(bricks == sd[...], 1.0, 0.0)
     rank = ranks(matches)
@@ -120,26 +127,13 @@
     place[...] = onehot(iota((SLOTS, SB), 0) == slot)
     tagged = jnp.where(bricks == rank, (sr[...] + 1).astype(f32), 0.0)
     sent = exact(matches, tagged, NT)
-    owner = rd[...]
-    oc = owner & (CC - 1)
-    ox = (owner >> 1) & (CX - 1)
-    oz = (owner >> 3) & (CZ - 1)
-    oy = owner >> 5
-    rank = ranks(jnp.where(bricks == owner, 1.0, 0.0))
-    lane = oz * CAP + rank
-    slot = ((oy * CX + ox) * CC + oc) * GROUP + lane
-    gather[...] = lax.dot_general(
-        onehot(iota((SLOTS, SB), 0) == slot),
-        onehot(iota((RPB, SB), 0) == rr[...]),
-        NT,
-        preferred_element_type=f32,
-    ).astype(bf16)
-    via = ((oy * CZ + zme) * CX + ox) * CC + oc
-    code = ((oz - zme) & (CZ - 1)) * NJ + rb[...] + 1
+    zme = flags[3]
+    y, z, x, core, lane = owners(rd[...])
+    via = ((y * CZ + zme) * CX + x) * CC + core
+    code = ((z - zme) & (CZ - 1)) * NJ + rb[...] + 1
     tagged = jnp.where(bricks == lane + CAP, code.astype(f32), 0.0)
     codes[...] = sent + exact(jnp.where(bricks == via, 1.0, 0.0), tagged, NT)
-    both = exact(remesh[...], sz[...])
-    high, low = split(both)
+    high, low = split(exact(remesh[...], sz[...]))
     merged[...] = jnp.concatenate(
         [
             jnp.concatenate([high, low], axis=1),
@@ -149,23 +143,35 @@
     )
 
 
-def decode_kernel(flags, codes, landing, cells):
-    zme = flags[3]
-    turned = codes[...].T
-    landing[...] = jnp.concatenate([turned[i : i + 1, :] for i in range(CAP)], axis=1).astype(i32)
-    target = iota((TARGETS, BRICKS), 0)
-    source = ((target >> 3) * CZ + zme) * (CX * CC) + (target & (CX * CC - 1))
-    chosen = exact(jnp.where(iota((TARGETS, BRICKS), 1) == source, 1.0, 0.0), codes[...])
-    wide = jnp.where(
-        iota((BRICKS, SLOTS), 0) == (iota((BRICKS, SLOTS), 1) & (GROUP - 1)) + CAP, 1.0, 0.0
-    )
-    chosen = exact(chosen, wide)
-    own = iota((TARGETS, SLOTS), 0) == (iota((TARGETS, SLOTS), 1) >> 4)
-    code = jnp.sum(jnp.where(own, chosen, 0.0), axis=0, keepdims=True).astype(i32)
-    cells[...] = onehot(iota((CZ * NJ, SLOTS), 0) == code - 1)
-
-
-def local_kernel(flags, state, courant, up, down, sz, out, layer):
+def decode_kernel(flags, codes, rd, rr, landing, cells, gather):
+    @pl.when(flags[0] != 0)
+    def _():
+        zme = flags[3]
+        turned = codes[...].T
+        landing[...] = jnp.concatenate(
+            [turned[i : i + 1, :] for i in range(CAP)], axis=1
+        ).astype(i32)
+        target = iota((TARGETS, BRICKS), 0)
+        source = ((target >> 3) * CZ + zme) * (CX * CC) + (target & (CX * CC - 1))
+        chosen = exact(jnp.where(iota((TARGETS, BRICKS), 1) == source, 1.0, 0.0), codes[...])
+        wide = jnp.where(
+            iota((BRICKS, SLOTS), 0) == (iota((BRICKS, SLOTS), 1) & (GROUP - 1)) + CAP, 1.0, 0.0
+        )
+        chosen = exact(chosen, wide)
+        own = iota((TARGETS, SLOTS), 0) == (iota((TARGETS, SLOTS), 1) >> 4)
+        code = jnp.sum(jnp.where(own, chosen, 0.0), axis=0, keepdims=True).astype(i32)
+        cells[...] = onehot(iota((CZ * NJ, SLOTS), 0) == code - 1)
+        y, _, x, core, lane = owners(rd[...])
+        slot = ((y * CX + x) * CC + core) * GROUP + lane
+        gather[...] = lax.dot_general(
+            onehot(iota((SLOTS, SB), 0) == slot),
+            onehot(iota((RPB, SB), 0) == rr[...]),
+            NT,
+            preferred_element_type=f32,
+        ).astype(bf16)
+
+
+def near_kernel(flags, state, courant, up, down, out, edge, layer):
     @pl.when(flags[0] == 0)
     def _():
         cr = jnp.concatenate([up[768:896, :], courant[...], down[768:896, :]], axis=0)
@@ -187,23 +193,39 @@
                 [up[c * 256 : (c + 1) * 256, :], state[c], down[c * 256 : (c + 1) * 256, :]], axis=0
             )
             field = step(field, cr)
-            out[c] = step(field, courant[...])
+            field = step(field, courant[...])
+            out[c] = field
+            edge[c] = field.reshape(NJ, NI, NK)[:, NI - 8 :, :]
             layer[c] = state[c, pl.ds(NI - 1, NJ, stride=NI), :]
 
+
+def ready_kernel(flags, state, speed, sz, kh, kl, out, th, tl, last, lead):
+    @pl.when(flags[0] == 0)
+    def _():
+        for c in range(3):
+            last[c * 256 : (c + 1) * 256, :] = state[c, 768:, :]
+            lead[c * 256 : (c + 1) * 256, :] = state[c, :256, :]
+        last[768:, :] = speed[896:, :]
+        lead[768:, :] = speed[:128, :]
+
     @pl.when(flags[0] != 0)
     def _():
         for c in range(3):
             out[c] = times_paired(state[c], sz[...])
-
-
-def bucket_kernel(blocks, place, merged, out):
-    for c in range(3):
-        moved = times_paired(blocks[c], merged[...])
-        slots = pick(place[...], moved)
-        for rank in range(CAP):
-            out[pl.ds(c * CAP + rank, BRICKS, stride=3 * CAP), :] = slots[
-                rank * BRICKS : (rank + 1) * BRICKS
-            ]
+        th[...] = kh[...].T
+        tl[...] = kl[...].T
+
+
+def bucket_kernel(flags, blocks, place, merged, out):
+    @pl.when(flags[0] != 0)
+    def _():
+        for c in range(3):
+            moved = times_paired(blocks[c], merged[...])
+            slots = pick(place[...], moved)
+            for rank in range(CAP):
+                out[pl.ds(c * CAP + rank, BRICKS, stride=3 * CAP), :] = slots[
+                    rank * BRICKS : (rank + 1) * BRICKS
+                ]
 
 
 def weights(beta):
@@ -215,57 +237,63 @@
 
 
 def forward_kernel(flags, received, landing, work, syh, syl, mu, planes, outgoing, kept):
-    beta = mu[...] + 2.0
-    g11, g12, g13 = weights(beta)
-    first = flags[1] == 0
-    spread = onehot(iota((RPB, SLOTS), 0) == landing[...] - 1)
-    for c in range(3):
-        rows = jnp.concatenate(
-            [received[pl.ds(c * CAP + r, BRICKS, stride=3 * CAP), :] for r in range(CAP)], axis=0
-        )
-        field = pick(spread, rows) + work[c]
-        field = jnp.concatenate([field[p * NY : (p + 1) * NY] for p in range(4)], axis=1)
-        field = table_times(syh[...], syl[...], field)
-        f0, f1, f2, f3 = (field[:, p * NZ : (p + 1) * NZ] for p in range(4))
-        for p, plane in enumerate((f0, f1, f2, f3)):
-            planes[c, p] = plane
-        low = g11 * f0 + g12 * f1 + g13 * f2
-        high = f3 + g13 * f0 + g12 * f1 + g11 * f2
-        outgoing[c * NY : (c + 1) * NY, :] = jnp.where(first, high, low)
-        kept[c * NY : (c + 1) * NY, :] = jnp.where(first, low, high)
-
-
-def reduce_kernel(outgoing, incoming, kept, mu, out):
-    g11, g12, g13 = weights(mu[...] + 2.0)
-    ratio = g13 / (mu[...] + 2.0 - 2.0 * g11)
-    for c in range(3):
-        block = slice(c * NY, (c + 1) * NY)
-        share = kept[block, :] + ratio * (outgoing[block, :] + incoming[block, :])
+    @pl.when(flags[0] != 0)
+    def _():
+        beta = mu[...] + 2.0
+        g11, g12, g13 = weights(beta)
+        first = flags[1] == 0
+        spread = onehot(iota((RPB, SLOTS), 0) == landing[...] - 1)
+        for c in range(3):
+            rows = jnp.concatenate(
+                [received[pl.ds(c * CAP + r, BRICKS, stride=3 * CAP), :] for r in range(CAP)], axis=0
+            )
+            field = (pick(spread, rows) + work[c]) * (4.0 / ((NY + 1) * (NZ + 1)))
+            field = jnp.concatenate([field[p * NY : (p + 1) * NY] for p in range(4)], axis=1)
+            field = table_times(syh[...], syl[...], field)
+            f0, f1, f2, f3 = (field[:, p * NZ : (p + 1) * NZ] for p in range(4))
+            for p, plane in enumerate((f0, f1, f2, f3)):
+                planes[c, p] = plane
+            low = g11 * f0 + g12 * f1 + g13 * f2
+            high = f3 + g13 * f0 + g12 * f1 + g11 * f2
+            outgoing[c * NY : (c + 1) * NY, :] = jnp.where(first, high, low)
+            kept[c * NY : (c + 1) * NY, :] = jnp.where(first, low, high)
+
+
+def reduce_kernel(flags, outgoing, incoming, kept, mu, out):
+    @pl.when(flags[0] != 0)
+    def _():
+        g11, g12, g13 = weights(mu[...] + 2.0)
+        ratio = g13 / (mu[...] + 2.0 - 2.0 * g11)
+        for c in range(3):
+            block = slice(c * NY, (c + 1) * NY)
+            share = kept[block, :] + ratio * (outgoing[block, :] + incoming[block, :])
+            for i in range(2):
+                out[pl.ds(c * 2 + i, BRICKS, stride=6), :] = share[i * BRICKS : (i + 1) * BRICKS]
+
+
+def line_kernel(flags, received, kh, kl, th, tl, lamx, mu, out):
+    @pl.when(flags[0] != 0)
+    def _():
+        shares = jnp.concatenate([received[pl.ds(j, BRICKS, stride=6), :] for j in range(6)], axis=1)
+        modes = table_times(kh[...], kl[...], shares)
+        factors = []
         for i in range(2):
-            out[pl.ds(c * 2 + i, BRICKS, stride=6), :] = share[i * BRICKS : (i + 1) * BRICKS]
-
-
-def line_kernel(flags, received, kh, kl, th, tl, lamx, mu, out):
-    shares = jnp.concatenate([received[pl.ds(j, BRICKS, stride=6), :] for j in range(6)], axis=1)
-    modes = table_times(kh[...], kl[...], shares)
-    factors = []
-    for i in range(2):
-        row = mu[pl.ds(flags[2] + i * BRICKS, 1), :]
-        factors.append((2.0 / (NX + 1)) / (lamx[...] + row))
-    modes = modes * jnp.concatenate(factors * 3, axis=1)
-    solved = table_times(th[...], tl[...], modes)
-    for j in range(6):
-        out[pl.ds(j, BRICKS, stride=6), :] = solved[:, j * NZ : (j + 1) * NZ]
+            row = mu[pl.ds(flags[2] + i * BRICKS, 1), :]
+            factors.append((2.0 / (NX + 1)) / (lamx[...] + row))
+        modes = modes * jnp.concatenate(factors * 3, axis=1)
+        solved = table_times(th[...], tl[...], modes)
+        for j in range(6):
+            out[pl.ds(j, BRICKS, stride=6), :] = solved[:, j * NZ : (j + 1) * NZ]
 
 
 def inverse_kernel(
     flags,
+    advanced,
     planes,
     outgoing,
     incoming,
     own,
     other,
-    work,
     gather,
     sz,
     syh,
@@ -278,12 +306,6 @@
     out_sems,
     send_sems,
 ):
-    @pl.when(flags[0] == 0)
-    def _():
-        copy = pltpu.make_async_copy(work, out, out_sems.at[0])
-        copy.start()
-        copy.wait()
-
     @pl.when(flags[0] != 0)
     def _():
         beta = mu[...] + 2.0
@@ -354,15 +376,17 @@
             copy.wait()
 
 
-def cell_kernel(received, cells, *outs):
-    for c in range(3):
-        rows = received[:, c * GROUP : (c + 1) * GROUP, :].reshape(SLOTS, NZ)
-        sums = pick(cells[...], rows)
-        for k in range(CZ):
-            outs[k][c * NJ : (c + 1) * NJ, :] = sums[k * NJ : (k + 1) * NJ]
-
-
-def close_kernel(flags, field, work, layer, remesh, b0, b1, b2, b3, out, slab, sem):
+def cell_kernel(flags, received, cells, *outs):
+    @pl.when(flags[0] != 0)
+    def _():
+        for c in range(3):
+            rows = received[:, c * GROUP : (c + 1) * GROUP, :].reshape(SLOTS, NZ)
+            sums = pick(cells[...], rows)
+            for k in range(CZ):
+                outs[k][c * NJ : (c + 1) * NJ, :] = sums[k * NJ : (k + 1) * NJ]
+
+
+def close_kernel(flags, field, edge, layer, remesh, b0, b1, b2, b3, out, slab, sem):
     @pl.when(flags[0] == 0)
     def _():
         total = exact((b0[...] + b1[...]) + (b2[...] + b3[...]), remesh[...], NT)
@@ -371,34 +395,67 @@
         for c in range(3):
             d, e = (c + 1) % 3, (c + 2) % 3
             cross = first[d] * second[e] - first[e] * second[d]
-            for j in range(NJ):
-                row = c * RPB + (j + 1) * NI
-                slab[c, j, :7, :] = work[c, row - c * RPB - 8 : row - c * RPB - 1, :]
-            slab[c, :, 7, :] = work[c, pl.ds(NI - 1, NJ, stride=NI), :] + coupling * cross
+            slab[c] = edge[c]
+            slab[c, :, 7, :] = edge[c, :, 7, :] + coupling * cross
         copy = pltpu.make_async_copy(slab, out.at[:, :, pl.ds(NI - 8, 8), :], sem)
         copy.start()
         copy.wait()
 
 
-def call(kernel, outs, flags, *args, home=pltpu.VMEM, alias=False, scratch=(), free=False):
-    scalars = [] if flags is None else [flags]
+def call(kernel, outs, flags, *args, fetch=False, raw=False, alias=False, scratch=()):
     args = [jnp.asarray(a) for a in args]
-    kept = [args.pop(0)] if alias else []
+    spaces = [pltpu.HBM if fetch or (alias and i == 0) else pltpu.VMEM for i in range(len(args))]
+    homes = [raw or len(o) > 2 for o in outs]
+    staged = [] if raw else [i for i, home in enumerate(homes) if home]
+    loads = [pltpu.VMEM(a.shape, a.dtype) for a in args] if fetch else []
+    stores = [pltpu.VMEM(*outs[i][:2]) for i in staged]
+    sems = [pltpu.SemaphoreType.DMA((len(loads) + len(stores),))] if loads or stores else []
+
+    def body(flags, *refs):
+        given, made = list(refs[: len(args)]), list(refs[len(args) : len(args) + len(outs)])
+        rest = refs[len(args) + len(outs) :]
+        held, kept = rest[: len(loads)], rest[len(loads) : len(loads) + len(stores)]
+        own = rest[len(loads) + len(stores) + len(sems) :]
+        if sems:
+            sem = rest[len(loads) + len(stores)]
+        copies = [
+            pltpu.make_async_copy(a, b, sem.at[i]) for i, (a, b) in enumerate(zip(given, held))
+        ]
+        for copy in copies:
+            copy.start()
+        for copy in copies:
+            copy.wait()
+        homes_out = [made[i] for i in staged]
+        for i, ref in zip(staged, kept):
+            made[i] = ref
+        kernel(flags, *(held if fetch else given), *made, *own)
+        copies = [
+            pltpu.make_async_copy(a, b, sem.at[len(loads) + i])
+            for i, (a, b) in enumerate(zip(kept, homes_out))
+        ]
+        for copy in copies:
+            copy.start()
+        for copy in copies:
+            copy.wait()
+
     return pl.pallas_call(
-        kernel,
-        out_shape=[(jax.ShapeDtypeStruct if free else home)(s, d) for s, d in outs],
-        in_specs=[pl.BlockSpec(memory_space=pltpu.SMEM)] * len(scalars)
-        + [pl.BlockSpec(memory_space=pltpu.HBM)] * len(kept)
-        + [pl.BlockSpec(memory_space=pltpu.VMEM)] * len(args),
-        out_specs=[pl.BlockSpec(memory_space=home)] * len(outs),
-        scratch_shapes=list(scratch),
-        input_output_aliases={len(scalars): 0} if alias else {},
+        body,
+        out_shape=[(pltpu.HBM if home else pltpu.VMEM)(*o[:2]) for o, home in zip(outs, homes)],
+        in_specs=[pl.BlockSpec(memory_space=pltpu.SMEM)]
+        + [pl.BlockSpec(memory_space=space) for space in spaces],
+        out_specs=[
+            pl.BlockSpec(memory_space=pltpu.HBM if home else pltpu.VMEM) for home in homes
+        ],
+        scratch_shapes=loads + stores + sems + list(scratch),
+        input_output_aliases={1: 0} if alias else {},
         compiler_params=pltpu.CompilerParams(vmem_limit_bytes=24 << 20),
         name=kernel.__name__,
     )(
-        *scalars,
-        *kept,
-        *[a if free else pltpu.with_memory_space_constraint(a, pltpu.VMEM) for a in args],
+        flags,
+        *[
+            a if alias and i == 0 else pltpu.with_memory_space_constraint(a, space)
+            for i, (a, space) in enumerate(zip(args, spaces))
+        ],
     )
 
 
@@ -421,10 +478,8 @@
     speed = courant.reshape(RPB, NK)
     sy, sz, line = sines(NY), sines(NZ), line_table()
     syh, syl = halves(sy)
-    iyh, iyl = halves(sy * (2.0 / (NY + 1)))
-    szp, izp = paired(sz), paired(sz * (2.0 / (NZ + 1)))
+    szp = paired(sz)
     kh, kl = halves(line)
-    th, tl = np.ascontiguousarray(kh.T), np.ascontiguousarray(kl.T)
     lamx = eigen(NX).astype(np.float32)[:, None]
     mu = (eigen(NY)[:, None] + eigen(NZ)[None, :]).astype(np.float32)
 
@@ -432,64 +487,79 @@
     across = [(place_of(0, *q), place_of(1, *q)) for q in chips()]
     blocks = lax.ppermute(blocks, ALL, across)
 
+    sd, sr, rd, rr, rb = (
+        v.reshape(1, SB) for v in (shell_dest, shell_row, return_dest, return_row, return_block)
+    )
+    place, codes, merged = call(
+        route_kernel,
+        [((SLOTS, SB), bf16), ((BRICKS, NZ), f32, "home"), ((2 * NK, 2 * NZ), bf16)],
+        flags,
+        sd,
+        sr,
+        rd,
+        rb,
+        remesh,
+        sz.astype(np.float32),
+        fetch=True,
+    )
+    codes = lax.all_to_all(codes.reshape(BRICKS, 1, NZ), DEV, 0, 0, tiled=True)
+    landing, cells, gather = call(
+        decode_kernel,
+        [((1, SLOTS), i32), ((CZ * NJ, SLOTS), bf16, "home"), ((SLOTS, RPB), bf16, "home")],
+        flags,
+        codes.reshape(BRICKS, NZ),
+        rd,
+        rr,
+        fetch=True,
+    )
+    turned, th, tl, last, lead = call(
+        ready_kernel,
+        [
+            ((3, RPB, NZ), f32),
+            ((BRICKS, NX), bf16, "home"),
+            ((BRICKS, NX), bf16, "home"),
+            ((896, NK), f32, "home"),
+            ((896, NK), f32, "home"),
+        ],
+        flags,
+        field,
+        speed,
+        szp,
+        kh,
+        kl,
+        fetch=True,
+    )
     ahead = [(d, (d + 1) % BRICKS) for d in range(BRICKS)]
-    last = jnp.concatenate([field[:, 768:, :].reshape(768, NK), speed[896:, :]], axis=0)
-    lead = jnp.concatenate([field[:, :256, :].reshape(768, NK), speed[:128, :]], axis=0)
     up = lax.ppermute(last, ALL, ahead)
     down = lax.ppermute(lead, ALL, [(b, a) for a, b in ahead])
-
-    rows = [
-        v.reshape(1, SB) for v in (shell_dest, shell_row, return_dest, return_row, return_block)
-    ]
-    place, gather, codes, merged = call(
-        route_kernel,
-        [
-            ((SLOTS, SB), bf16),
-            ((SLOTS, RPB), bf16),
-            ((BRICKS, NZ), f32),
-            ((2 * NK, 2 * NZ), bf16),
-        ],
-        flags,
-        *rows,
-        remesh,
-        sz.astype(np.float32),
-        free=True,
-    )
-    codes = lax.all_to_all(codes.reshape(BRICKS, 1, NZ), DEV, 0, 0, tiled=True)
-    landing, cells = call(
-        decode_kernel,
-        [((1, SLOTS), i32), ((CZ * NJ, SLOTS), bf16)],
-        flags,
-        codes.reshape(BRICKS, NZ),
-        free=True,
-    )
-    work, layer = call(
-        local_kernel,
-        [((3, RPB, NK), f32), ((3, NJ, NK), f32)],
+    advanced, edge, layer = call(
+        near_kernel,
+        [((3, RPB, NK), f32, "home"), ((3, NJ, 8, NK), f32, "home"), ((3, NJ, NK), f32, "home")],
         flags,
         field,
         speed,
         up,
         down,
-        szp,
-    )
-
-    (bundle,) = call(bucket_kernel, [((3 * SLOTS, NZ), f32)], None, blocks, place, merged)
+        fetch=True,
+    )
+
+    (bundle,) = call(bucket_kernel, [((3 * SLOTS, NZ), f32)], flags, blocks, place, merged)
     bundle = lax.all_to_all(bundle.reshape(BRICKS, 3, CAP, NZ), DEV, 0, 0, tiled=True)
+    bundle, advanced, gather = lax.optimization_barrier((bundle, advanced, gather))
     planes, outgoing, kept = call(
         forward_kernel,
         [((3, 4, NY, NZ), f32), ((3 * NY, NZ), f32), ((3 * NY, NZ), f32)],
         flags,
         bundle.reshape(3 * SLOTS, NZ),
         landing,
-        work,
+        turned,
         syh,
         syl,
         mu,
     )
     swap = [(0, 1), (1, 0)]
     incoming = lax.ppermute(outgoing, "core", swap)
-    (share,) = call(reduce_kernel, [((3 * NY, NZ), f32)], None, outgoing, incoming, kept, mu)
+    (share,) = call(reduce_kernel, [((3 * NY, NZ), f32)], flags, outgoing, incoming, kept, mu)
     share = lax.all_to_all(share.reshape(BRICKS, 3, 2, NZ), DEV, 0, 0, tiled=True)
     (solved,) = call(
         line_kernel,
@@ -510,18 +580,19 @@
         inverse_kernel,
         [((3, RPB, NZ), f32), ((TARGETS, 3 * GROUP, NZ), f32)],
         flags,
+        advanced,
         planes,
         outgoing,
         incoming,
         own,
         other,
-        work,
         gather,
-        izp,
-        iyh,
-        iyl,
+        szp,
+        syh,
+        syl,
         mu,
-        home=pltpu.HBM,
+        raw=True,
+        alias=True,
         scratch=[
             pltpu.VMEM((3, RPB, NZ), f32),
             pltpu.VMEM((3, TARGETS, GROUP, NZ), f32),
@@ -530,7 +601,7 @@
         ],
     )
     returned = lax.all_to_all(send, ("y", "x", "core"), 0, 0, tiled=True)
-    sums = call(cell_kernel, [((3 * NJ, NZ), f32)] * CZ, None, returned, cells)
+    sums = call(cell_kernel, [((3 * NJ, NZ), f32)] * CZ, flags, returned, cells)
     parts = []
     for k in range(CZ):
         pairs = [
@@ -542,11 +613,11 @@
         [((3, NJ, NI, NZ), f32)],
         flags,
         result.reshape(3, NJ, NI, NZ),
-        work,
+        edge,
         layer,
         remesh,
         *parts,
-        home=pltpu.HBM,
+        raw=True,
         alias=True,
         scratch=[pltpu.VMEM((3, NJ, 8, NZ), f32), pltpu.SemaphoreType.DMA],
     )

time: 165 us -> 159 us (0.964)
  local copies, waits for them, and re-layouts: 9.32 us -> 1.91 us
  waiting for transfers between devices: 34.3 us -> 29.6 us
  starting transfers between devices: 40.6 us -> 44 us
  Pallas kernels: 17.5 us -> 20.2 us
    unnamed x56 -> x34, local copies, waits for them, and re-layouts: 7.35 us -> 0.88 us
    all_to_all x1, waiting for transfers between devices: 9.03 us -> 3.79 us  [on_device(): lax.all_to_all(bundle.reshape(BRICKS, 3, CAP, NZ), DEV, 0, 0, tiled=True)]
    ppermute x1, starting transfers between devices: 1.35 us -> 5.33 us  [on_device(): incoming = lax.ppermute(outgoing, 'core', swap)]
    pallas_call x10 -> x11, Pallas kernels: 17.5 us -> 20.2 us  [call(): pl.pallas_call(body, out_shape=[(pltpu.HBM if home else pltpu.VMEM)(*o[:2...]
  transfers between devices with their start and end apart: 11 -> 11, of which waited for: 9 -> 9; matrix products, arithmetic and copies ran while one was open for 1% -> 0% of each run, Pallas kernels for 5% -> 10%
where the time goes in v2:
time: 159 us; the launch traced here: 158 us
  blocking collectives  62 us (39%)
  starting transfers between devices  44 us (28%)
  waiting for transfers between devices  29.6 us (19%)
  Pallas kernels  20.2 us (13%)
  local copies, waits for them, and re-layouts  1.91 us (1%)
    all_to_all x1, blocking collectives, on_device(): lax.all_to_all(share.reshape(BRICKS, 3, 2, NZ), DEV, 0, 0, tiled=True)  22 us
    all_to_all x1, blocking collectives, on_device(): lax.all_to_all(solved.reshape(BRICKS, 3, 2, NZ), DEV, 0, 0, tiled=True)  21.6 us
    pallas_call x11, Pallas kernels, call(): pl.pallas_call(body, out_shape=[(pltpu.HBM if home else pltpu.VMEM)(*o[:2...  20.2 us
    all_to_all x1, blocking collectives, on_device(): returned = lax.all_to_all(send, ('y', 'x', 'core'), 0, 0, tiled=True)  18.4 us
    all_to_all x1, starting transfers between devices, on_device(): codes = lax.all_to_all(codes.reshape(BRICKS, 1, NZ), DEV, 0, 0, tiled=True)  10.6 us
    ppermute x1, starting transfers between devices, on_device(): blocks = lax.ppermute(blocks, ALL, across)  9.66 us
    all_to_all x1, waiting for transfers between devices, on_device(): codes = lax.all_to_all(codes.reshape(BRICKS, 1, NZ), DEV, 0, 0, tiled=True)  9.49 us
    all_to_all x1, starting transfers between devices, on_device(): lax.all_to_all(bundle.reshape(BRICKS, 3, CAP, NZ), DEV, 0, 0, tiled=True)  6.53 us
  transfers between devices with their start and end apart: 11, of which 9 were waited for; matrix products, arithmetic and copies ran while one was open for 0% of the time, Pallas kernels for 10%

profile of v2, /device:TPU:1, one launch (start us, length us, event | category | flops | bytes accessed | tf_op | source)
XLA Modules:
  0.0 158.2 jit_solution(17531517708526188868)
XLA Ops:
  0.0 1.0 slice.4
  1.0 9.7 %collective-permute-start = (f32[3,256,128]{2,1,0:T(8,128)S(1)}, f32[3,256,128]{2,1,0:T(8,128)S(1)}, u32[]{:S(2)}, u32[]{:S(2)}) collective-permute-start(f32[3,256,128]{2,1,0:T(8,128)S(1)} %bitcast.37), channel_id=1, source_target_pairs={{0,128},{1,129},{2,130},{3,131},{4,132},{5,133},{6,134},{7,135},{8... | collective-permute-start | bytes 1179656 | tf_op jit(solution)/shard_map/ppermute | solution.py:488
  10.8 3.0 %route_kernel.1 = (bf16[512,256]{1,0:T(8,128)(2,1)S(1)}, f32[128,128]{1,0:T(8,128)}, bf16[256,256]{1,0:T(8,128)(2,1)S(1)}) custom-call(s32[4]{0:T(128)S(1)} %pad_add_fusion.flags, s32[1,256]{1,0:T(1,128)} %bitcast.42, s32[1,256]{1,0:T(1,128)} %bitcast.43, s32[1,256]{1,0:T(1,128)} %bitcast.40, s32[1,256]{1,0:T(1,128)} %bitcast.44, f32[128,128]{1,0:T(8,128)} %refs_3_.4, ...), custom_call_target="tpu_custom_call" | custom-call | tf_op jit(solution)/shard_map/route_kernel/pallas_call | solution.py:441
  13.8 10.6 %all-to-all-start.1 = ((f32[128,1,128]{2,1,0:T(1,128)}), f32[128,1,128]{2,1,0:T(1,128)S(1)}, u32[]{:S(2)}, u32[]{:S(2)}) async-start(f32[128,1,128]{2,1,0:T(1,128)} %bitcast.39), calls=%async_computation.1 | async-start | bytes 131072 | tf_op jit(solution)/shard_map/all_to_all | solution.py:505
  24.4 1.5 bucket_kernel.1
  25.8 9.5 %all-to-all-done.1 = f32[128,1,128]{2,1,0:T(1,128)S(1)} async-done(((f32[128,1,128]{2,1,0:T(1,128)}), f32[128,1,128]{2,1,0:T(1,128)S(1)}, u32[]{:S(2)}, u32[]{:S(2)}) %all-to-all-start.1) | async-done | bytes 65568 | tf_op jit(solution)/shard_map/all_to_all | solution.py:505
  35.3 6.5 %all-to-all-start = ((f32[128,3,4,128]{3,2,1,0:T(4,128)}), f32[128,3,4,128]{3,2,1,0:T(4,128)S(1)}, u32[]{:S(2)}, u32[]{:S(2)}) async-start(f32[128,3,4,128]{3,2,1,0:T(4,128)} %bitcast.10), calls=%async_computation | async-start | bytes 1572864 | tf_op jit(solution)/shard_map/all_to_all | solution.py:547
  41.9 3.3 %ready_kernel.1 = (f32[3,1024,128]{2,1,0:T(8,128)S(1)}, bf16[128,512]{1,0:T(8,128)(2,1)}, bf16[128,512]{1,0:T(8,128)(2,1)}, f32[896,128]{1,0:T(8,128)}, f32[896,128]{1,0:T(8,128)}) custom-call(s32[4]{0:T(128)S(1)} %pad_add_fusion.flags, f32[3,1024,128]{2,1,0:T(8,128)} %bitcast.32, f32[1024,128]{1,0:T(8,128)} %bitcast.35, ...), custom_call_target="tpu_custom_call" | custom-call | tf_op jit(solution)/shard_map/ready_kernel/pallas_call | solution.py:441
  45.2 3.7 %collective-permute-start.1 = (f32[896,128]{1,0:T(8,128)}, f32[896,128]{1,0:T(8,128)S(1)}, u32[]{:S(2)}, u32[]{:S(2)}) collective-permute-start(f32[896,128]{1,0:T(8,128)} %get-tuple-element.33), channel_id=1, source_target_pairs={{0,1},{1,2},{2,3},{3,4},{4,5},{5,6},{6,7},{7,8},{8,9},{9,10},{10,1... | collective-permute-start | bytes 1376264 | tf_op jit(solution)/shard_map/ppermute | solution.py:533
  48.9 1.9 %collective-permute-start.2 = (f32[896,128]{1,0:T(8,128)}, f32[896,128]{1,0:T(8,128)S(1)}, u32[]{:S(2)}, u32[]{:S(2)}) collective-permute-start(f32[896,128]{1,0:T(8,128)} %get-tuple-element.34), channel_id=1, source_target_pairs={{1,0},{2,1},{3,2},{4,3},{5,4},{6,5},{7,6},{8,7},{9,8},{10,9},{11,1... | collective-permute-start | bytes 1376264 | tf_op jit(solution)/shard_map/ppermute | solution.py:534
  50.9 2.4 %decode_kernel.1 = (s32[1,512]{1,0:T(1,128)S(1)}, bf16[64,512]{1,0:T(8,128)(2,1)}, bf16[512,1024]{1,0:T(8,128)(2,1)}) custom-call(s32[4]{0:T(128)S(1)} %pad_add_fusion.flags, f32[128,128]{1,0:T(8,128)} %bitcast.38, s32[1,256]{1,0:T(1,128)} %bitcast.41, s32[1,256]{1,0:T(1,128)} %bitcast.45), custom_call_target="tpu_custom_call" | custom-call | tf_op jit(solution)/shard_map/decode_kernel/pallas_call | solution.py:441
  53.3 3.1 %collective-permute-done.1.refs_2_ = f32[896,128]{1,0:T(8,128)S(1)} collective-permute-done((f32[896,128]{1,0:T(8,128)}, f32[896,128]{1,0:T(8,128)S(1)}, u32[]{:S(2)}, u32[]{:S(2)}) %collective-permute-start.1) | collective-permute-done | bytes 458784 | tf_op jit(solution)/shard_map/ppermute | solution.py:533
  56.4 4.1 %collective-permute-done.2.refs_3_ = f32[896,128]{1,0:T(8,128)S(1)} collective-permute-done((f32[896,128]{1,0:T(8,128)}, f32[896,128]{1,0:T(8,128)S(1)}, u32[]{:S(2)}, u32[]{:S(2)}) %collective-permute-start.2) | collective-permute-done | bytes 458784 | tf_op jit(solution)/shard_map/ppermute | solution.py:534
  60.6 0.8 copy-done.15
  61.4 5.5 %near_kernel.1 = (f32[3,1024,128]{2,1,0:T(8,128)}, f32[3,16,8,128]{3,2,1,0:T(8,128)}, f32[3,16,128]{2,1,0:T(8,128)}) custom-call(s32[4]{0:T(128)S(1)} %pad_add_fusion.flags, f32[3,1024,128]{2,1,0:T(8,128)} %bitcast.33, f32[1024,128]{1,0:T(8,128)} %bitcast.36, f32[896,128]{1,0:T(8,128)} %copy-done.14, f32[896,128]{1,0:T(8,128)} %copy-done.15), custom_call_target="tpu_custom_call" | custom-call | tf_op jit(solution)/shard_map/near_kernel/pallas_call | solution.py:441
  66.9 3.8 %all-to-all-done = f32[128,3,4,128]{3,2,1,0:T(4,128)S(1)} async-done(((f32[128,3,4,128]{3,2,1,0:T(4,128)}), f32[128,3,4,128]{3,2,1,0:T(4,128)S(1)}, u32[]{:S(2)}, u32[]{:S(2)}) %all-to-all-start) | async-done | bytes 786464 | tf_op jit(solution)/shard_map/all_to_all | solution.py:547
  71.4 5.3 %collective-permute-start.3 = (f32[768,128]{1,0:T(8,128)S(1)}, f32[768,128]{1,0:T(8,128)S(1)}, u32[]{:S(2)}, u32[]{:S(2)}) collective-permute-start(f32[768,128]{1,0:T(8,128)S(1)} %get-tuple-element.43.refs_0_.refs_2_), channel_id=1, source_target_pairs={{0,1},{1,0},{2,3},{3,2},{4,5},{5,4},{6,7},{7,6},{8,9},{9,8},{10,11... | collective-permute-start | bytes 1179656 | tf_op jit(solution)/shard_map/ppermute | solution.py:561
  76.7 1.3 collective-permute-done.3.refs_1_.refs_3_
  78.0 0.7 reduce_kernel.1
  78.8 22.0 %all_to_all.25 = f32[128,3,2,128]{3,2,1,0:T(2,128)S(1)} all-to-all(f32[128,3,2,128]{3,2,1,0:T(2,128)S(1)} %bitcast.30), channel_id=1, replica_groups=mesh['grp'=2,'y'=4,'z'=4,'x'=4,'core'=2] {'y','z','x','core'}, dimensions={0} | all-to-all | bytes 786432 | tf_op jit(solution)/shard_map/all_to_all | solution.py:563
  101.4 21.6 %all_to_all.26 = f32[128,3,2,128]{3,2,1,0:T(2,128)S(1)} all-to-all(f32[128,3,2,128]{3,2,1,0:T(2,128)S(1)} %bitcast.29), channel_id=1, replica_groups=mesh['grp'=2,'y'=4,'z'=4,'x'=4,'core'=2] {'y','z','x','core'}, dimensions={0} | all-to-all | bytes 786432 | tf_op jit(solution)/shard_map/all_to_all | solution.py:576
  123.0 1.1 collective-permute-start.4
  124.1 1.3 collective-permute-done.4.refs_5_
  126.1 18.4 %all_to_all.27.refs_0_ = f32[32,48,128]{2,1,0:T(8,128)S(1)} all-to-all(f32[32,48,128]{2,1,0:T(8,128)} %get-tuple-element.51), channel_id=1, replica_groups=mesh['grp'=2,'y'=4,'z'=4,'x'=4,'core'=2] {'y','x','core'}, dimensions={0} | all-to-all | bytes 1572864 | tf_op jit(solution)/shard_map/all_to_all | solution.py:603
  145.1 1.3 collective-permute-start.5
  146.4 1.3 collective-permute-start.6
  147.7 1.3 collective-permute-start.7
  149.0 1.3 collective-permute-start.8
  150.3 3.3 %collective-permute-done.5.refs_4_ = f32[48,128]{1,0:T(8,128)S(1)} collective-permute-done((f32[48,128]{1,0:T(8,128)S(1)}, f32[48,128]{1,0:T(8,128)S(1)}, u32[]{:S(2)}, u32[]{:S(2)}) %collective-permute-start.5) | collective-permute-done | bytes 24608 | tf_op jit(solution)/shard_map/ppermute | solution.py:610
  153.6 1.1 collective-permute-done.7.refs_6_
  154.7 1.9 %collective-permute-done.8.refs_7_ = f32[48,128]{1,0:T(8,128)S(1)} collective-permute-done((f32[48,128]{1,0:T(8,128)S(1)}, f32[48,128]{1,0:T(8,128)S(1)}, u32[]{:S(2)}, u32[]{:S(2)}) %collective-permute-start.8) | collective-permute-done | bytes 24608 | tf_op jit(solution)/shard_map/ppermute | solution.py:610
  156.6 1.5 close_kernel.1
  (40 shorter events, 2.4 us)
Async XLA Ops:
  1.0 23.3 %collective-permute-start = (f32[3,256,128]{2,1,0:T(8,128)S(1)}, f32[3,256,128]{2,1,0:T(8,128)S(1)}, u32[]{:S(2)}, u32[]{:S(2)}) collective-permute-start(f32[3,256,128]{2,1,0:T(8,128)S(1)} %bitcast.37), channel_id=1, source_target_pairs={{0,128},{1,129},{2,130},{3,131},{4,132},{5,133},{6,134},{7,135},{8... | collective-permute-start | bytes 1179656 | tf_op jit(solution)/shard_map/ppermute | solution.py:488
  13.8 21.6 %all-to-all-start.1 = ((f32[128,1,128]{2,1,0:T(1,128)}), f32[128,1,128]{2,1,0:T(1,128)S(1)}, u32[]{:S(2)}, u32[]{:S(2)}) async-start(f32[128,1,128]{2,1,0:T(1,128)} %bitcast.39), calls=%async_computation.1 | async-start | bytes 131072 | tf_op jit(solution)/shard_map/all_to_all | solution.py:505
  35.3 9.9 %copy-start.16 = (f32[128,1,128]{2,1,0:T(1,128)}, f32[128,1,128]{2,1,0:T(1,128)S(1)}, u32[]{:S(2)}) copy-start(f32[128,1,128]{2,1,0:T(1,128)S(1)} %all-to-all-done.1) | copy-start | bytes 196612
  35.3 35.4 %all-to-all-start = ((f32[128,3,4,128]{3,2,1,0:T(4,128)}), f32[128,3,4,128]{3,2,1,0:T(4,128)S(1)}, u32[]{:S(2)}, u32[]{:S(2)}) async-start(f32[128,3,4,128]{3,2,1,0:T(4,128)} %bitcast.10), calls=%async_computation | async-start | bytes 1572864 | tf_op jit(solution)/shard_map/all_to_all | solution.py:547
  45.2 25.5 %copy-start = (f32[256,128]{1,0:T(8,128)S(1)}, f32[256,128]{1,0:T(8,128)}, u32[]{:S(2)}) copy-start(f32[256,128]{1,0:T(8,128)} %constant.47.clone.refs_5_.refs_3_.refs_6_.refs_10_) | copy-start | bytes 393220
  45.2 25.5 %copy-start.3 = (bf16[256,256]{1,0:T(8,128)(2,1)S(1)}, bf16[256,256]{1,0:T(8,128)(2,1)}, u32[]{:S(2)}) copy-start(bf16[256,256]{1,0:T(8,128)(2,1)} %constant.46.clone.refs_4_.refs_9_) | copy-start | bytes 393220
  45.2 25.5 %copy-start.4 = (bf16[256,256]{1,0:T(8,128)(2,1)S(1)}, bf16[256,256]{1,0:T(8,128)(2,1)}, u32[]{:S(2)}) copy-start(bf16[256,256]{1,0:T(8,128)(2,1)} %constant.45.clone.refs_3_.refs_8_) | copy-start | bytes 393220
  45.2 11.2 %collective-permute-start.1 = (f32[896,128]{1,0:T(8,128)}, f32[896,128]{1,0:T(8,128)S(1)}, u32[]{:S(2)}, u32[]{:S(2)}) collective-permute-start(f32[896,128]{1,0:T(8,128)} %get-tuple-element.33), channel_id=1, source_target_pairs={{0,1},{1,2},{2,3},{3,4},{4,5},{5,6},{6,7},{7,8},{8,9},{9,10},{10,1... | collective-permute-start | bytes 1376264 | tf_op jit(solution)/shard_map/ppermute | solution.py:533
  48.9 11.7 %collective-permute-start.2 = (f32[896,128]{1,0:T(8,128)}, f32[896,128]{1,0:T(8,128)S(1)}, u32[]{:S(2)}, u32[]{:S(2)}) collective-permute-start(f32[896,128]{1,0:T(8,128)} %get-tuple-element.34), channel_id=1, source_target_pairs={{1,0},{2,1},{3,2},{4,3},{5,4},{6,5},{7,6},{8,7},{9,8},{10,9},{11,1... | collective-permute-start | bytes 1376264 | tf_op jit(solution)/shard_map/ppermute | solution.py:534
  56.4 4.2 %copy-start.14 = (f32[896,128]{1,0:T(8,128)}, f32[896,128]{1,0:T(8,128)S(1)}, u32[]{:S(2)}) copy-start(f32[896,128]{1,0:T(8,128)S(1)} %collective-permute-done.1.refs_2_) | copy-start | bytes 1376260
  60.6 0.8 copy-start.15
  71.3 29.5 %copy-start.5 = (bf16[512,128]{1,0:T(8,128)(2,1)S(1)}, bf16[512,128]{1,0:T(8,128)(2,1)}, u32[]{:S(2)}) copy-start(bf16[512,128]{1,0:T(8,128)(2,1)} %constant.44.clone.refs_4_.refs_2_) | copy-start | bytes 393220
  71.3 29.5 %copy-start.6 = (bf16[512,128]{1,0:T(8,128)(2,1)S(1)}, bf16[512,128]{1,0:T(8,128)(2,1)}, u32[]{:S(2)}) copy-start(bf16[512,128]{1,0:T(8,128)(2,1)} %constant.43.clone.refs_3_.refs_1_) | copy-start | bytes 393220
  71.3 29.5 %copy-start.7 = (f32[512,1]{1,0:T(8,128)S(1)}, f32[512,1]{1,0:T(8,128)}, u32[]{:S(2)}) copy-start(f32[512,1]{1,0:T(8,128)} %constant.48.clone.refs_5_) | copy-start | bytes 6148
  71.3 29.5 %copy-start.10 = (bf16[128,512]{1,0:T(8,128)(2,1)S(1)}, bf16[128,512]{1,0:T(8,128)(2,1)}, u32[]{:S(2)}) copy-start(bf16[128,512]{1,0:T(8,128)(2,1)} %get-tuple-element.45.refs_3_) | copy-start | bytes 393220
  71.3 29.5 %copy-start.11 = (bf16[128,512]{1,0:T(8,128)(2,1)S(1)}, bf16[128,512]{1,0:T(8,128)(2,1)}, u32[]{:S(2)}) copy-start(bf16[128,512]{1,0:T(8,128)(2,1)} %get-tuple-element.46.refs_4_) | copy-start | bytes 393220
  71.4 6.7 %collective-permute-start.3 = (f32[768,128]{1,0:T(8,128)S(1)}, f32[768,128]{1,0:T(8,128)S(1)}, u32[]{:S(2)}, u32[]{:S(2)}) collective-permute-start(f32[768,128]{1,0:T(8,128)S(1)} %get-tuple-element.43.refs_0_.refs_2_), channel_id=1, source_target_pairs={{0,1},{1,0},{2,3},{3,2},{4,5},{5,4},{6,7},{7,6},{8,9},{9,8},{10,11... | collective-permute-start | bytes 1179656 | tf_op jit(solution)/shard_map/ppermute | solution.py:561
  78.8 46.7 %copy-start.1 = (bf16[512,1024]{1,0:T(8,128)(2,1)S(1)}, bf16[512,1024]{1,0:T(8,128)(2,1)}, u32[]{:S(2)}) copy-start(bf16[512,1024]{1,0:T(8,128)(2,1)} %get-tuple-element.47.refs_6_) | copy-start | bytes 3145732
  78.8 46.7 %copy-start.2 = (bf16[256,256]{1,0:T(8,128)(2,1)S(1)}, bf16[256,256]{1,0:T(8,128)(2,1)}, u32[]{:S(2)}) copy-start(bf16[256,256]{1,0:T(8,128)(2,1)} %constant.42.clone.refs_2_.refs_7_) | copy-start | bytes 393220
  123.0 2.5 %collective-permute-start.4 = (f32[768,128]{1,0:T(8,128)S(1)}, f32[768,128]{1,0:T(8,128)S(1)}, u32[]{:S(2)}, u32[]{:S(2)}) collective-permute-start(f32[768,128]{1,0:T(8,128)S(1)} %bitcast.26), channel_id=1, source_target_pairs={{0,1},{1,0},{2,3},{3,2},{4,5},{5,4},{6,7},{7,6},{8,9},{9,8},{10,11... | collective-permute-start | bytes 1179656 | tf_op jit(solution)/shard_map/ppermute | solution.py:578
  126.1 18.5 %copy-start.12 = (bf16[64,512]{1,0:T(8,128)(2,1)S(1)}, bf16[64,512]{1,0:T(8,128)(2,1)}, u32[]{:S(2)}) copy-start(bf16[64,512]{1,0:T(8,128)(2,1)} %get-tuple-element.52.refs_1_) | copy-start | bytes 196612
  126.1 30.5 %copy-start.8 = (f32[128,128]{1,0:T(8,128)S(1)}, f32[128,128]{1,0:T(8,128)}, u32[]{:S(2)}) copy-start(f32[128,128]{1,0:T(8,128)} %refs_3_.4) | copy-start | bytes 196612
  126.1 30.5 %copy-start.9 = (f32[3,16,8,128]{3,2,1,0:T(8,128)S(1)}, f32[3,16,8,128]{3,2,1,0:T(8,128)}, u32[]{:S(2)}) copy-start(f32[3,16,8,128]{3,2,1,0:T(8,128)} %get-tuple-element.49.refs_1_) | copy-start | bytes 589828
  126.1 30.5 %copy-start.13 = (f32[3,16,128]{2,1,0:T(8,128)S(1)}, f32[3,16,128]{2,1,0:T(8,128)}, u32[]{:S(2)}) copy-start(f32[3,16,128]{2,1,0:T(8,128)} %get-tuple-element.50.refs_2_) | copy-start | bytes 73732
  145.1 8.5 %collective-permute-start.5 = (f32[48,128]{1,0:T(8,128)S(1)}, f32[48,128]{1,0:T(8,128)S(1)}, u32[]{:S(2)}, u32[]{:S(2)}) collective-permute-start(f32[48,128]{1,0:T(8,128)S(1)} %get-tuple-element.53), channel_id=1, source_target_pairs={{128,0},{129,1},{130,2},{131,3},{132,4},{133,5},{134,6},{135,7},{1... | collective-permute-start | bytes 73736 | tf_op jit(solution)/shard_map/ppermute | solution.py:610
  146.4 7.2 %collective-permute-start.6 = (f32[48,128]{1,0:T(8,128)S(1)}, f32[48,128]{1,0:T(8,128)S(1)}, u32[]{:S(2)}, u32[]{:S(2)}) collective-permute-start(f32[48,128]{1,0:T(8,128)S(1)} %get-tuple-element.54), channel_id=1, source_target_pairs={{128,8},{129,9},{130,10},{131,11},{132,12},{133,13},{134,14},{135,... | collective-permute-start | bytes 73736 | tf_op jit(solution)/shard_map/ppermute | solution.py:610
  147.7 7.0 %collective-permute-start.7 = (f32[48,128]{1,0:T(8,128)S(1)}, f32[48,128]{1,0:T(8,128)S(1)}, u32[]{:S(2)}, u32[]{:S(2)}) collective-permute-start(f32[48,128]{1,0:T(8,128)S(1)} %get-tuple-element.55), channel_id=1, source_target_pairs={{128,16},{129,17},{130,18},{131,19},{132,20},{133,21},{134,22},{13... | collective-permute-start | bytes 73736 | tf_op jit(solution)/shard_map/ppermute | solution.py:610
  149.0 7.6 %collective-permute-start.8 = (f32[48,128]{1,0:T(8,128)S(1)}, f32[48,128]{1,0:T(8,128)S(1)}, u32[]{:S(2)}, u32[]{:S(2)}) collective-permute-start(f32[48,128]{1,0:T(8,128)S(1)} %get-tuple-element.56), channel_id=1, source_target_pairs={{128,24},{129,25},{130,26},{131,27},{132,28},{133,29},{134,30},{13... | collective-permute-start | bytes 73736 | tf_op jit(solution)/shard_map/ppermute | solution.py:610

commit v3 on v2

--- a/solution.py
+++ b/solution.py
@@ -19,6 +19,8 @@
 TARGETS = CY * CX * CC
 GROUP = CZ * CAP
 SLOTS = BRICKS * CAP
+CHUNK = 3 * CAP + 1
+BACK = 3 * GROUP + 1
 DEV = ("y", "z", "x", "core")
 ALL = ("grp",) + DEV
 
@@ -119,20 +121,13 @@
     return owner >> 5, z, x, core, lane
 
 
-def route_kernel(flags, sd, sr, rd, rb, remesh, sz, place, codes, merged):
+def route_kernel(flags, sd, sr, remesh, sz, place, codes, merged):
     bricks = iota((BRICKS, SB), 0)
     matches = jnp.where(bricks == sd[...], 1.0, 0.0)
     rank = ranks(matches)
-    slot = rank * BRICKS + sd[...]
-    place[...] = onehot(iota((SLOTS, SB), 0) == slot)
+    place[...] = onehot(iota((SLOTS, SB), 0) == rank * BRICKS + sd[...])
     tagged = jnp.where(bricks == rank, (sr[...] + 1).astype(f32), 0.0)
-    sent = exact(matches, tagged, NT)
-    zme = flags[3]
-    y, z, x, core, lane = owners(rd[...])
-    via = ((y * CZ + zme) * CX + x) * CC + core
-    code = ((z - zme) & (CZ - 1)) * NJ + rb[...] + 1
-    tagged = jnp.where(bricks == lane + CAP, code.astype(f32), 0.0)
-    codes[...] = sent + exact(jnp.where(bricks == via, 1.0, 0.0), tagged, NT)
+    codes[...] = exact(matches, tagged, NT)
     high, low = split(exact(remesh[...], sz[...]))
     merged[...] = jnp.concatenate(
         [
@@ -143,87 +138,59 @@
     )
 
 
-def decode_kernel(flags, codes, rd, rr, landing, cells, gather):
+def ready_kernel(
+    flags, state, speed, sz, kh, kl, rd, rr, rb, out, th, tl, gather, codes, last, lead
+):
+    @pl.when(flags[0] == 0)
+    def _():
+        for c in range(3):
+            last[c * 256 : (c + 1) * 256, :] = state[c, 768:, :]
+            lead[c * 256 : (c + 1) * 256, :] = state[c, :256, :]
+        last[768:, :] = speed[896:, :]
+        lead[768:, :] = speed[:128, :]
+
     @pl.when(flags[0] != 0)
     def _():
-        zme = flags[3]
-        turned = codes[...].T
-        landing[...] = jnp.concatenate(
-            [turned[i : i + 1, :] for i in range(CAP)], axis=1
-        ).astype(i32)
-        target = iota((TARGETS, BRICKS), 0)
-        source = ((target >> 3) * CZ + zme) * (CX * CC) + (target & (CX * CC - 1))
-        chosen = exact(jnp.where(iota((TARGETS, BRICKS), 1) == source, 1.0, 0.0), codes[...])
-        wide = jnp.where(
-            iota((BRICKS, SLOTS), 0) == (iota((BRICKS, SLOTS), 1) & (GROUP - 1)) + CAP, 1.0, 0.0
-        )
-        chosen = exact(chosen, wide)
-        own = iota((TARGETS, SLOTS), 0) == (iota((TARGETS, SLOTS), 1) >> 4)
-        code = jnp.sum(jnp.where(own, chosen, 0.0), axis=0, keepdims=True).astype(i32)
-        cells[...] = onehot(iota((CZ * NJ, SLOTS), 0) == code - 1)
-        y, _, x, core, lane = owners(rd[...])
-        slot = ((y * CX + x) * CC + core) * GROUP + lane
+        for c in range(3):
+            out[c] = times_paired(state[c], sz[...])
+        th[...] = kh[...].T
+        tl[...] = kl[...].T
+        y, z, x, core, lane = owners(rd[...])
+        target = (y * CX + x) * CC + core
         gather[...] = lax.dot_general(
-            onehot(iota((SLOTS, SB), 0) == slot),
+            onehot(iota((SLOTS, SB), 0) == lane * TARGETS + target),
             onehot(iota((RPB, SB), 0) == rr[...]),
             NT,
             preferred_element_type=f32,
         ).astype(bf16)
-
-
-def near_kernel(flags, state, courant, up, down, out, edge, layer):
-    @pl.when(flags[0] == 0)
-    def _():
-        cr = jnp.concatenate([up[768:896, :], courant[...], down[768:896, :]], axis=0)
-
-        def step(field, speed):
-            rows = speed.shape[0]
-            centre = field[128 : 128 + rows]
-            transport = (
-                8.0 * (field[192 : 192 + rows] - field[64 : 64 + rows])
-                - (field[256 : 256 + rows] - field[:rows])
-            ) / 12.0
-            place = iota((rows, NK), 0) & (NI - 1)
-            above = jnp.where(place == NI - 1, 0.0, pltpu.roll(centre, rows - 1, 0))
-            below = jnp.where(place == 0, 0.0, pltpu.roll(centre, 1, 0))
-            return centre - speed * transport + viscosity * (above - 2.0 * centre + below)
-
-        for c in range(3):
-            field = jnp.concatenate(
-                [up[c * 256 : (c + 1) * 256, :], state[c], down[c * 256 : (c + 1) * 256, :]], axis=0
-            )
-            field = step(field, cr)
-            field = step(field, courant[...])
-            out[c] = field
-            edge[c] = field.reshape(NJ, NI, NK)[:, NI - 8 :, :]
-            layer[c] = state[c, pl.ds(NI - 1, NJ, stride=NI), :]
-
-
-def ready_kernel(flags, state, speed, sz, kh, kl, out, th, tl, last, lead):
-    @pl.when(flags[0] == 0)
-    def _():
-        for c in range(3):
-            last[c * 256 : (c + 1) * 256, :] = state[c, 768:, :]
-            lead[c * 256 : (c + 1) * 256, :] = state[c, :256, :]
-        last[768:, :] = speed[896:, :]
-        lead[768:, :] = speed[:128, :]
-
+        code = ((z - flags[3]) & (CZ - 1)) * NJ + rb[...] + 1
+        tagged = jnp.where(iota((NZ, SB), 0) == lane, code.astype(f32), 0.0)
+        sent = onehot(iota((TARGETS, SB), 0) == target)
+        codes[...] = lax.dot_general(sent, tagged.astype(bf16), NT, preferred_element_type=f32)
+
+
+def near_step(field, speed):
+    rows = speed.shape[0]
+    centre = field[128 : 128 + rows]
+    transport = (
+        8.0 * (field[192 : 192 + rows] - field[64 : 64 + rows])
+        - (field[256 : 256 + rows] - field[:rows])
+    ) / 12.0
+    place = iota((rows, NK), 0) & (NI - 1)
+    above = jnp.where(place == NI - 1, 0.0, pltpu.roll(centre, rows - 1, 0))
+    below = jnp.where(place == 0, 0.0, pltpu.roll(centre, 1, 0))
+    return centre - speed * transport + viscosity * (above - 2.0 * centre + below)
+
+
+def bucket_kernel(flags, blocks, codes, place, merged, out):
     @pl.when(flags[0] != 0)
     def _():
-        for c in range(3):
-            out[c] = times_paired(state[c], sz[...])
-        th[...] = kh[...].T
-        tl[...] = kl[...].T
-
-
-def bucket_kernel(flags, blocks, place, merged, out):
-    @pl.when(flags[0] != 0)
-    def _():
+        out[pl.ds(3 * CAP, BRICKS, stride=CHUNK), :] = codes[...]
         for c in range(3):
             moved = times_paired(blocks[c], merged[...])
             slots = pick(place[...], moved)
             for rank in range(CAP):
-                out[pl.ds(c * CAP + rank, BRICKS, stride=3 * CAP), :] = slots[
+                out[pl.ds(c * CAP + rank, BRICKS, stride=CHUNK), :] = slots[
                     rank * BRICKS : (rank + 1) * BRICKS
                 ]
 
@@ -236,16 +203,18 @@
     return g11, g12, g13
 
 
-def forward_kernel(flags, received, landing, work, syh, syl, mu, planes, outgoing, kept):
+def forward_kernel(flags, received, work, syh, syl, mu, planes, outgoing, kept):
     @pl.when(flags[0] != 0)
     def _():
         beta = mu[...] + 2.0
         g11, g12, g13 = weights(beta)
         first = flags[1] == 0
-        spread = onehot(iota((RPB, SLOTS), 0) == landing[...] - 1)
+        codes = received[pl.ds(3 * CAP, BRICKS, stride=CHUNK), :].T
+        landing = jnp.concatenate([codes[r : r + 1, :] for r in range(CAP)], axis=1).astype(i32)
+        spread = onehot(iota((RPB, SLOTS), 0) == landing - 1)
         for c in range(3):
             rows = jnp.concatenate(
-                [received[pl.ds(c * CAP + r, BRICKS, stride=3 * CAP), :] for r in range(CAP)], axis=0
+                [received[pl.ds(c * CAP + r, BRICKS, stride=CHUNK), :] for r in range(CAP)], axis=0
             )
             field = (pick(spread, rows) + work[c]) * (4.0 / ((NY + 1) * (NZ + 1)))
             field = jnp.concatenate([field[p * NY : (p + 1) * NY] for p in range(4)], axis=1)
@@ -288,24 +257,59 @@
 
 def inverse_kernel(
     flags,
-    advanced,
     planes,
     outgoing,
     incoming,
     own,
     other,
     gather,
+    codes,
     sz,
     syh,
     syl,
     mu,
+    state_home,
+    speed_home,
+    up_home,
+    down_home,
+    send,
     out,
-    send,
+    edge_home,
+    layer_home,
     held,
-    rows_held,
-    out_sems,
-    send_sems,
+    edge,
+    layer,
+    state,
+    speed,
+    up,
+    down,
+    sems,
 ):
+    @pl.when(flags[0] == 0)
+    def _():
+        pairs = [(state_home, state), (speed_home, speed), (up_home, up), (down_home, down)]
+        copies = [pltpu.make_async_copy(a, b, sems.at[i]) for i, (a, b) in enumerate(pairs)]
+        for copy in copies:
+            copy.start()
+        for copy in copies:
+            copy.wait()
+        wide = jnp.concatenate([up[768:896, :], speed[...], down[768:896, :]], axis=0)
+        copies = []
+        for c in range(3):
+            block = slice(c * 256, (c + 1) * 256)
+            field = jnp.concatenate([up[block, :], state[c], down[block, :]], axis=0)
+            field = near_step(near_step(field, wide), speed[...])
+            held[c] = field
+            copies.append(pltpu.make_async_copy(held.at[c], out.at[c], sems.at[c]))
+            copies[-1].start()
+            edge[c] = field.reshape(NJ, NI, NK)[:, NI - 8 :, :]
+            layer[c] = state[c, pl.ds(NI - 1, NJ, stride=NI), :]
+        for a, b, i in ((edge, edge_home, 3), (layer, layer_home, 4)):
+            copies.append(pltpu.make_async_copy(a, b, sems.at[i]))
+            copies[-1].start()
+        for copy in copies:
+            copy.wait()
+
     @pl.when(flags[0] != 0)
     def _():
         beta = mu[...] + 2.0
@@ -364,24 +368,36 @@
         copies = []
         for c in range(3):
             held[c] = velocity[c]
-            copies.append(pltpu.make_async_copy(held.at[c], out.at[c], out_sems.at[c]))
+            copies.append(pltpu.make_async_copy(held.at[c], out.at[c], sems.at[c]))
             copies[-1].start()
+        send[pl.ds(3 * GROUP, TARGETS, stride=BACK), :] = codes[...]
         for c in range(3):
             rows_out = pick(gather[...], velocity[c])
-            rows_held[c] = rows_out.reshape(TARGETS, GROUP, NZ)
-            target = send.at[:, pl.ds(c * GROUP, GROUP), :]
-            copies.append(pltpu.make_async_copy(rows_held.at[c], target, send_sems.at[c]))
-            copies[-1].start()
+            for lane in range(GROUP):
+                send[pl.ds(c * GROUP + lane, TARGETS, stride=BACK), :] = rows_out[
+                    lane * TARGETS : (lane + 1) * TARGETS
+                ]
         for copy in copies:
             copy.wait()
 
 
-def cell_kernel(flags, received, cells, *outs):
+def cell_kernel(flags, received, *outs):
     @pl.when(flags[0] != 0)
     def _():
-        for c in range(3):
-            rows = received[:, c * GROUP : (c + 1) * GROUP, :].reshape(SLOTS, NZ)
-            sums = pick(cells[...], rows)
+        codes = received[pl.ds(3 * GROUP, TARGETS, stride=BACK), :].astype(bf16)
+        codes = mm(codes, onehot(iota((NZ, SLOTS), 0) == (iota((NZ, SLOTS), 1) >> 5)))
+        mine = iota((TARGETS, SLOTS), 0) == (iota((TARGETS, SLOTS), 1) & (TARGETS - 1))
+        code = jnp.sum(jnp.where(mine, codes, 0.0), axis=0, keepdims=True).astype(i32)
+        cells = onehot(iota((CZ * NJ, SLOTS), 0) == code - 1)
+        for c in range(3):
+            rows = jnp.concatenate(
+                [
+                    received[pl.ds(c * GROUP + lane, TARGETS, stride=BACK), :]
+                    for lane in range(GROUP)
+                ],
+                axis=0,
+            )
+            sums = pick(cells, rows)
             for k in range(CZ):
                 outs[k][c * NJ : (c + 1) * NJ, :] = sums[k * NJ : (k + 1) * NJ]
 
@@ -402,11 +418,14 @@
         copy.wait()
 
 
-def call(kernel, outs, flags, *args, fetch=False, raw=False, alias=False, scratch=()):
+def call(kernel, outs, flags, *args, fetch=False, alias=False, far=0, scratch=()):
     args = [jnp.asarray(a) for a in args]
-    spaces = [pltpu.HBM if fetch or (alias and i == 0) else pltpu.VMEM for i in range(len(args))]
-    homes = [raw or len(o) > 2 for o in outs]
-    staged = [] if raw else [i for i, home in enumerate(homes) if home]
+    spaces = [
+        pltpu.HBM if fetch or (alias and i == 0) or i >= len(args) - far else pltpu.VMEM
+        for i in range(len(args))
+    ]
+    homes = [len(o) > 2 for o in outs]
+    staged = [i for i, o in enumerate(outs) if o[2:] == ("home",)]
     loads = [pltpu.VMEM(a.shape, a.dtype) for a in args] if fetch else []
     stores = [pltpu.VMEM(*outs[i][:2]) for i in staged]
     sems = [pltpu.SemaphoreType.DMA((len(loads) + len(stores),))] if loads or stores else []
@@ -492,32 +511,26 @@
     )
     place, codes, merged = call(
         route_kernel,
-        [((SLOTS, SB), bf16), ((BRICKS, NZ), f32, "home"), ((2 * NK, 2 * NZ), bf16)],
+        [((SLOTS, SB), bf16), ((BRICKS, NZ), f32), ((2 * NK, 2 * NZ), bf16)],
         flags,
         sd,
         sr,
-        rd,
-        rb,
         remesh,
         sz.astype(np.float32),
         fetch=True,
     )
-    codes = lax.all_to_all(codes.reshape(BRICKS, 1, NZ), DEV, 0, 0, tiled=True)
-    landing, cells, gather = call(
-        decode_kernel,
-        [((1, SLOTS), i32), ((CZ * NJ, SLOTS), bf16, "home"), ((SLOTS, RPB), bf16, "home")],
-        flags,
-        codes.reshape(BRICKS, NZ),
-        rd,
-        rr,
-        fetch=True,
-    )
-    turned, th, tl, last, lead = call(
+    (bundle,) = call(
+        bucket_kernel, [((BRICKS * CHUNK, NZ), f32)], flags, blocks, codes, place, merged
+    )
+    bundle = lax.all_to_all(bundle.reshape(BRICKS, CHUNK, 1, NZ), DEV, 0, 0, tiled=True)
+    turned, th, tl, gather, codes, last, lead = call(
         ready_kernel,
         [
             ((3, RPB, NZ), f32),
             ((BRICKS, NX), bf16, "home"),
             ((BRICKS, NX), bf16, "home"),
+            ((SLOTS, RPB), bf16, "home"),
+            ((TARGETS, NZ), f32, "home"),
             ((896, NK), f32, "home"),
             ((896, NK), f32, "home"),
         ],
@@ -527,31 +540,20 @@
         szp,
         kh,
         kl,
+        rd,
+        rr,
+        rb,
         fetch=True,
     )
     ahead = [(d, (d + 1) % BRICKS) for d in range(BRICKS)]
     up = lax.ppermute(last, ALL, ahead)
     down = lax.ppermute(lead, ALL, [(b, a) for a, b in ahead])
-    advanced, edge, layer = call(
-        near_kernel,
-        [((3, RPB, NK), f32, "home"), ((3, NJ, 8, NK), f32, "home"), ((3, NJ, NK), f32, "home")],
-        flags,
-        field,
-        speed,
-        up,
-        down,
-        fetch=True,
-    )
-
-    (bundle,) = call(bucket_kernel, [((3 * SLOTS, NZ), f32)], flags, blocks, place, merged)
-    bundle = lax.all_to_all(bundle.reshape(BRICKS, 3, CAP, NZ), DEV, 0, 0, tiled=True)
-    bundle, advanced, gather = lax.optimization_barrier((bundle, advanced, gather))
+    bundle, up, down = lax.optimization_barrier((bundle, up, down))
     planes, outgoing, kept = call(
         forward_kernel,
         [((3, 4, NY, NZ), f32), ((3 * NY, NZ), f32), ((3 * NY, NZ), f32)],
         flags,
-        bundle.reshape(3 * SLOTS, NZ),
-        landing,
+        bundle.reshape(BRICKS * CHUNK, NZ),
         turned,
         syh,
         syl,
@@ -576,32 +578,49 @@
     own = lax.all_to_all(solved.reshape(BRICKS, 3, 2, NZ), DEV, 0, 0, tiled=True)
     own = own.reshape(3 * NY, NZ)
     other = lax.ppermute(own, "core", swap)
-    result, send = call(
+    halo = pltpu.VMEM((896, NK), f32)
+    send, result, edge, layer = call(
         inverse_kernel,
-        [((3, RPB, NZ), f32), ((TARGETS, 3 * GROUP, NZ), f32)],
+        [
+            ((TARGETS * BACK, NZ), f32),
+            ((3, RPB, NZ), f32, "raw"),
+            ((3, NJ, 8, NK), f32, "raw"),
+            ((3, NJ, NK), f32, "raw"),
+        ],
         flags,
-        advanced,
         planes,
         outgoing,
         incoming,
         own,
         other,
         gather,
+        codes,
         szp,
         syh,
         syl,
         mu,
-        raw=True,
-        alias=True,
+        field,
+        speed,
+        up,
+        down,
+        far=4,
         scratch=[
             pltpu.VMEM((3, RPB, NZ), f32),
-            pltpu.VMEM((3, TARGETS, GROUP, NZ), f32),
-            pltpu.SemaphoreType.DMA((3,)),
-            pltpu.SemaphoreType.DMA((3,)),
+            pltpu.VMEM((3, NJ, 8, NK), f32),
+            pltpu.VMEM((3, NJ, NK), f32),
+            pltpu.VMEM((3, RPB, NK), f32),
+            pltpu.VMEM((RPB, NK), f32),
+            halo,
+            halo,
+            pltpu.SemaphoreType.DMA((5,)),
         ],
     )
-    returned = lax.all_to_all(send, ("y", "x", "core"), 0, 0, tiled=True)
-    sums = call(cell_kernel, [((3 * NJ, NZ), f32)] * CZ, flags, returned, cells)
+    returned = lax.all_to_all(
+        send.reshape(TARGETS, BACK, 1, NZ), ("y", "x", "core"), 0, 0, tiled=True
+    )
+    sums = call(
+        cell_kernel, [((3 * NJ, NZ), f32)] * CZ, flags, returned.reshape(TARGETS * BACK, NZ)
+    )
     parts = []
     for k in range(CZ):
         pairs = [
@@ -610,14 +629,13 @@
         parts.append(lax.ppermute(sums[k], ALL, pairs))
     (result,) = call(
         close_kernel,
-        [((3, NJ, NI, NZ), f32)],
+        [((3, NJ, NI, NZ), f32, "raw")],
         flags,
         result.reshape(3, NJ, NI, NZ),
         edge,
         layer,
         remesh,
         *parts,
-        raw=True,
         alias=True,
         scratch=[pltpu.VMEM((3, NJ, 8, NZ), f32), pltpu.SemaphoreType.DMA],
     )

time: 159 us -> 156 us (0.981)
  waiting for transfers between devices: 29.6 us -> 35.7 us
  Pallas kernels: 20.2 us -> 16.2 us
  starting transfers between devices: 44 us -> 41.9 us
  blocking collectives: 62 us -> 60.4 us
    ppermute x1, waiting for transfers between devices: 0.01 us -> 5.54 us  [on_device(): blocks = lax.ppermute(blocks, ALL, across)]
    pallas_call x11 -> x9, Pallas kernels: 20.2 us -> 16.2 us  [call(): pl.pallas_call(body, out_shape=[(pltpu.HBM if home else pltpu.VMEM)(*o[:2...]
    ppermute x1, starting transfers between devices: 5.33 us -> 1.35 us  [on_device(): incoming = lax.ppermute(outgoing, 'core', swap)]
    ppermute x1, waiting for transfers between devices: 3.14 us -> 5.88 us  [on_device(): up = lax.ppermute(last, ALL, ahead)]
    all_to_all x2 -> x1, starting transfers between devices: 17.1 us -> 19.1 us  [on_device(): lax.all_to_all(bundle.reshape(BRICKS, CHUNK, 1, NZ), DEV, 0, 0, tiled=True)]
    all_to_all x2 -> x1, waiting for transfers between devices: 13.3 us -> 11.4 us  [on_device(): lax.all_to_all(bundle.reshape(BRICKS, CHUNK, 1, NZ), DEV, 0, 0, tiled=True)]
  transfers between devices with their start and end apart: 11 -> 10, of which waited for: 9 -> 9; matrix products, arithmetic and copies ran while one was open for 0% -> 0% of each run, Pallas kernels for 10% -> 4%
where the time goes in v3:
time: 156 us
  blocking collectives  60.4 us (39%)
  starting transfers between devices  41.9 us (27%)
  waiting for transfers between devices  35.7 us (23%)
  Pallas kernels  16.2 us (10%)
    all_to_all x1, blocking collectives, on_device(): lax.all_to_all(solved.reshape(BRICKS, 3, 2, NZ), DEV, 0, 0, tiled=True)  21.6 us
    all_to_all x1, blocking collectives, on_device(): lax.all_to_all(share.reshape(BRICKS, 3, 2, NZ), DEV, 0, 0, tiled=True)  20.7 us
    all_to_all x1, starting transfers between devices, on_device(): lax.all_to_all(bundle.reshape(BRICKS, CHUNK, 1, NZ), DEV, 0, 0, tiled=True)  19.1 us
    all_to_all x1, blocking collectives, on_device(): lax.all_to_all(send.reshape(TARGETS, BACK, 1, NZ), ('y', 'x', 'core'), 0,...  18.2 us
    pallas_call x9, Pallas kernels, call(): pl.pallas_call(body, out_shape=[(pltpu.HBM if home else pltpu.VMEM)(*o[:2...  16.2 us
    all_to_all x1, waiting for transfers between devices, on_device(): lax.all_to_all(bundle.reshape(BRICKS, CHUNK, 1, NZ), DEV, 0, 0, tiled=True)  11.4 us
    ppermute x1, starting transfers between devices, on_device(): blocks = lax.ppermute(blocks, ALL, across)  9.66 us
    ppermute x4, waiting for transfers between devices, on_device(): parts.append(lax.ppermute(sums[k], ALL, pairs))  6.4 us
  transfers between devices with their start and end apart: 10, of which 9 were waited for; matrix products, arithmetic and copies ran while one was open for 0% of the time, Pallas kernels for 4%

profile of v3, /device:TPU:1, one launch (start us, length us, event | category | flops | bytes accessed | tf_op | source)
XLA Modules:
  0.0 155.8 jit_solution(11179519523048118568)
XLA Ops:
  0.0 1.0 slice.4
  1.0 9.7 %collective-permute-start = (f32[3,256,128]{2,1,0:T(8,128)S(1)}, f32[3,256,128]{2,1,0:T(8,128)S(1)}, u32[]{:S(2)}, u32[]{:S(2)}) collective-permute-start(f32[3,256,128]{2,1,0:T(8,128)S(1)} %bitcast.37), channel_id=1, source_target_pairs={{0,128},{1,129},{2,130},{3,131},{4,132},{5,133},{6,134},{7,135},{8... | collective-permute-start | bytes 1179656 | tf_op jit(solution)/shard_map/ppermute | solution.py:507
  10.8 2.1 %route_kernel.1 = (bf16[512,256]{1,0:T(8,128)(2,1)S(1)}, f32[128,128]{1,0:T(8,128)S(1)}, bf16[256,256]{1,0:T(8,128)(2,1)S(1)}) custom-call(s32[4]{0:T(128)S(1)} %pad_add_fusion.flags, s32[1,256]{1,0:T(1,128)} %bitcast.38, s32[1,256]{1,0:T(1,128)} %bitcast.39, f32[128,128]{1,0:T(8,128)} %refs_3_.5, f32[128,128]{1,0:T(8,128)} %constant.41.clone.refs_3_), custom_call_target="tpu_custom_call" | custom-call | tf_op jit(solution)/shard_map/route_kernel/pallas_call | solution.py:460
  12.9 5.5 %collective-permute-done.refs_0_ = f32[3,256,128]{2,1,0:T(8,128)S(1)} collective-permute-done((f32[3,256,128]{2,1,0:T(8,128)S(1)}, f32[3,256,128]{2,1,0:T(8,128)S(1)}, u32[]{:S(2)}, u32[]{:S(2)}) %collective-permute-start) | collective-permute-done | bytes 393248 | tf_op jit(solution)/shard_map/ppermute | solution.py:507
  18.5 1.5 bucket_kernel.1
  19.9 19.1 %all-to-all-start = ((f32[128,13,1,128]{3,2,1,0:T(1,128)}), f32[128,13,1,128]{3,2,1,0:T(1,128)S(1)}, u32[]{:S(2)}, u32[]{:S(2)}) async-start(f32[128,13,1,128]{3,2,1,0:T(1,128)} %bitcast.8), calls=%async_computation | async-start | bytes 1703936 | tf_op jit(solution)/shard_map/all_to_all | solution.py:525
  39.1 3.7 %ready_kernel.1 = (f32[3,1024,128]{2,1,0:T(8,128)S(1)}, bf16[128,512]{1,0:T(8,128)(2,1)}, bf16[128,512]{1,0:T(8,128)(2,1)}, bf16[512,1024]{1,0:T(8,128)(2,1)}, f...) custom-call(s32[4]{0:T(128)S(1)} %pad_add_fusion.flags, f32[3,1024,128]{2,1,0:T(8,128)} %bitcast.32, ...), custom_call_target="tpu_custom_call" | custom-call | tf_op jit(solution)/shard_map/ready_kernel/pallas_call | solution.py:460
  42.8 3.5 %collective-permute-start.1 = (f32[896,128]{1,0:T(8,128)}, f32[896,128]{1,0:T(8,128)S(1)}, u32[]{:S(2)}, u32[]{:S(2)}) collective-permute-start(f32[896,128]{1,0:T(8,128)} %get-tuple-element.32), channel_id=1, source_target_pairs={{0,1},{1,2},{2,3},{3,4},{4,5},{5,6},{6,7},{7,8},{8,9},{9,10},{10,1... | collective-permute-start | bytes 1376264 | tf_op jit(solution)/shard_map/ppermute | solution.py:549
  46.4 1.9 %collective-permute-start.2 = (f32[896,128]{1,0:T(8,128)}, f32[896,128]{1,0:T(8,128)}, u32[]{:S(2)}, u32[]{:S(2)}) collective-permute-start(f32[896,128]{1,0:T(8,128)} %get-tuple-element.33), channel_id=1, source_target_pairs={{1,0},{2,1},{3,2},{4,3},{5,4},{6,5},{7,6},{8,7},{9,8},{10,9},{11,1... | collective-permute-start | bytes 1376264 | tf_op jit(solution)/shard_map/ppermute | solution.py:550
  48.3 5.9 %collective-permute-done.1.refs_13_ = f32[896,128]{1,0:T(8,128)S(1)} collective-permute-done((f32[896,128]{1,0:T(8,128)}, f32[896,128]{1,0:T(8,128)S(1)}, u32[]{:S(2)}, u32[]{:S(2)}) %collective-permute-start.1) | collective-permute-done | bytes 458784 | tf_op jit(solution)/shard_map/ppermute | solution.py:549
  54.2 3.8 %collective-permute-done.2.refs_14_ = f32[896,128]{1,0:T(8,128)} collective-permute-done((f32[896,128]{1,0:T(8,128)}, f32[896,128]{1,0:T(8,128)}, u32[]{:S(2)}, u32[]{:S(2)}) %collective-permute-start.2) | collective-permute-done | bytes 458784 | tf_op jit(solution)/shard_map/ppermute | solution.py:550
  58.0 11.4 %all-to-all-done = f32[128,13,1,128]{3,2,1,0:T(1,128)S(1)} async-done(((f32[128,13,1,128]{3,2,1,0:T(1,128)}), f32[128,13,1,128]{3,2,1,0:T(1,128)S(1)}, u32[]{:S(2)}, u32[]{:S(2)}) %all-to-all-start) | async-done | bytes 852000 | tf_op jit(solution)/shard_map/all_to_all | solution.py:525
  69.4 0.6 forward_kernel.1
  70.0 1.3 collective-permute-start.3
  71.4 1.3 collective-permute-done.3.refs_1_.refs_2_
  72.7 0.5 reduce_kernel.1
  73.3 20.7 %all_to_all.20 = f32[128,3,2,128]{3,2,1,0:T(2,128)S(1)} all-to-all(f32[128,3,2,128]{3,2,1,0:T(2,128)S(1)} %bitcast.29), channel_id=1, replica_groups=mesh['grp'=2,'y'=4,'z'=4,'x'=4,'core'=2] {'y','z','x','core'}, dimensions={0} | all-to-all | bytes 786432 | tf_op jit(solution)/shard_map/all_to_all | solution.py:565
  94.1 0.6 line_kernel.1
  94.6 21.6 %all_to_all.21 = f32[128,3,2,128]{3,2,1,0:T(2,128)S(1)} all-to-all(f32[128,3,2,128]{3,2,1,0:T(2,128)S(1)} %bitcast.28), channel_id=1, replica_groups=mesh['grp'=2,'y'=4,'z'=4,'x'=4,'core'=2] {'y','z','x','core'}, dimensions={0} | all-to-all | bytes 786432 | tf_op jit(solution)/shard_map/all_to_all | solution.py:578
  116.2 1.1 collective-permute-start.4
  117.3 1.3 collective-permute-done.4.refs_4_
  118.7 5.2 %inverse_kernel.1 = (f32[1568,128]{1,0:T(8,128)S(1)}, f32[3,1024,128]{2,1,0:T(8,128)}, f32[3,16,8,128]{3,2,1,0:T(8,128)}, f32[3,16,128]{2,1,0:T(8,128)}) custom-call(s32[4]{0:T(128)S(1)} %pad_add_fusion.flags, f32[3,4,256,128]{3,2,1,0:T(8,128)S(1)} %get-tuple-element.36.refs_0_, f32[768,128]{1,0:T(8,128)S(1)} %get-tuple-element.37.refs_0_.refs_1_, ...), custom_call_target="tpu_custom_call" | custom-call | tf_op jit(solution)/shard_map/inverse_kernel/pallas_call | solution.py:460
  123.9 18.2 %all_to_all.22 = f32[32,49,1,128]{3,2,1,0:T(1,128)S(1)} all-to-all(f32[32,49,1,128]{3,2,1,0:T(1,128)S(1)} %bitcast.30), channel_id=1, replica_groups=mesh['grp'=2,'y'=4,'z'=4,'x'=4,'core'=2] {'y','x','core'}, dimensions={0} | all-to-all | bytes 1605632 | tf_op jit(solution)/shard_map/all_to_all | solution.py:618
  142.0 0.5 cell_kernel.1
  142.6 1.3 collective-permute-start.5
  143.9 1.3 collective-permute-start.6
  145.2 1.3 collective-permute-start.7
  146.5 1.3 collective-permute-start.8
  147.8 3.3 %collective-permute-done.5.refs_4_ = f32[48,128]{1,0:T(8,128)S(1)} collective-permute-done((f32[48,128]{1,0:T(8,128)S(1)}, f32[48,128]{1,0:T(8,128)S(1)}, u32[]{:S(2)}, u32[]{:S(2)}) %collective-permute-start.5) | collective-permute-done | bytes 24608 | tf_op jit(solution)/shard_map/ppermute | solution.py:629
  151.1 1.1 collective-permute-done.7.refs_6_
  152.2 2.0 %collective-permute-done.8.refs_7_ = f32[48,128]{1,0:T(8,128)S(1)} collective-permute-done((f32[48,128]{1,0:T(8,128)S(1)}, f32[48,128]{1,0:T(8,128)S(1)}, u32[]{:S(2)}, u32[]{:S(2)}) %collective-permute-start.8) | collective-permute-done | bytes 24608 | tf_op jit(solution)/shard_map/ppermute | solution.py:629
  154.2 1.5 close_kernel.1
  (32 shorter events, 0.2 us)
Async XLA Ops:
  1.0 17.4 %collective-permute-start = (f32[3,256,128]{2,1,0:T(8,128)S(1)}, f32[3,256,128]{2,1,0:T(8,128)S(1)}, u32[]{:S(2)}, u32[]{:S(2)}) collective-permute-start(f32[3,256,128]{2,1,0:T(8,128)S(1)} %bitcast.37), channel_id=1, source_target_pairs={{0,128},{1,129},{2,130},{3,131},{4,132},{5,133},{6,134},{7,135},{8... | collective-permute-start | bytes 1179656 | tf_op jit(solution)/shard_map/ppermute | solution.py:507
  19.9 49.5 %all-to-all-start = ((f32[128,13,1,128]{3,2,1,0:T(1,128)}), f32[128,13,1,128]{3,2,1,0:T(1,128)S(1)}, u32[]{:S(2)}, u32[]{:S(2)}) async-start(f32[128,13,1,128]{3,2,1,0:T(1,128)} %bitcast.8), calls=%async_computation | async-start | bytes 1703936 | tf_op jit(solution)/shard_map/all_to_all | solution.py:525
  39.1 30.3 %copy-start = (f32[256,128]{1,0:T(8,128)S(1)}, f32[256,128]{1,0:T(8,128)}, u32[]{:S(2)}) copy-start(f32[256,128]{1,0:T(8,128)} %constant.47.clone.refs_4_.refs_3_.refs_6_.refs_10_) | copy-start | bytes 393220
  39.1 30.3 %copy-start.3 = (bf16[256,256]{1,0:T(8,128)(2,1)S(1)}, bf16[256,256]{1,0:T(8,128)(2,1)}, u32[]{:S(2)}) copy-start(bf16[256,256]{1,0:T(8,128)(2,1)} %constant.46.clone.refs_3_.refs_9_) | copy-start | bytes 393220
  39.1 30.3 %copy-start.4 = (bf16[256,256]{1,0:T(8,128)(2,1)S(1)}, bf16[256,256]{1,0:T(8,128)(2,1)}, u32[]{:S(2)}) copy-start(bf16[256,256]{1,0:T(8,128)(2,1)} %constant.45.clone.refs_2_.refs_8_) | copy-start | bytes 393220
  42.8 11.4 %collective-permute-start.1 = (f32[896,128]{1,0:T(8,128)}, f32[896,128]{1,0:T(8,128)S(1)}, u32[]{:S(2)}, u32[]{:S(2)}) collective-permute-start(f32[896,128]{1,0:T(8,128)} %get-tuple-element.32), channel_id=1, source_target_pairs={{0,1},{1,2},{2,3},{3,4},{4,5},{5,6},{6,7},{7,8},{8,9},{9,10},{10,1... | collective-permute-start | bytes 1376264 | tf_op jit(solution)/shard_map/ppermute | solution.py:549
  46.4 11.6 %collective-permute-start.2 = (f32[896,128]{1,0:T(8,128)}, f32[896,128]{1,0:T(8,128)}, u32[]{:S(2)}, u32[]{:S(2)}) collective-permute-start(f32[896,128]{1,0:T(8,128)} %get-tuple-element.33), channel_id=1, source_target_pairs={{1,0},{2,1},{3,2},{4,3},{5,4},{6,5},{7,6},{8,7},{9,8},{10,9},{11,1... | collective-permute-start | bytes 1376264 | tf_op jit(solution)/shard_map/ppermute | solution.py:550
  54.2 19.1 %copy-start.14 = (f32[896,128]{1,0:T(8,128)}, f32[896,128]{1,0:T(8,128)S(1)}, u32[]{:S(2)}) copy-start(f32[896,128]{1,0:T(8,128)S(1)} %collective-permute-done.1.refs_13_) | copy-start | bytes 1376260
  70.0 24.1 %copy-start.5 = (bf16[512,128]{1,0:T(8,128)(2,1)S(1)}, bf16[512,128]{1,0:T(8,128)(2,1)}, u32[]{:S(2)}) copy-start(bf16[512,128]{1,0:T(8,128)(2,1)} %constant.44.clone.refs_4_.refs_2_) | copy-start | bytes 393220
  70.0 24.1 %copy-start.6 = (bf16[512,128]{1,0:T(8,128)(2,1)S(1)}, bf16[512,128]{1,0:T(8,128)(2,1)}, u32[]{:S(2)}) copy-start(bf16[512,128]{1,0:T(8,128)(2,1)} %constant.43.clone.refs_3_.refs_1_) | copy-start | bytes 393220
  70.0 24.1 %copy-start.7 = (f32[512,1]{1,0:T(8,128)S(1)}, f32[512,1]{1,0:T(8,128)}, u32[]{:S(2)}) copy-start(f32[512,1]{1,0:T(8,128)} %constant.48.clone.refs_5_) | copy-start | bytes 6148
  70.0 24.0 %copy-start.10 = (bf16[128,512]{1,0:T(8,128)(2,1)S(1)}, bf16[128,512]{1,0:T(8,128)(2,1)}, u32[]{:S(2)}) copy-start(bf16[128,512]{1,0:T(8,128)(2,1)} %get-tuple-element.39.refs_3_) | copy-start | bytes 393220
  70.0 24.0 %copy-start.11 = (bf16[128,512]{1,0:T(8,128)(2,1)S(1)}, bf16[128,512]{1,0:T(8,128)(2,1)}, u32[]{:S(2)}) copy-start(bf16[128,512]{1,0:T(8,128)(2,1)} %get-tuple-element.40.refs_4_) | copy-start | bytes 393220
  70.0 2.7 %collective-permute-start.3 = (f32[768,128]{1,0:T(8,128)S(1)}, f32[768,128]{1,0:T(8,128)S(1)}, u32[]{:S(2)}, u32[]{:S(2)}) collective-permute-start(f32[768,128]{1,0:T(8,128)S(1)} %get-tuple-element.37.refs_0_.refs_1_), channel_id=1, source_target_pairs={{0,1},{1,0},{2,3},{3,2},{4,5},{5,4},{6,7},{7,6},{8,9},{9,8},{10,11... | collective-permute-start | bytes 1179656 | tf_op jit(solution)/shard_map/ppermute | solution.py:563
  73.3 45.4 %copy-start.1 = (bf16[512,1024]{1,0:T(8,128)(2,1)S(1)}, bf16[512,1024]{1,0:T(8,128)(2,1)}, u32[]{:S(2)}) copy-start(bf16[512,1024]{1,0:T(8,128)(2,1)} %get-tuple-element.41.refs_5_) | copy-start | bytes 3145732
  73.3 45.4 %copy-start.2 = (bf16[256,256]{1,0:T(8,128)(2,1)S(1)}, bf16[256,256]{1,0:T(8,128)(2,1)}, u32[]{:S(2)}) copy-start(bf16[256,256]{1,0:T(8,128)(2,1)} %constant.42.clone.refs_2_.refs_7_) | copy-start | bytes 393220
  73.3 45.4 %copy-start.13 = (f32[32,128]{1,0:T(8,128)S(1)}, f32[32,128]{1,0:T(8,128)}, u32[]{:S(2)}) copy-start(f32[32,128]{1,0:T(8,128)} %get-tuple-element.42.refs_6_) | copy-start | bytes 49156
  116.2 2.5 %collective-permute-start.4 = (f32[768,128]{1,0:T(8,128)S(1)}, f32[768,128]{1,0:T(8,128)S(1)}, u32[]{:S(2)}, u32[]{:S(2)}) collective-permute-start(f32[768,128]{1,0:T(8,128)S(1)} %bitcast.25), channel_id=1, source_target_pairs={{0,1},{1,0},{2,3},{3,2},{4,5},{5,4},{6,7},{7,6},{8,9},{9,8},{10,11... | collective-permute-start | bytes 1179656 | tf_op jit(solution)/shard_map/ppermute | solution.py:580
  123.8 30.3 %copy-start.8 = (f32[128,128]{1,0:T(8,128)S(1)}, f32[128,128]{1,0:T(8,128)}, u32[]{:S(2)}) copy-start(f32[128,128]{1,0:T(8,128)} %refs_3_.5) | copy-start | bytes 196612
  123.9 30.3 %copy-start.9 = (f32[3,16,8,128]{3,2,1,0:T(8,128)S(1)}, f32[3,16,8,128]{3,2,1,0:T(8,128)}, u32[]{:S(2)}) copy-start(f32[3,16,8,128]{3,2,1,0:T(8,128)} %get-tuple-element.46.refs_1_) | copy-start | bytes 589828
  123.9 30.3 %copy-start.12 = (f32[3,16,128]{2,1,0:T(8,128)S(1)}, f32[3,16,128]{2,1,0:T(8,128)}, u32[]{:S(2)}) copy-start(f32[3,16,128]{2,1,0:T(8,128)} %get-tuple-element.47.refs_2_) | copy-start | bytes 73732
  142.6 8.5 %collective-permute-start.5 = (f32[48,128]{1,0:T(8,128)S(1)}, f32[48,128]{1,0:T(8,128)S(1)}, u32[]{:S(2)}, u32[]{:S(2)}) collective-permute-start(f32[48,128]{1,0:T(8,128)S(1)} %get-tuple-element.49), channel_id=1, source_target_pairs={{128,0},{129,1},{130,2},{131,3},{132,4},{133,5},{134,6},{135,7},{1... | collective-permute-start | bytes 73736 | tf_op jit(solution)/shard_map/ppermute | solution.py:629
  143.9 7.2 %collective-permute-start.6 = (f32[48,128]{1,0:T(8,128)S(1)}, f32[48,128]{1,0:T(8,128)S(1)}, u32[]{:S(2)}, u32[]{:S(2)}) collective-permute-start(f32[48,128]{1,0:T(8,128)S(1)} %get-tuple-element.50), channel_id=1, source_target_pairs={{128,8},{129,9},{130,10},{131,11},{132,12},{133,13},{134,14},{135,... | collective-permute-start | bytes 73736 | tf_op jit(solution)/shard_map/ppermute | solution.py:629
  145.2 7.0 %collective-permute-start.7 = (f32[48,128]{1,0:T(8,128)S(1)}, f32[48,128]{1,0:T(8,128)S(1)}, u32[]{:S(2)}, u32[]{:S(2)}) collective-permute-start(f32[48,128]{1,0:T(8,128)S(1)} %get-tuple-element.51), channel_id=1, source_target_pairs={{128,16},{129,17},{130,18},{131,19},{132,20},{133,21},{134,22},{13... | collective-permute-start | bytes 73736 | tf_op jit(solution)/shard_map/ppermute | solution.py:629
  146.5 7.7 %collective-permute-start.8 = (f32[48,128]{1,0:T(8,128)S(1)}, f32[48,128]{1,0:T(8,128)S(1)}, u32[]{:S(2)}, u32[]{:S(2)}) collective-permute-start(f32[48,128]{1,0:T(8,128)S(1)} %get-tuple-element.52), channel_id=1, source_target_pairs={{128,24},{129,25},{130,26},{131,27},{132,28},{133,29},{134,30},{13... | collective-permute-start | bytes 73736 | tf_op jit(solution)/shard_map/ppermute | solution.py:629

commit v4 on v3

--- a/solution.py
+++ b/solution.py
@@ -13,6 +13,8 @@
 NJ = 16
 CY, CZ, CX, CC = 4, 4, 4, 2
 BRICKS = 128
+CHIPS = 64
+HALF = 128
 CAP = 4
 SB = 256
 RPB = 1024
@@ -57,8 +59,7 @@
 
 
 def line_table():
-    dev = np.arange(BRICKS)
-    plane = np.where(dev % 2 == 1, 4 * dev + 3, 4 * dev - 1) + 1
+    plane = 8 * (np.arange(CHIPS) + 1)
     phase = (np.arange(NX) + 1)[:, None] * plane[None, :] % (2 * (NX + 1))
     return np.sin(np.pi * phase / (NX + 1))
 
@@ -139,7 +140,7 @@
 
 
 def ready_kernel(
-    flags, state, speed, sz, kh, kl, rd, rr, rb, out, th, tl, gather, codes, last, lead
+    flags, state, speed, sz, rd, rr, rb, out, gather, codes, last, lead
 ):
     @pl.when(flags[0] == 0)
     def _():
@@ -153,8 +154,6 @@
     def _():
         for c in range(3):
             out[c] = times_paired(state[c], sz[...])
-        th[...] = kh[...].T
-        tl[...] = kl[...].T
         y, z, x, core, lane = owners(rd[...])
         target = (y * CX + x) * CC + core
         gather[...] = lax.dot_general(
@@ -163,7 +162,7 @@
             NT,
             preferred_element_type=f32,
         ).astype(bf16)
-        code = ((z - flags[3]) & (CZ - 1)) * NJ + rb[...] + 1
+        code = z * NJ + rb[...] + 1
         tagged = jnp.where(iota((NZ, SB), 0) == lane, code.astype(f32), 0.0)
         sent = onehot(iota((TARGETS, SB), 0) == target)
         codes[...] = lax.dot_general(sent, tagged.astype(bf16), NT, preferred_element_type=f32)
@@ -182,6 +181,14 @@
     return centre - speed * transport + viscosity * (above - 2.0 * centre + below)
 
 
+def shell_kernel(group, state, out, sem):
+    @pl.when(group[0] == 0)
+    def _():
+        copy = pltpu.make_async_copy(state.at[:, :, pl.ds(NI - NI // 4, NI // 4), :], out, sem)
+        copy.start()
+        copy.wait()
+
+
 def bucket_kernel(flags, blocks, codes, place, merged, out):
     @pl.when(flags[0] != 0)
     def _():
@@ -224,42 +231,74 @@
                 planes[c, p] = plane
             low = g11 * f0 + g12 * f1 + g13 * f2
             high = f3 + g13 * f0 + g12 * f1 + g11 * f2
-            outgoing[c * NY : (c + 1) * NY, :] = jnp.where(first, high, low)
-            kept[c * NY : (c + 1) * NY, :] = jnp.where(first, low, high)
-
-
-def reduce_kernel(flags, outgoing, incoming, kept, mu, out):
+            for kind, value in enumerate((low, high)):
+                block = slice((kind * 3 + c) * HALF, (kind * 3 + c + 1) * HALF)
+                outgoing[block, :] = jnp.where(first, value[HALF:], value[:HALF])
+                kept[block, :] = jnp.where(first, value[:HALF], value[HALF:])
+
+
+def reduce_kernel(flags, incoming, kept, mu, out, joint):
     @pl.when(flags[0] != 0)
     def _():
-        g11, g12, g13 = weights(mu[...] + 2.0)
-        ratio = g13 / (mu[...] + 2.0 - 2.0 * g11)
-        for c in range(3):
-            block = slice(c * NY, (c + 1) * NY)
-            share = kept[block, :] + ratio * (outgoing[block, :] + incoming[block, :])
+        beta = mu[pl.ds(pl.multiple_of(flags[1] * HALF, HALF), HALF), :] + 2.0
+        g11, g12, g13 = weights(beta)
+        ratio = g13 / (beta - 2.0 * g11)
+        first = flags[1] == 0
+        for c in range(3):
+            low, high = (slice((k * 3 + c) * HALF, (k * 3 + c + 1) * HALF) for k in range(2))
+            low0, low1 = (
+                jnp.where(first, kept[low, :], incoming[low, :]),
+                jnp.where(first, incoming[low, :], kept[low, :]),
+            )
+            high0, high1 = (
+                jnp.where(first, kept[high, :], incoming[high, :]),
+                jnp.where(first, incoming[high, :], kept[high, :]),
+            )
+            middle = high0 + low1
+            joint[c * HALF : (c + 1) * HALF, :] = middle
+            for kind, value in enumerate((low0 + ratio * middle, high1 + ratio * middle)):
+                for i in range(2):
+                    out[pl.ds(c * 4 + kind * 2 + i, CHIPS, stride=12), :] = value[
+                        i * CHIPS : (i + 1) * CHIPS
+                    ]
+
+
+def line_kernel(flags, received, spread, th, tl, lamx, mu, out):
+    @pl.when(flags[0] != 0)
+    def _():
+        def part(c, kind, i):
+            return received[pl.ds(c * 4 + kind * 2 + i, CHIPS, stride=12), :]
+
+        place = iota((CHIPS, NZ), 0)
+        rows = []
+        for c in range(3):
             for i in range(2):
-                out[pl.ds(c * 2 + i, BRICKS, stride=6), :] = share[i * BRICKS : (i + 1) * BRICKS]
-
-
-def line_kernel(flags, received, kh, kl, th, tl, lamx, mu, out):
-    @pl.when(flags[0] != 0)
-    def _():
-        shares = jnp.concatenate([received[pl.ds(j, BRICKS, stride=6), :] for j in range(6)], axis=1)
-        modes = table_times(kh[...], kl[...], shares)
+                ahead = jnp.where(
+                    place == CHIPS - 1, 0.0, pltpu.roll(part(c, 0, i), CHIPS - 1, 0)
+                )
+                rows.append(part(c, 1, i) + ahead)
+        high, low = split(jnp.concatenate(rows, axis=1))
+        modes = mm(spread[...], jnp.concatenate([high, low, high], axis=0))
         factors = []
         for i in range(2):
-            row = mu[pl.ds(flags[2] + i * BRICKS, 1), :]
+            row = mu[pl.ds(flags[1] * HALF + i * CHIPS + (flags[2] >> 1), 1), :]
             factors.append((2.0 / (NX + 1)) / (lamx[...] + row))
         modes = modes * jnp.concatenate(factors * 3, axis=1)
         solved = table_times(th[...], tl[...], modes)
-        for j in range(6):
-            out[pl.ds(j, BRICKS, stride=6), :] = solved[:, j * NZ : (j + 1) * NZ]
+        for c in range(3):
+            for i in range(2):
+                j = c * 2 + i
+                value = solved[:, j * NZ : (j + 1) * NZ]
+                behind = jnp.where(place == 0, 0.0, pltpu.roll(value, 1, 0))
+                out[pl.ds(c * 4 + i, CHIPS, stride=12), :] = behind
+                out[pl.ds(c * 4 + 2 + i, CHIPS, stride=12), :] = value
 
 
 def inverse_kernel(
     flags,
     planes,
-    outgoing,
-    incoming,
+    joint,
+    joined,
     own,
     other,
     gather,
@@ -320,15 +359,24 @@
         potentials = []
         for c in range(3):
 
-            def unpacked(ref):
-                return jnp.concatenate(
-                    [ref[pl.ds(c * 2 + i, BRICKS, stride=6), :] for i in range(2)], axis=0
+            def full(pieces):
+                a, b = pieces(own, joint), pieces(other, joined)
+                return jnp.concatenate([jnp.where(first, a, b), jnp.where(first, b, a)], axis=0)
+
+            def solved(kind):
+                return full(
+                    lambda ref, _: jnp.concatenate(
+                        [
+                            ref[pl.ds(c * 4 + kind * 2 + i, CHIPS, stride=12), :]
+                            for i in range(2)
+                        ],
+                        axis=0,
+                    )
                 )
 
-            block = slice(c * NY, (c + 1) * NY)
-            a, b = unpacked(own), unpacked(other)
-            before, after = jnp.where(first, a, b), jnp.where(first, b, a)
-            middle = (outgoing[block, :] + incoming[block, :] + g13 * (before + after)) * inv
+            before, after = solved(0), solved(1)
+            middle = full(lambda _, ref: ref[c * HALF : (c + 1) * HALF, :])
+            middle = (middle + g13 * (before + after)) * inv
             left = jnp.where(first, before, middle)
             right = jnp.where(first, middle, after)
             f0, f1, f2, f3 = (planes[c, p] for p in range(4))
@@ -381,7 +429,7 @@
             copy.wait()
 
 
-def cell_kernel(flags, received, *outs):
+def cell_kernel(flags, received, out):
     @pl.when(flags[0] != 0)
     def _():
         codes = received[pl.ds(3 * GROUP, TARGETS, stride=BACK), :].astype(bf16)
@@ -399,13 +447,13 @@
             )
             sums = pick(cells, rows)
             for k in range(CZ):
-                outs[k][c * NJ : (c + 1) * NJ, :] = sums[k * NJ : (k + 1) * NJ]
-
-
-def close_kernel(flags, field, edge, layer, remesh, b0, b1, b2, b3, out, slab, sem):
+                out[k, c * NJ : (c + 1) * NJ, :] = sums[k * NJ : (k + 1) * NJ]
+
+
+def close_kernel(flags, field, edge, layer, remesh, sums, out, slab, sem):
     @pl.when(flags[0] == 0)
     def _():
-        total = exact((b0[...] + b1[...]) + (b2[...] + b3[...]), remesh[...], NT)
+        total = exact((sums[4] + sums[5]) + (sums[6] + sums[7]), remesh[...], NT)
         first = [total[c * NJ : (c + 1) * NJ] for c in range(3)]
         second = [layer[c] for c in range(3)]
         for c in range(3):
@@ -499,12 +547,22 @@
     syh, syl = halves(sy)
     szp = paired(sz)
     kh, kl = halves(line)
+    triple = np.concatenate([kh, kh, kl], axis=1)
+    th, tl = np.ascontiguousarray(kh.T), np.ascontiguousarray(kl.T)
     lamx = eigen(NX).astype(np.float32)[:, None]
     mu = (eigen(NY)[:, None] + eigen(NZ)[None, :]).astype(np.float32)
 
-    blocks = field.reshape(3, NJ, NI, NK)[:, :, NI - NI // 4 :, :].reshape(3, SB, NK)
+    group = lax.axis_index("grp").astype(i32).reshape(1)
+    (blocks,) = call(
+        shell_kernel,
+        [((3, NJ, NI // 4, NK), f32)],
+        group,
+        field.reshape(3, NJ, NI, NK),
+        far=1,
+        scratch=[pltpu.SemaphoreType.DMA],
+    )
     across = [(place_of(0, *q), place_of(1, *q)) for q in chips()]
-    blocks = lax.ppermute(blocks, ALL, across)
+    blocks = lax.ppermute(blocks.reshape(3, SB, NK), ALL, across)
 
     sd, sr, rd, rr, rb = (
         v.reshape(1, SB) for v in (shell_dest, shell_row, return_dest, return_row, return_block)
@@ -523,12 +581,10 @@
         bucket_kernel, [((BRICKS * CHUNK, NZ), f32)], flags, blocks, codes, place, merged
     )
     bundle = lax.all_to_all(bundle.reshape(BRICKS, CHUNK, 1, NZ), DEV, 0, 0, tiled=True)
-    turned, th, tl, gather, codes, last, lead = call(
+    turned, gather, codes, last, lead = call(
         ready_kernel,
         [
             ((3, RPB, NZ), f32),
-            ((BRICKS, NX), bf16, "home"),
-            ((BRICKS, NX), bf16, "home"),
             ((SLOTS, RPB), bf16, "home"),
             ((TARGETS, NZ), f32, "home"),
             ((896, NK), f32, "home"),
@@ -538,8 +594,6 @@
         field,
         speed,
         szp,
-        kh,
-        kl,
         rd,
         rr,
         rb,
@@ -560,23 +614,32 @@
         mu,
     )
     swap = [(0, 1), (1, 0)]
+    same = ("y", "z", "x")
     incoming = lax.ppermute(outgoing, "core", swap)
-    (share,) = call(reduce_kernel, [((3 * NY, NZ), f32)], flags, outgoing, incoming, kept, mu)
-    share = lax.all_to_all(share.reshape(BRICKS, 3, 2, NZ), DEV, 0, 0, tiled=True)
+    share, joint = call(
+        reduce_kernel,
+        [((CHIPS * 12, NZ), f32), ((3 * HALF, NZ), f32)],
+        flags,
+        incoming,
+        kept,
+        mu,
+    )
+    joined = lax.ppermute(joint, "core", swap)
+    share = lax.all_to_all(share.reshape(CHIPS, 3, 4, NZ), same, 0, 0, tiled=True)
+    share, joined = lax.optimization_barrier((share, joined))
     (solved,) = call(
         line_kernel,
-        [((3 * NY, NZ), f32)],
+        [((CHIPS * 12, NZ), f32)],
         flags,
-        share.reshape(3 * NY, NZ),
-        kh,
-        kl,
+        share.reshape(CHIPS * 12, NZ),
+        triple,
         th,
         tl,
         lamx,
         mu,
     )
-    own = lax.all_to_all(solved.reshape(BRICKS, 3, 2, NZ), DEV, 0, 0, tiled=True)
-    own = own.reshape(3 * NY, NZ)
+    own = lax.all_to_all(solved.reshape(CHIPS, 3, 4, NZ), same, 0, 0, tiled=True)
+    own = own.reshape(CHIPS * 12, NZ)
     other = lax.ppermute(own, "core", swap)
     halo = pltpu.VMEM((896, NK), f32)
     send, result, edge, layer = call(
@@ -589,8 +652,8 @@
         ],
         flags,
         planes,
-        outgoing,
-        incoming,
+        joint,
+        joined,
         own,
         other,
         gather,
@@ -618,15 +681,10 @@
     returned = lax.all_to_all(
         send.reshape(TARGETS, BACK, 1, NZ), ("y", "x", "core"), 0, 0, tiled=True
     )
-    sums = call(
-        cell_kernel, [((3 * NJ, NZ), f32)] * CZ, flags, returned.reshape(TARGETS * BACK, NZ)
-    )
-    parts = []
-    for k in range(CZ):
-        pairs = [
-            (place_of(1, y, z, x, c), place_of(0, y, (z + k) % CZ, x, c)) for y, z, x, c in chips()
-        ]
-        parts.append(lax.ppermute(sums[k], ALL, pairs))
+    (sums,) = call(
+        cell_kernel, [((2 * CZ, 3 * NJ, NZ), f32)], flags, returned.reshape(TARGETS * BACK, NZ)
+    )
+    sums = lax.all_to_all(sums, ("grp", "z"), 0, 0, tiled=True)
     (result,) = call(
         close_kernel,
         [((3, NJ, NI, NZ), f32, "raw")],
@@ -635,7 +693,7 @@
         edge,
         layer,
         remesh,
-        *parts,
+        sums,
         alias=True,
         scratch=[pltpu.VMEM((3, NJ, 8, NZ), f32), pltpu.SemaphoreType.DMA],
     )

time: 156 us -> 161 us (1.032)
  blocking collectives: 60.4 us -> 52 us
  waiting for transfers between devices: 35.7 us -> 43.3 us
  local copies, waits for them, and re-layouts: 1.11 us -> 3.83 us
  Pallas kernels: 16.2 us -> 17.9 us
    all_to_all x0 -> x1, waiting for transfers between devices: none -> 12.7 us  [on_device(): lax.all_to_all(share.reshape(CHIPS, 3, 4, NZ), same, 0, 0, tiled=True)]
    all_to_all x2, blocking collectives: 42.3 us -> 34 us  [the longest x1 18.5 us: on_device(): lax.all_to_all(solved.reshape(CHIPS, 3, 4, NZ), same, 0, 0, tiled=True)]
    ppermute x5 -> x2, starting transfers between devices: 14.8 us -> 9.12 us  [the longest x1 8.66 us: on_device(): blocks = lax.ppermute(blocks.reshape(3, SB, NK), ALL, across)]
    ppermute x5 -> x2, waiting for transfers between devices: 11.9 us -> 6.61 us  [the longest x1 5.54 us: on_device(): blocks = lax.ppermute(blocks.reshape(3, SB, NK), ALL, across)]
    all_to_all x0 -> x1, starting transfers between devices: none -> 4.76 us  [on_device(): lax.all_to_all(share.reshape(CHIPS, 3, 4, NZ), same, 0, 0, tiled=True)]
    unnamed x30 -> x40, local copies, waits for them, and re-layouts: 0.09 us -> 3.83 us
    ppermute x1, starting transfers between devices: 1.1 us -> 2.9 us  [on_device(): other = lax.ppermute(own, 'core', swap)]
    pallas_call x9 -> x10, Pallas kernels: 16.2 us -> 17.9 us  [call(): pl.pallas_call(body, out_shape=[(pltpu.HBM if home else pltpu.VMEM)(*o[:2...]
  transfers between devices with their start and end apart: 10 -> 8, of which waited for: 9 -> 8; matrix products, arithmetic and copies ran while one was open for 0% -> 0% of each run, Pallas kernels for 4% -> 4%
where the time goes in v4:
time: 161 us; the launch traced here: 160 us
  blocking collectives  52 us (32%)
  waiting for transfers between devices  43.3 us (27%)
  starting transfers between devices  42.8 us (27%)
  Pallas kernels  17.9 us (11%)
  local copies, waits for them, and re-layouts  3.83 us (2%)
    all_to_all x1, starting transfers between devices, on_device(): lax.all_to_all(bundle.reshape(BRICKS, CHUNK, 1, NZ), DEV, 0, 0, tiled=True)  19.3 us
    all_to_all x1, blocking collectives, on_device(): lax.all_to_all(solved.reshape(CHIPS, 3, 4, NZ), same, 0, 0, tiled=True)  18.5 us
    all_to_all x1, blocking collectives, on_device(): lax.all_to_all(send.reshape(TARGETS, BACK, 1, NZ), ('y', 'x', 'core'), 0,...  18 us
    pallas_call x10, Pallas kernels, call(): pl.pallas_call(body, out_shape=[(pltpu.HBM if home else pltpu.VMEM)(*o[:2...  17.9 us
    all_to_all x1, blocking collectives, on_device(): sums = lax.all_to_all(sums, ('grp', 'z'), 0, 0, tiled=True)  15.6 us
    all_to_all x1, waiting for transfers between devices, on_device(): lax.all_to_all(share.reshape(CHIPS, 3, 4, NZ), same, 0, 0, tiled=True)  12.7 us
    all_to_all x1, waiting for transfers between devices, on_device(): lax.all_to_all(bundle.reshape(BRICKS, CHUNK, 1, NZ), DEV, 0, 0, tiled=True)  11.7 us
    ppermute x1, starting transfers between devices, on_device(): blocks = lax.ppermute(blocks.reshape(3, SB, NK), ALL, across)  8.66 us
  transfers between devices with their start and end apart: 8, of which 8 were waited for; matrix products, arithmetic and copies ran while one was open for 0% of the time, Pallas kernels for 4%

profile of v4, /device:TPU:1, one launch (start us, length us, event | category | flops | bytes accessed | tf_op | source)
XLA Modules:
  0.0 160.2 jit_solution(15173902574433295350)
XLA Ops:
  0.0 1.0 shell_kernel.1
  1.0 8.7 %collective-permute-start = (f32[3,256,128]{2,1,0:T(8,128)S(1)}, f32[3,256,128]{2,1,0:T(8,128)S(1)}, u32[]{:S(2)}, u32[]{:S(2)}) collective-permute-start(f32[3,256,128]{2,1,0:T(8,128)S(1)} %bitcast.30), channel_id=1, source_target_pairs={{0,128},{1,129},{2,130},{3,131},{4,132},{5,133},{6,134},{7,135},{8... | collective-permute-start | bytes 1179656 | tf_op jit(solution)/shard_map/ppermute | solution.py:565
  9.8 2.1 %route_kernel.1 = (bf16[512,256]{1,0:T(8,128)(2,1)S(1)}, f32[128,128]{1,0:T(8,128)S(1)}, bf16[256,256]{1,0:T(8,128)(2,1)S(1)}) custom-call(s32[4]{0:T(128)S(1)} %pad_add_fusion.flags, s32[1,256]{1,0:T(1,128)} %bitcast.37, s32[1,256]{1,0:T(1,128)} %bitcast.38, f32[128,128]{1,0:T(8,128)} %refs_3_.4, f32[128,128]{1,0:T(8,128)} %constant.43.clone.refs_3_), custom_call_target="tpu_custom_call" | custom-call | tf_op jit(solution)/shard_map/route_kernel/pallas_call | solution.py:508
  11.9 5.5 %collective-permute-done.refs_0_ = f32[3,256,128]{2,1,0:T(8,128)S(1)} collective-permute-done((f32[3,256,128]{2,1,0:T(8,128)S(1)}, f32[3,256,128]{2,1,0:T(8,128)S(1)}, u32[]{:S(2)}, u32[]{:S(2)}) %collective-permute-start) | collective-permute-done | bytes 393248 | tf_op jit(solution)/shard_map/ppermute | solution.py:565
  17.4 1.4 bucket_kernel.1
  18.9 19.3 %all-to-all-start = ((f32[128,13,1,128]{3,2,1,0:T(1,128)}), f32[128,13,1,128]{3,2,1,0:T(1,128)S(1)}, u32[]{:S(2)}, u32[]{:S(2)}) async-start(f32[128,13,1,128]{3,2,1,0:T(1,128)} %bitcast.8), calls=%async_computation | async-start | bytes 1703936 | tf_op jit(solution)/shard_map/all_to_all | solution.py:583
  38.2 3.5 %ready_kernel.1 = (f32[3,1024,128]{2,1,0:T(8,128)S(1)}, bf16[512,1024]{1,0:T(8,128)(2,1)}, f32[32,128]{1,0:T(8,128)}, f32[896,128]{1,0:T(8,128)}, f32[896,128]{1,0:T(8,128)}) custom-call(s32[4]{0:T(128)S(1)} %pad_add_fusion.flags, f32[3,1024,128]{2,1,0:T(8,128)} %bitcast.32, f32[1024,128]{1,0:T(8,128)} %bitcast.34, ...), custom_call_target="tpu_custom_call" | custom-call | tf_op jit(solution)/shard_map/ready_kernel/pallas_call | solution.py:508
  41.7 3.5 %collective-permute-start.1 = (f32[896,128]{1,0:T(8,128)}, f32[896,128]{1,0:T(8,128)S(1)}, u32[]{:S(2)}, u32[]{:S(2)}) collective-permute-start(f32[896,128]{1,0:T(8,128)} %get-tuple-element.30), channel_id=1, source_target_pairs={{0,1},{1,2},{2,3},{3,4},{4,5},{5,6},{6,7},{7,8},{8,9},{9,10},{10,1... | collective-permute-start | bytes 1376264 | tf_op jit(solution)/shard_map/ppermute | solution.py:603
  45.2 1.9 %collective-permute-start.2 = (f32[896,128]{1,0:T(8,128)}, f32[896,128]{1,0:T(8,128)}, u32[]{:S(2)}, u32[]{:S(2)}) collective-permute-start(f32[896,128]{1,0:T(8,128)} %get-tuple-element.31), channel_id=1, source_target_pairs={{1,0},{2,1},{3,2},{4,3},{5,4},{6,5},{7,6},{8,7},{9,8},{10,9},{11,1... | collective-permute-start | bytes 1376264 | tf_op jit(solution)/shard_map/ppermute | solution.py:604
  47.2 5.9 %collective-permute-done.1.refs_13_ = f32[896,128]{1,0:T(8,128)S(1)} collective-permute-done((f32[896,128]{1,0:T(8,128)}, f32[896,128]{1,0:T(8,128)S(1)}, u32[]{:S(2)}, u32[]{:S(2)}) %collective-permute-start.1) | collective-permute-done | bytes 458784 | tf_op jit(solution)/shard_map/ppermute | solution.py:603
  53.1 3.8 %collective-permute-done.2.refs_14_ = f32[896,128]{1,0:T(8,128)} collective-permute-done((f32[896,128]{1,0:T(8,128)}, f32[896,128]{1,0:T(8,128)}, u32[]{:S(2)}, u32[]{:S(2)}) %collective-permute-start.2) | collective-permute-done | bytes 458784 | tf_op jit(solution)/shard_map/ppermute | solution.py:604
  56.8 11.7 %all-to-all-done = f32[128,13,1,128]{3,2,1,0:T(1,128)S(1)} async-done(((f32[128,13,1,128]{3,2,1,0:T(1,128)}), f32[128,13,1,128]{3,2,1,0:T(1,128)S(1)}, u32[]{:S(2)}, u32[]{:S(2)}) %all-to-all-start) | async-done | bytes 852000 | tf_op jit(solution)/shard_map/all_to_all | solution.py:583
  68.5 0.6 forward_kernel.1
  69.1 1.1 copy-done.1
  70.2 1.3 collective-permute-start.3
  71.5 1.3 collective-permute-done.3.refs_0_
  72.9 1.3 reduce_kernel.1
  74.2 4.8 %all-to-all-start.1 = ((f32[64,3,4,128]{3,2,1,0:T(4,128)}), f32[64,3,4,128]{3,2,1,0:T(4,128)S(1)}, u32[]{:S(2)}, u32[]{:S(2)}) async-start(f32[64,3,4,128]{3,2,1,0:T(4,128)} %bitcast.15), calls=%async_computation.1 | async-start | bytes 786432 | tf_op jit(solution)/shard_map/all_to_all | solution.py:628
  79.4 1.1 collective-permute-done.4.refs_2_
  80.5 0.7 copy-done.13
  81.1 12.7 %all-to-all-done.1 = f32[64,3,4,128]{3,2,1,0:T(4,128)S(1)} async-done(((f32[64,3,4,128]{3,2,1,0:T(4,128)}), f32[64,3,4,128]{3,2,1,0:T(4,128)S(1)}, u32[]{:S(2)}, u32[]{:S(2)}) %all-to-all-start.1) | async-done | bytes 393248 | tf_op jit(solution)/shard_map/all_to_all | solution.py:628
  93.9 0.6 line_kernel.1
  94.4 18.5 %all_to_all.25 = f32[64,3,4,128]{3,2,1,0:T(4,128)S(1)} all-to-all(f32[64,3,4,128]{3,2,1,0:T(4,128)S(1)} %bitcast.26), channel_id=1, replica_groups=mesh['grp'=2,'y'=4,'z'=4,'x'=4,'core'=2] {'y','z','x'}, dimensions={0} | all-to-all | bytes 786432 | tf_op jit(solution)/shard_map/all_to_all | solution.py:641
  112.9 2.9 %collective-permute-start.5 = (f32[768,128]{1,0:T(8,128)S(1)}, f32[768,128]{1,0:T(8,128)S(1)}, u32[]{:S(2)}, u32[]{:S(2)}) collective-permute-start(f32[768,128]{1,0:T(8,128)S(1)} %bitcast.27), channel_id=1, source_target_pairs={{0,1},{1,0},{2,3},{3,2},{4,5},{5,4},{6,7},{7,6},{8,9},{9,8},{10,11... | collective-permute-start | bytes 1179656 | tf_op jit(solution)/shard_map/ppermute | solution.py:643
  115.8 1.3 collective-permute-done.5.refs_4_
  117.2 1.2 copy-done.3
  118.4 0.7 copy-done.18
  119.1 5.4 %inverse_kernel.1 = (f32[1568,128]{1,0:T(8,128)S(1)}, f32[3,1024,128]{2,1,0:T(8,128)}, f32[3,16,8,128]{3,2,1,0:T(8,128)}, f32[3,16,128]{2,1,0:T(8,128)}) custom-call(s32[4]{0:T(128)S(1)} %pad_add_fusion.flags, f32[3,4,256,128]{3,2,1,0:T(8,128)S(1)} %copy-done.2, f32[384,128]{1,0:T(8,128)S(1)} %copy-done.12, f32[384,128]{1,0:T(8,128)S(1)} %copy-done.14, ...), custom_call_target="tpu_custom_call" | custom-call | tf_op jit(solution)/shard_map/inverse_kernel/pallas_call | solution.py:508
  124.5 18.0 %all_to_all.26 = f32[32,49,1,128]{3,2,1,0:T(1,128)S(1)} all-to-all(f32[32,49,1,128]{3,2,1,0:T(1,128)S(1)} %bitcast.29), channel_id=1, replica_groups=mesh['grp'=2,'y'=4,'z'=4,'x'=4,'core'=2] {'y','x','core'}, dimensions={0} | all-to-all | bytes 1605632 | tf_op jit(solution)/shard_map/all_to_all | solution.py:681
  142.4 0.5 cell_kernel.1
  143.0 15.6 %all_to_all.27.refs_4_ = f32[8,48,128]{2,1,0:T(8,128)S(1)} all-to-all(f32[8,48,128]{2,1,0:T(8,128)S(1)} %cell_kernel.1), channel_id=1, replica_groups=mesh['grp'=2,'y'=4,'z'=4,'x'=4,'core'=2] {'grp','z'}, dimensions={0} | all-to-all | bytes 393216 | tf_op jit(solution)/shard_map/all_to_all | solution.py:687
  158.6 1.5 close_kernel.1
  (38 shorter events, 0.6 us)
Async XLA Ops:
  1.0 16.4 %collective-permute-start = (f32[3,256,128]{2,1,0:T(8,128)S(1)}, f32[3,256,128]{2,1,0:T(8,128)S(1)}, u32[]{:S(2)}, u32[]{:S(2)}) collective-permute-start(f32[3,256,128]{2,1,0:T(8,128)S(1)} %bitcast.30), channel_id=1, source_target_pairs={{0,128},{1,129},{2,130},{3,131},{4,132},{5,133},{6,134},{7,135},{8... | collective-permute-start | bytes 1179656 | tf_op jit(solution)/shard_map/ppermute | solution.py:565
  18.9 49.6 %copy-start = (f32[256,128]{1,0:T(8,128)S(1)}, f32[256,128]{1,0:T(8,128)}, u32[]{:S(2)}) copy-start(f32[256,128]{1,0:T(8,128)} %constant.47.clone.refs_4_.refs_2_.refs_5_.refs_10_) | copy-start | bytes 393220
  18.9 49.6 %copy-start.4 = (bf16[256,256]{1,0:T(8,128)(2,1)S(1)}, bf16[256,256]{1,0:T(8,128)(2,1)}, u32[]{:S(2)}) copy-start(bf16[256,256]{1,0:T(8,128)(2,1)} %constant.46.clone.refs_3_.refs_9_) | copy-start | bytes 393220
  18.9 49.6 %copy-start.5 = (bf16[256,256]{1,0:T(8,128)(2,1)S(1)}, bf16[256,256]{1,0:T(8,128)(2,1)}, u32[]{:S(2)}) copy-start(bf16[256,256]{1,0:T(8,128)(2,1)} %constant.45.clone.refs_2_.refs_8_) | copy-start | bytes 393220
  18.9 49.6 %all-to-all-start = ((f32[128,13,1,128]{3,2,1,0:T(1,128)}), f32[128,13,1,128]{3,2,1,0:T(1,128)S(1)}, u32[]{:S(2)}, u32[]{:S(2)}) async-start(f32[128,13,1,128]{3,2,1,0:T(1,128)} %bitcast.8), calls=%async_computation | async-start | bytes 1703936 | tf_op jit(solution)/shard_map/all_to_all | solution.py:583
  41.7 11.4 %collective-permute-start.1 = (f32[896,128]{1,0:T(8,128)}, f32[896,128]{1,0:T(8,128)S(1)}, u32[]{:S(2)}, u32[]{:S(2)}) collective-permute-start(f32[896,128]{1,0:T(8,128)} %get-tuple-element.30), channel_id=1, source_target_pairs={{0,1},{1,2},{2,3},{3,4},{4,5},{5,6},{6,7},{7,8},{8,9},{9,10},{10,1... | collective-permute-start | bytes 1376264 | tf_op jit(solution)/shard_map/ppermute | solution.py:603
  45.2 11.6 %collective-permute-start.2 = (f32[896,128]{1,0:T(8,128)}, f32[896,128]{1,0:T(8,128)}, u32[]{:S(2)}, u32[]{:S(2)}) collective-permute-start(f32[896,128]{1,0:T(8,128)} %get-tuple-element.31), channel_id=1, source_target_pairs={{1,0},{2,1},{3,2},{4,3},{5,4},{6,5},{7,6},{8,7},{9,8},{10,9},{11,1... | collective-permute-start | bytes 1376264 | tf_op jit(solution)/shard_map/ppermute | solution.py:604
  53.1 15.4 %copy-start.19 = (f32[896,128]{1,0:T(8,128)}, f32[896,128]{1,0:T(8,128)S(1)}, u32[]{:S(2)}) copy-start(f32[896,128]{1,0:T(8,128)S(1)} %collective-permute-done.1.refs_13_) | copy-start | bytes 1376260
  68.5 25.3 %copy-start.8 = (f32[512,1]{1,0:T(8,128)S(1)}, f32[512,1]{1,0:T(8,128)}, u32[]{:S(2)}) copy-start(f32[512,1]{1,0:T(8,128)} %constant.51.clone.refs_4_) | copy-start | bytes 6148
  68.5 25.3 %copy-start.9 = (bf16[512,192]{1,0:T(8,128)(2,1)S(1)}, bf16[512,192]{1,0:T(8,128)(2,1)}, u32[]{:S(2)}) copy-start(bf16[512,192]{1,0:T(8,128)(2,1)} %constant.48.clone.refs_1_) | copy-start | bytes 589828
  68.5 25.3 %copy-start.15 = (bf16[64,512]{1,0:T(8,128)(2,1)S(1)}, bf16[64,512]{1,0:T(8,128)(2,1)}, u32[]{:S(2)}) copy-start(bf16[64,512]{1,0:T(8,128)(2,1)} %constant.50.clone.refs_3_) | copy-start | bytes 196612
  69.1 1.1 copy-start.1
  70.2 23.6 %copy-start.16 = (bf16[64,512]{1,0:T(8,128)(2,1)S(1)}, bf16[64,512]{1,0:T(8,128)(2,1)}, u32[]{:S(2)}) copy-start(bf16[64,512]{1,0:T(8,128)(2,1)} %constant.49.clone.refs_2_) | copy-start | bytes 196612
  70.2 2.6 %collective-permute-start.3 = (f32[768,128]{1,0:T(8,128)S(1)}, f32[768,128]{1,0:T(8,128)S(1)}, u32[]{:S(2)}, u32[]{:S(2)}) collective-permute-start(f32[768,128]{1,0:T(8,128)S(1)} %get-tuple-element.35), channel_id=1, source_target_pairs={{0,1},{1,0},{2,3},{3,2},{4,5},{5,4},{6,7},{7,6},{8,9},{9,8},{10,11... | collective-permute-start | bytes 1179656 | tf_op jit(solution)/shard_map/ppermute | solution.py:618
  74.2 19.7 %copy-start.11 = (f32[384,128]{1,0:T(8,128)}, f32[384,128]{1,0:T(8,128)S(1)}, u32[]{:S(2)}) copy-start(f32[384,128]{1,0:T(8,128)S(1)} %get-tuple-element.37.refs_1_) | copy-start | bytes 589828
  74.2 43.0 %copy-start.2 = (f32[3,4,256,128]{3,2,1,0:T(8,128)S(1)}, f32[3,4,256,128]{3,2,1,0:T(8,128)}, u32[]{:S(2)}) copy-start(f32[3,4,256,128]{3,2,1,0:T(8,128)} %copy-done.1) | copy-start | bytes 4718596
  74.2 43.0 %copy-start.6 = (bf16[256,256]{1,0:T(8,128)(2,1)S(1)}, bf16[256,256]{1,0:T(8,128)(2,1)}, u32[]{:S(2)}) copy-start(bf16[256,256]{1,0:T(8,128)(2,1)} %constant.44.clone.refs_2_.refs_7_) | copy-start | bytes 393220
  74.2 19.7 %all-to-all-start.1 = ((f32[64,3,4,128]{3,2,1,0:T(4,128)}), f32[64,3,4,128]{3,2,1,0:T(4,128)S(1)}, u32[]{:S(2)}, u32[]{:S(2)}) async-start(f32[64,3,4,128]{3,2,1,0:T(4,128)} %bitcast.15), calls=%async_computation.1 | async-start | bytes 786432 | tf_op jit(solution)/shard_map/all_to_all | solution.py:628
  78.9 1.5 collective-permute-start.4
  80.5 0.7 copy-start.13
  93.8 23.3 %copy-start.14 = (f32[384,128]{1,0:T(8,128)S(1)}, f32[384,128]{1,0:T(8,128)}, u32[]{:S(2)}) copy-start(f32[384,128]{1,0:T(8,128)} %copy-done.13) | copy-start | bytes 589828
  93.9 23.3 %copy-start.12 = (f32[384,128]{1,0:T(8,128)S(1)}, f32[384,128]{1,0:T(8,128)}, u32[]{:S(2)}) copy-start(f32[384,128]{1,0:T(8,128)} %copy-done.11) | copy-start | bytes 589828
  112.9 4.2 %collective-permute-start.5 = (f32[768,128]{1,0:T(8,128)S(1)}, f32[768,128]{1,0:T(8,128)S(1)}, u32[]{:S(2)}, u32[]{:S(2)}) collective-permute-start(f32[768,128]{1,0:T(8,128)S(1)} %bitcast.27), channel_id=1, source_target_pairs={{0,1},{1,0},{2,3},{3,2},{4,5},{5,4},{6,7},{7,6},{8,9},{9,8},{10,11... | collective-permute-start | bytes 1179656 | tf_op jit(solution)/shard_map/ppermute | solution.py:643
  117.1 1.2 copy-start.3
  118.4 0.7 copy-start.18
  124.4 34.1 %copy-start.7 = (f32[128,128]{1,0:T(8,128)S(1)}, f32[128,128]{1,0:T(8,128)}, u32[]{:S(2)}) copy-start(f32[128,128]{1,0:T(8,128)} %refs_3_.4) | copy-start | bytes 196612
  124.5 34.1 %copy-start.10 = (f32[3,16,8,128]{3,2,1,0:T(8,128)S(1)}, f32[3,16,8,128]{3,2,1,0:T(8,128)}, u32[]{:S(2)}) copy-start(f32[3,16,8,128]{3,2,1,0:T(8,128)} %get-tuple-element.46.refs_1_) | copy-start | bytes 589828
  124.5 34.1 %copy-start.17 = (f32[3,16,128]{2,1,0:T(8,128)S(1)}, f32[3,16,128]{2,1,0:T(8,128)}, u32[]{:S(2)}) copy-start(f32[3,16,128]{2,1,0:T(8,128)} %get-tuple-element.47.refs_2_) | copy-start | bytes 73732

commit v5 on v4

--- a/solution.py
+++ b/solution.py
@@ -162,7 +162,7 @@
             NT,
             preferred_element_type=f32,
         ).astype(bf16)
-        code = z * NJ + rb[...] + 1
+        code = ((z - flags[3]) & (CZ - 1)) * NJ + rb[...] + 1
         tagged = jnp.where(iota((NZ, SB), 0) == lane, code.astype(f32), 0.0)
         sent = onehot(iota((TARGETS, SB), 0) == target)
         codes[...] = lax.dot_general(sent, tagged.astype(bf16), NT, preferred_element_type=f32)
@@ -241,7 +241,7 @@
     @pl.when(flags[0] != 0)
     def _():
         beta = mu[pl.ds(pl.multiple_of(flags[1] * HALF, HALF), HALF), :] + 2.0
-        g11, g12, g13 = weights(beta)
+        g11, _, g13 = weights(beta)
         ratio = g13 / (beta - 2.0 * g11)
         first = flags[1] == 0
         for c in range(3):
@@ -429,7 +429,7 @@
             copy.wait()
 
 
-def cell_kernel(flags, received, out):
+def cell_kernel(flags, received, *outs):
     @pl.when(flags[0] != 0)
     def _():
         codes = received[pl.ds(3 * GROUP, TARGETS, stride=BACK), :].astype(bf16)
@@ -447,13 +447,13 @@
             )
             sums = pick(cells, rows)
             for k in range(CZ):
-                out[k, c * NJ : (c + 1) * NJ, :] = sums[k * NJ : (k + 1) * NJ]
-
-
-def close_kernel(flags, field, edge, layer, remesh, sums, out, slab, sem):
+                outs[k][c * NJ : (c + 1) * NJ, :] = sums[k * NJ : (k + 1) * NJ]
+
+
+def close_kernel(flags, field, edge, layer, remesh, b0, b1, b2, b3, out, slab, sem):
     @pl.when(flags[0] == 0)
     def _():
-        total = exact((sums[4] + sums[5]) + (sums[6] + sums[7]), remesh[...], NT)
+        total = exact((b0[...] + b1[...]) + (b2[...] + b3[...]), remesh[...], NT)
         first = [total[c * NJ : (c + 1) * NJ] for c in range(3)]
         second = [layer[c] for c in range(3)]
         for c in range(3):
@@ -516,7 +516,6 @@
         scratch_shapes=loads + stores + sems + list(scratch),
         input_output_aliases={1: 0} if alias else {},
         compiler_params=pltpu.CompilerParams(vmem_limit_bytes=24 << 20),
-        name=kernel.__name__,
     )(
         flags,
         *[
@@ -567,7 +566,7 @@
     sd, sr, rd, rr, rb = (
         v.reshape(1, SB) for v in (shell_dest, shell_row, return_dest, return_row, return_block)
     )
-    place, codes, merged = call(
+    place, rows, merged = call(
         route_kernel,
         [((SLOTS, SB), bf16), ((BRICKS, NZ), f32), ((2 * NK, 2 * NZ), bf16)],
         flags,
@@ -577,10 +576,6 @@
         sz.astype(np.float32),
         fetch=True,
     )
-    (bundle,) = call(
-        bucket_kernel, [((BRICKS * CHUNK, NZ), f32)], flags, blocks, codes, place, merged
-    )
-    bundle = lax.all_to_all(bundle.reshape(BRICKS, CHUNK, 1, NZ), DEV, 0, 0, tiled=True)
     turned, gather, codes, last, lead = call(
         ready_kernel,
         [
@@ -599,6 +594,12 @@
         rb,
         fetch=True,
     )
+    blocks, turned = lax.optimization_barrier((blocks, turned))
+    (bundle,) = call(
+        bucket_kernel, [((BRICKS * CHUNK, NZ), f32)], flags, blocks, rows, place, merged
+    )
+    bundle, last, lead = lax.optimization_barrier((bundle, last, lead))
+    bundle = lax.all_to_all(bundle.reshape(BRICKS, CHUNK, 1, NZ), DEV, 0, 0, tiled=True)
     ahead = [(d, (d + 1) % BRICKS) for d in range(BRICKS)]
     up = lax.ppermute(last, ALL, ahead)
     down = lax.ppermute(lead, ALL, [(b, a) for a, b in ahead])
@@ -626,7 +627,6 @@
     )
     joined = lax.ppermute(joint, "core", swap)
     share = lax.all_to_all(share.reshape(CHIPS, 3, 4, NZ), same, 0, 0, tiled=True)
-    share, joined = lax.optimization_barrier((share, joined))
     (solved,) = call(
         line_kernel,
         [((CHIPS * 12, NZ), f32)],
@@ -681,10 +681,15 @@
     returned = lax.all_to_all(
         send.reshape(TARGETS, BACK, 1, NZ), ("y", "x", "core"), 0, 0, tiled=True
     )
-    (sums,) = call(
-        cell_kernel, [((2 * CZ, 3 * NJ, NZ), f32)], flags, returned.reshape(TARGETS * BACK, NZ)
-    )
-    sums = lax.all_to_all(sums, ("grp", "z"), 0, 0, tiled=True)
+    sums = call(
+        cell_kernel, [((3 * NJ, NZ), f32)] * CZ, flags, returned.reshape(TARGETS * BACK, NZ)
+    )
+    parts = []
+    for k in range(CZ):
+        pairs = [
+            (place_of(1, y, z, x, c), place_of(0, y, (z + k) % CZ, x, c)) for y, z, x, c in chips()
+        ]
+        parts.append(lax.ppermute(sums[k], ALL, pairs))
     (result,) = call(
         close_kernel,
         [((3, NJ, NI, NZ), f32, "raw")],
@@ -693,7 +698,7 @@
         edge,
         layer,
         remesh,
-        sums,
+        *parts,
         alias=True,
         scratch=[pltpu.VMEM((3, NJ, 8, NZ), f32), pltpu.SemaphoreType.DMA],
     )

time: 161 us -> 152 us (0.944)
  waiting for transfers between devices: 43.3 us -> 36.3 us
  local copies, waits for them, and re-layouts: 3.83 us -> 0.07 us
  blocking collectives: 52 us -> 55 us
    all_to_all x1 -> x0, waiting for transfers between devices: 12.7 us -> none  [on_device(): lax.all_to_all(share.reshape(CHIPS, 3, 4, NZ), same, 0, 0, tiled=True)]
    ppermute x0 -> x4, waiting for transfers between devices: none -> 6.44 us  [on_device(): parts.append(lax.ppermute(sums[k], ALL, pairs))]
    ppermute x0 -> x4, starting transfers between devices: none -> 5.17 us  [on_device(): parts.append(lax.ppermute(sums[k], ALL, pairs))]
    all_to_all x1 -> x0, starting transfers between devices: 4.76 us -> none  [on_device(): lax.all_to_all(share.reshape(CHIPS, 3, 4, NZ), same, 0, 0, tiled=True)]
    unnamed x40 -> x28, local copies, waits for them, and re-layouts: 3.83 us -> 0.07 us
    ppermute x1, waiting for transfers between devices: 5.54 us -> 2.03 us  [on_device(): blocks = lax.ppermute(blocks.reshape(3, SB, NK), ALL, across)]
    all_to_all x1, blocking collectives: 15.6 us -> 18.5 us  [on_device(): lax.all_to_all(share.reshape(CHIPS, 3, 4, NZ), same, 0, 0, tiled=True)]
    all_to_all x1, waiting for transfers between devices: 11.7 us -> 14 us  [on_device(): lax.all_to_all(bundle.reshape(BRICKS, CHUNK, 1, NZ), DEV, 0, 0, tiled=True)]
  transfers between devices with their start and end apart: 8 -> 11, of which waited for: 8 -> 9; matrix products, arithmetic and copies ran while one was open for 0% -> 0% of each run, Pallas kernels for 4% -> 4%
where the time goes in v5:
time: 152 us
  blocking collectives  55 us (36%)
  starting transfers between devices  42.8 us (28%)
  waiting for transfers between devices  36.3 us (24%)
  Pallas kernels  17.1 us (11%)
    all_to_all x1, starting transfers between devices, on_device(): lax.all_to_all(bundle.reshape(BRICKS, CHUNK, 1, NZ), DEV, 0, 0, tiled=True)  19.1 us
    all_to_all x1, blocking collectives, on_device(): lax.all_to_all(solved.reshape(CHIPS, 3, 4, NZ), same, 0, 0, tiled=True)  18.5 us
    all_to_all x1, blocking collectives, on_device(): lax.all_to_all(share.reshape(CHIPS, 3, 4, NZ), same, 0, 0, tiled=True)  18.5 us
    all_to_all x1, blocking collectives, on_device(): lax.all_to_all(send.reshape(TARGETS, BACK, 1, NZ), ('y', 'x', 'core'), 0,...  18 us
    pallas_call x10, Pallas kernels, call(): pl.pallas_call(body, out_shape=[(pltpu.HBM if home else pltpu.VMEM)(*o[:2...  17.1 us
    all_to_all x1, waiting for transfers between devices, on_device(): lax.all_to_all(bundle.reshape(BRICKS, CHUNK, 1, NZ), DEV, 0, 0, tiled=True)  14 us
    ppermute x1, starting transfers between devices, on_device(): blocks = lax.ppermute(blocks.reshape(3, SB, NK), ALL, across)  8.66 us
    ppermute x1, waiting for transfers between devices, on_device(): up = lax.ppermute(last, ALL, ahead)  7.49 us
  transfers between devices with their start and end apart: 11, of which 9 were waited for; matrix products, arithmetic and copies ran while one was open for 0% of the time, Pallas kernels for 4%

profile of v5, /device:TPU:1, one launch (start us, length us, event | category | flops | bytes accessed | tf_op | source)
XLA Modules:
  0.0 151.8 jit_solution(7714353329358054745)
XLA Ops:
  0.0 1.0 shard_map.163
  1.0 8.7 %collective-permute-start = (f32[3,256,128]{2,1,0:T(8,128)S(1)}, f32[3,256,128]{2,1,0:T(8,128)S(1)}, u32[]{:S(2)}, u32[]{:S(2)}) collective-permute-start(f32[3,256,128]{2,1,0:T(8,128)S(1)} %bitcast.31), channel_id=1, source_target_pairs={{0,128},{1,129},{2,130},{3,131},{4,132},{5,133},{6,134},{7,135},{8... | collective-permute-start | bytes 1179656 | tf_op jit(solution)/shard_map/ppermute | solution.py:564
  9.8 2.1 %shard_map.165 = (bf16[512,256]{1,0:T(8,128)(2,1)S(1)}, f32[128,128]{1,0:T(8,128)S(1)}, bf16[256,256]{1,0:T(8,128)(2,1)S(1)}) custom-call(s32[4]{0:T(128)S(1)} %pad_add_fusion.flags, s32[1,256]{1,0:T(1,128)} %bitcast.38, s32[1,256]{1,0:T(1,128)} %bitcast.39, f32[128,128]{1,0:T(8,128)} %refs_3_.4, f32[128,128]{1,0:T(8,128)} %constant.43.clone.refs_3_), custom_call_target="tpu_custom_call" | custom-call | tf_op jit(solution)/shard_map/pallas_call | solution.py:508
  11.9 3.5 %shard_map.164 = (f32[3,1024,128]{2,1,0:T(8,128)S(1)}, bf16[512,1024]{1,0:T(8,128)(2,1)}, f32[32,128]{1,0:T(8,128)}, f32[896,128]{1,0:T(8,128)}, f32[896,128]{1,0:T(8,128)}) custom-call(s32[4]{0:T(128)S(1)} %pad_add_fusion.flags, f32[3,1024,128]{2,1,0:T(8,128)} %bitcast.33, f32[1024,128]{1,0:T(8,128)} %bitcast.35, ...), custom_call_target="tpu_custom_call" | custom-call | tf_op jit(solution)/shard_map/pallas_call | solution.py:508
  15.4 2.0 %collective-permute-done.refs_0_ = f32[3,256,128]{2,1,0:T(8,128)S(1)} collective-permute-done((f32[3,256,128]{2,1,0:T(8,128)S(1)}, f32[3,256,128]{2,1,0:T(8,128)S(1)}, u32[]{:S(2)}, u32[]{:S(2)}) %collective-permute-start) | collective-permute-done | bytes 393248 | tf_op jit(solution)/shard_map/ppermute | solution.py:564
  17.4 1.5 shard_map.166
  18.9 19.1 %all-to-all-start = ((f32[128,13,1,128]{3,2,1,0:T(1,128)}), f32[128,13,1,128]{3,2,1,0:T(1,128)S(1)}, u32[]{:S(2)}, u32[]{:S(2)}) async-start(f32[128,13,1,128]{3,2,1,0:T(1,128)} %bitcast.13), calls=%async_computation | async-start | bytes 1703936 | tf_op jit(solution)/shard_map/all_to_all | solution.py:602
  38.1 3.5 %collective-permute-start.1 = (f32[896,128]{1,0:T(8,128)}, f32[896,128]{1,0:T(8,128)S(1)}, u32[]{:S(2)}, u32[]{:S(2)}) collective-permute-start(f32[896,128]{1,0:T(8,128)} %get-tuple-element.42), channel_id=1, source_target_pairs={{0,1},{1,2},{2,3},{3,4},{4,5},{5,6},{6,7},{7,8},{8,9},{9,10},{10,1... | collective-permute-start | bytes 1376264 | tf_op jit(solution)/shard_map/ppermute | solution.py:604
  41.6 1.9 %collective-permute-start.2 = (f32[896,128]{1,0:T(8,128)}, f32[896,128]{1,0:T(8,128)}, u32[]{:S(2)}, u32[]{:S(2)}) collective-permute-start(f32[896,128]{1,0:T(8,128)} %get-tuple-element.43), channel_id=1, source_target_pairs={{1,0},{2,1},{3,2},{4,3},{5,4},{6,5},{7,6},{8,7},{9,8},{10,9},{11,1... | collective-permute-start | bytes 1376264 | tf_op jit(solution)/shard_map/ppermute | solution.py:605
  43.5 7.5 %collective-permute-done.1.refs_13_ = f32[896,128]{1,0:T(8,128)S(1)} collective-permute-done((f32[896,128]{1,0:T(8,128)}, f32[896,128]{1,0:T(8,128)S(1)}, u32[]{:S(2)}, u32[]{:S(2)}) %collective-permute-start.1) | collective-permute-done | bytes 458784 | tf_op jit(solution)/shard_map/ppermute | solution.py:604
  51.0 3.4 %collective-permute-done.2.refs_14_ = f32[896,128]{1,0:T(8,128)} collective-permute-done((f32[896,128]{1,0:T(8,128)}, f32[896,128]{1,0:T(8,128)}, u32[]{:S(2)}, u32[]{:S(2)}) %collective-permute-start.2) | collective-permute-done | bytes 458784 | tf_op jit(solution)/shard_map/ppermute | solution.py:605
  54.4 14.0 %all-to-all-done = f32[128,13,1,128]{3,2,1,0:T(1,128)S(1)} async-done(((f32[128,13,1,128]{3,2,1,0:T(1,128)}), f32[128,13,1,128]{3,2,1,0:T(1,128)S(1)}, u32[]{:S(2)}, u32[]{:S(2)}) %all-to-all-start) | async-done | bytes 852000 | tf_op jit(solution)/shard_map/all_to_all | solution.py:602
  68.4 0.6 shard_map.167
  69.0 1.3 collective-permute-start.3
  70.3 1.3 collective-permute-done.3.refs_0_
  71.7 0.5 shard_map.168
  72.3 18.5 %all_to_all.20 = f32[64,3,4,128]{3,2,1,0:T(4,128)S(1)} all-to-all(f32[64,3,4,128]{3,2,1,0:T(4,128)S(1)} %bitcast.30), channel_id=1, replica_groups=mesh['grp'=2,'y'=4,'z'=4,'x'=4,'core'=2] {'y','z','x'}, dimensions={0} | all-to-all | bytes 786432 | tf_op jit(solution)/shard_map/all_to_all | solution.py:629
  90.8 0.6 shard_map.169
  91.4 18.5 %all_to_all.21 = f32[64,3,4,128]{3,2,1,0:T(4,128)S(1)} all-to-all(f32[64,3,4,128]{3,2,1,0:T(4,128)S(1)} %bitcast.26), channel_id=1, replica_groups=mesh['grp'=2,'y'=4,'z'=4,'x'=4,'core'=2] {'y','z','x'}, dimensions={0} | all-to-all | bytes 786432 | tf_op jit(solution)/shard_map/all_to_all | solution.py:641
  110.0 3.0 %collective-permute-start.5 = (f32[768,128]{1,0:T(8,128)S(1)}, f32[768,128]{1,0:T(8,128)S(1)}, u32[]{:S(2)}, u32[]{:S(2)}) collective-permute-start(f32[768,128]{1,0:T(8,128)S(1)} %bitcast.27), channel_id=1, source_target_pairs={{0,1},{1,0},{2,3},{3,2},{4,5},{5,4},{6,7},{7,6},{8,9},{9,8},{10,11... | collective-permute-start | bytes 1179656 | tf_op jit(solution)/shard_map/ppermute | solution.py:643
  113.0 1.6 %collective-permute-done.4.refs_2_ = f32[384,128]{1,0:T(8,128)S(1)} collective-permute-done((f32[384,128]{1,0:T(8,128)S(1)}, f32[384,128]{1,0:T(8,128)S(1)}, u32[]{:S(2)}, u32[]{:S(2)}) %collective-permute-start.4) | collective-permute-done | bytes 196640 | tf_op jit(solution)/shard_map/ppermute | solution.py:628
  114.6 5.4 %shard_map.170 = (f32[1568,128]{1,0:T(8,128)S(1)}, f32[3,1024,128]{2,1,0:T(8,128)}, f32[3,16,8,128]{3,2,1,0:T(8,128)}, f32[3,16,128]{2,1,0:T(8,128)}) custom-call(s32[4]{0:T(128)S(1)} %pad_add_fusion.flags, f32[3,4,256,128]{3,2,1,0:T(8,128)S(1)} %get-tuple-element.46.refs_0_, f32[384,128]{1,0:T(8,128)S(1)} %get-tuple-element.49.refs_1_, ...), custom_call_target="tpu_custom_call" | custom-call | tf_op jit(solution)/shard_map/pallas_call | solution.py:508
  120.0 18.0 %all_to_all.22 = f32[32,49,1,128]{3,2,1,0:T(1,128)S(1)} all-to-all(f32[32,49,1,128]{3,2,1,0:T(1,128)S(1)} %bitcast.29), channel_id=1, replica_groups=mesh['grp'=2,'y'=4,'z'=4,'x'=4,'core'=2] {'y','x','core'}, dimensions={0} | all-to-all | bytes 1605632 | tf_op jit(solution)/shard_map/all_to_all | solution.py:681
  138.0 0.5 shard_map.171
  138.5 1.3 collective-permute-start.6
  139.8 1.3 collective-permute-start.7
  141.1 1.3 collective-permute-start.8
  142.4 1.3 collective-permute-start.9
  143.7 3.3 %collective-permute-done.6.refs_4_ = f32[48,128]{1,0:T(8,128)S(1)} collective-permute-done((f32[48,128]{1,0:T(8,128)S(1)}, f32[48,128]{1,0:T(8,128)S(1)}, u32[]{:S(2)}, u32[]{:S(2)}) %collective-permute-start.6) | collective-permute-done | bytes 24608 | tf_op jit(solution)/shard_map/ppermute | solution.py:692
  147.0 1.3 collective-permute-done.8.refs_6_
  148.3 1.9 %collective-permute-done.9.refs_7_ = f32[48,128]{1,0:T(8,128)S(1)} collective-permute-done((f32[48,128]{1,0:T(8,128)S(1)}, f32[48,128]{1,0:T(8,128)S(1)}, u32[]{:S(2)}, u32[]{:S(2)}) %collective-permute-start.9) | collective-permute-done | bytes 24608 | tf_op jit(solution)/shard_map/ppermute | solution.py:692
  150.2 1.5 shard_map.172
  (32 shorter events, 0.2 us)
Async XLA Ops:
  1.0 16.4 %collective-permute-start = (f32[3,256,128]{2,1,0:T(8,128)S(1)}, f32[3,256,128]{2,1,0:T(8,128)S(1)}, u32[]{:S(2)}, u32[]{:S(2)}) collective-permute-start(f32[3,256,128]{2,1,0:T(8,128)S(1)} %bitcast.31), channel_id=1, source_target_pairs={{0,128},{1,129},{2,130},{3,131},{4,132},{5,133},{6,134},{7,135},{8... | collective-permute-start | bytes 1179656 | tf_op jit(solution)/shard_map/ppermute | solution.py:564
  17.4 50.9 %copy-start = (f32[256,128]{1,0:T(8,128)S(1)}, f32[256,128]{1,0:T(8,128)}, u32[]{:S(2)}) copy-start(f32[256,128]{1,0:T(8,128)} %constant.47.clone.refs_4_.refs_2_.refs_5_.refs_10_) | copy-start | bytes 393220
  17.4 50.9 %copy-start.2 = (bf16[256,256]{1,0:T(8,128)(2,1)S(1)}, bf16[256,256]{1,0:T(8,128)(2,1)}, u32[]{:S(2)}) copy-start(bf16[256,256]{1,0:T(8,128)(2,1)} %constant.46.clone.refs_3_.refs_9_) | copy-start | bytes 393220
  17.4 50.9 %copy-start.3 = (bf16[256,256]{1,0:T(8,128)(2,1)S(1)}, bf16[256,256]{1,0:T(8,128)(2,1)}, u32[]{:S(2)}) copy-start(bf16[256,256]{1,0:T(8,128)(2,1)} %constant.45.clone.refs_2_.refs_8_) | copy-start | bytes 393220
  18.9 49.5 %all-to-all-start = ((f32[128,13,1,128]{3,2,1,0:T(1,128)}), f32[128,13,1,128]{3,2,1,0:T(1,128)S(1)}, u32[]{:S(2)}, u32[]{:S(2)}) async-start(f32[128,13,1,128]{3,2,1,0:T(1,128)} %bitcast.13), calls=%async_computation | async-start | bytes 1703936 | tf_op jit(solution)/shard_map/all_to_all | solution.py:602
  38.1 13.0 %collective-permute-start.1 = (f32[896,128]{1,0:T(8,128)}, f32[896,128]{1,0:T(8,128)S(1)}, u32[]{:S(2)}, u32[]{:S(2)}) collective-permute-start(f32[896,128]{1,0:T(8,128)} %get-tuple-element.42), channel_id=1, source_target_pairs={{0,1},{1,2},{2,3},{3,4},{4,5},{5,6},{6,7},{7,8},{8,9},{9,10},{10,1... | collective-permute-start | bytes 1376264 | tf_op jit(solution)/shard_map/ppermute | solution.py:604
  41.6 12.8 %collective-permute-start.2 = (f32[896,128]{1,0:T(8,128)}, f32[896,128]{1,0:T(8,128)}, u32[]{:S(2)}, u32[]{:S(2)}) collective-permute-start(f32[896,128]{1,0:T(8,128)} %get-tuple-element.43), channel_id=1, source_target_pairs={{1,0},{2,1},{3,2},{4,3},{5,4},{6,5},{7,6},{8,7},{9,8},{10,9},{11,1... | collective-permute-start | bytes 1376264 | tf_op jit(solution)/shard_map/ppermute | solution.py:605
  51.0 21.2 %copy-start.13 = (f32[896,128]{1,0:T(8,128)}, f32[896,128]{1,0:T(8,128)S(1)}, u32[]{:S(2)}) copy-start(f32[896,128]{1,0:T(8,128)S(1)} %collective-permute-done.1.refs_13_) | copy-start | bytes 1376260
  68.4 22.4 %copy-start.5 = (f32[512,1]{1,0:T(8,128)S(1)}, f32[512,1]{1,0:T(8,128)}, u32[]{:S(2)}) copy-start(f32[512,1]{1,0:T(8,128)} %constant.51.clone.refs_4_) | copy-start | bytes 6148
  68.4 22.4 %copy-start.6 = (bf16[512,192]{1,0:T(8,128)(2,1)S(1)}, bf16[512,192]{1,0:T(8,128)(2,1)}, u32[]{:S(2)}) copy-start(bf16[512,192]{1,0:T(8,128)(2,1)} %constant.48.clone.refs_1_) | copy-start | bytes 589828
  68.4 22.4 %copy-start.9 = (bf16[64,512]{1,0:T(8,128)(2,1)S(1)}, bf16[64,512]{1,0:T(8,128)(2,1)}, u32[]{:S(2)}) copy-start(bf16[64,512]{1,0:T(8,128)(2,1)} %constant.50.clone.refs_3_) | copy-start | bytes 196612
  68.4 22.4 %copy-start.10 = (bf16[64,512]{1,0:T(8,128)(2,1)S(1)}, bf16[64,512]{1,0:T(8,128)(2,1)}, u32[]{:S(2)}) copy-start(bf16[64,512]{1,0:T(8,128)(2,1)} %constant.49.clone.refs_2_) | copy-start | bytes 196612
  69.0 2.7 %collective-permute-start.3 = (f32[768,128]{1,0:T(8,128)S(1)}, f32[768,128]{1,0:T(8,128)S(1)}, u32[]{:S(2)}, u32[]{:S(2)}) collective-permute-start(f32[768,128]{1,0:T(8,128)S(1)} %get-tuple-element.47), channel_id=1, source_target_pairs={{0,1},{1,0},{2,3},{3,2},{4,5},{5,4},{6,7},{7,6},{8,9},{9,8},{10,11... | collective-permute-start | bytes 1179656 | tf_op jit(solution)/shard_map/ppermute | solution.py:619
  72.3 42.4 %copy-start.1 = (bf16[512,1024]{1,0:T(8,128)(2,1)S(1)}, bf16[512,1024]{1,0:T(8,128)(2,1)}, u32[]{:S(2)}) copy-start(bf16[512,1024]{1,0:T(8,128)(2,1)} %get-tuple-element.51.refs_5_) | copy-start | bytes 3145732
  72.3 42.4 %copy-start.4 = (bf16[256,256]{1,0:T(8,128)(2,1)S(1)}, bf16[256,256]{1,0:T(8,128)(2,1)}, u32[]{:S(2)}) copy-start(bf16[256,256]{1,0:T(8,128)(2,1)} %constant.44.clone.refs_2_.refs_7_) | copy-start | bytes 393220
  72.3 42.4 %copy-start.12 = (f32[32,128]{1,0:T(8,128)S(1)}, f32[32,128]{1,0:T(8,128)}, u32[]{:S(2)}) copy-start(f32[32,128]{1,0:T(8,128)} %get-tuple-element.52.refs_6_) | copy-start | bytes 49156
  110.0 4.7 %collective-permute-start.5 = (f32[768,128]{1,0:T(8,128)S(1)}, f32[768,128]{1,0:T(8,128)S(1)}, u32[]{:S(2)}, u32[]{:S(2)}) collective-permute-start(f32[768,128]{1,0:T(8,128)S(1)} %bitcast.27), channel_id=1, source_target_pairs={{0,1},{1,0},{2,3},{3,2},{4,5},{5,4},{6,7},{7,6},{8,9},{9,8},{10,11... | collective-permute-start | bytes 1179656 | tf_op jit(solution)/shard_map/ppermute | solution.py:643
  113.0 1.6 %collective-permute-start.4 = (f32[384,128]{1,0:T(8,128)S(1)}, f32[384,128]{1,0:T(8,128)S(1)}, u32[]{:S(2)}, u32[]{:S(2)}) collective-permute-start(f32[384,128]{1,0:T(8,128)S(1)} %get-tuple-element.49.refs_1_), channel_id=1, source_target_pairs={{0,1},{1,0},{2,3},{3,2},{4,5},{5,4},{6,7},{7,6},{8,9},{9,8},{10,11... | collective-permute-start | bytes 589832 | tf_op jit(solution)/shard_map/ppermute | solution.py:628
  120.0 30.2 %copy-start.7 = (f32[128,128]{1,0:T(8,128)S(1)}, f32[128,128]{1,0:T(8,128)}, u32[]{:S(2)}) copy-start(f32[128,128]{1,0:T(8,128)} %refs_3_.4) | copy-start | bytes 196612
  120.0 30.2 %copy-start.8 = (f32[3,16,8,128]{3,2,1,0:T(8,128)S(1)}, f32[3,16,8,128]{3,2,1,0:T(8,128)}, u32[]{:S(2)}) copy-start(f32[3,16,8,128]{3,2,1,0:T(8,128)} %get-tuple-element.56.refs_1_) | copy-start | bytes 589828
  120.0 30.2 %copy-start.11 = (f32[3,16,128]{2,1,0:T(8,128)S(1)}, f32[3,16,128]{2,1,0:T(8,128)}, u32[]{:S(2)}) copy-start(f32[3,16,128]{2,1,0:T(8,128)} %get-tuple-element.57.refs_2_) | copy-start | bytes 73732
  138.5 8.5 %collective-permute-start.6 = (f32[48,128]{1,0:T(8,128)S(1)}, f32[48,128]{1,0:T(8,128)S(1)}, u32[]{:S(2)}, u32[]{:S(2)}) collective-permute-start(f32[48,128]{1,0:T(8,128)S(1)} %get-tuple-element.59), channel_id=1, source_target_pairs={{128,0},{129,1},{130,2},{131,3},{132,4},{133,5},{134,6},{135,7},{1... | collective-permute-start | bytes 73736 | tf_op jit(solution)/shard_map/ppermute | solution.py:692
  139.8 7.2 %collective-permute-start.7 = (f32[48,128]{1,0:T(8,128)S(1)}, f32[48,128]{1,0:T(8,128)S(1)}, u32[]{:S(2)}, u32[]{:S(2)}) collective-permute-start(f32[48,128]{1,0:T(8,128)S(1)} %get-tuple-element.60), channel_id=1, source_target_pairs={{128,8},{129,9},{130,10},{131,11},{132,12},{133,13},{134,14},{135,... | collective-permute-start | bytes 73736 | tf_op jit(solution)/shard_map/ppermute | solution.py:692
  141.1 7.2 %collective-permute-start.8 = (f32[48,128]{1,0:T(8,128)S(1)}, f32[48,128]{1,0:T(8,128)S(1)}, u32[]{:S(2)}, u32[]{:S(2)}) collective-permute-start(f32[48,128]{1,0:T(8,128)S(1)} %get-tuple-element.61), channel_id=1, source_target_pairs={{128,16},{129,17},{130,18},{131,19},{132,20},{133,21},{134,22},{13... | collective-permute-start | bytes 73736 | tf_op jit(solution)/shard_map/ppermute | solution.py:692
  142.4 7.7 %collective-permute-start.9 = (f32[48,128]{1,0:T(8,128)S(1)}, f32[48,128]{1,0:T(8,128)S(1)}, u32[]{:S(2)}, u32[]{:S(2)}) collective-permute-start(f32[48,128]{1,0:T(8,128)S(1)} %get-tuple-element.62), channel_id=1, source_target_pairs={{128,24},{129,25},{130,26},{131,27},{132,28},{133,29},{134,30},{13... | collective-permute-start | bytes 73736 | tf_op jit(solution)/shard_map/ppermute | solution.py:692

commit v6 on v5

--- a/solution.py
+++ b/solution.py
@@ -181,8 +181,8 @@
     return centre - speed * transport + viscosity * (above - 2.0 * centre + below)
 
 
-def shell_kernel(group, state, out, sem):
-    @pl.when(group[0] == 0)
+def shell_kernel(flags, state, out, sem):
+    @pl.when(flags[0] == 0)
     def _():
         copy = pltpu.make_async_copy(state.at[:, :, pl.ds(NI - NI // 4, NI // 4), :], out, sem)
         copy.start()
@@ -326,24 +326,26 @@
 ):
     @pl.when(flags[0] == 0)
     def _():
-        pairs = [(state_home, state), (speed_home, speed), (up_home, up), (down_home, down)]
-        copies = [pltpu.make_async_copy(a, b, sems.at[i]) for i, (a, b) in enumerate(pairs)]
-        for copy in copies:
+        pairs = [(speed_home, speed), (up_home, up), (down_home, down)]
+        pairs += [(state_home.at[c], state.at[c]) for c in range(3)]
+        loads = [pltpu.make_async_copy(a, b, sems.at[i]) for i, (a, b) in enumerate(pairs)]
+        for copy in loads:
             copy.start()
-        for copy in copies:
+        for copy in loads[:3]:
             copy.wait()
         wide = jnp.concatenate([up[768:896, :], speed[...], down[768:896, :]], axis=0)
         copies = []
         for c in range(3):
             block = slice(c * 256, (c + 1) * 256)
+            loads[3 + c].wait()
             field = jnp.concatenate([up[block, :], state[c], down[block, :]], axis=0)
             field = near_step(near_step(field, wide), speed[...])
             held[c] = field
-            copies.append(pltpu.make_async_copy(held.at[c], out.at[c], sems.at[c]))
+            copies.append(pltpu.make_async_copy(held.at[c], out.at[c], sems.at[6 + c]))
             copies[-1].start()
             edge[c] = field.reshape(NJ, NI, NK)[:, NI - 8 :, :]
             layer[c] = state[c, pl.ds(NI - 1, NJ, stride=NI), :]
-        for a, b, i in ((edge, edge_home, 3), (layer, layer_home, 4)):
+        for a, b, i in ((edge, edge_home, 9), (layer, layer_home, 10)):
             copies.append(pltpu.make_async_copy(a, b, sems.at[i]))
             copies[-1].start()
         for copy in copies:
@@ -478,7 +480,8 @@
     stores = [pltpu.VMEM(*outs[i][:2]) for i in staged]
     sems = [pltpu.SemaphoreType.DMA((len(loads) + len(stores),))] if loads or stores else []
 
-    def body(flags, *refs):
+    def body(*refs):
+        flags, refs = [ref[0] for ref in refs[:4]], refs[4:]
         given, made = list(refs[: len(args)]), list(refs[len(args) : len(args) + len(outs)])
         rest = refs[len(args) + len(outs) :]
         held, kept = rest[: len(loads)], rest[len(loads) : len(loads) + len(stores)]
@@ -508,16 +511,16 @@
     return pl.pallas_call(
         body,
         out_shape=[(pltpu.HBM if home else pltpu.VMEM)(*o[:2]) for o, home in zip(outs, homes)],
-        in_specs=[pl.BlockSpec(memory_space=pltpu.SMEM)]
+        in_specs=[pl.BlockSpec(memory_space=pltpu.SMEM)] * 4
         + [pl.BlockSpec(memory_space=space) for space in spaces],
         out_specs=[
             pl.BlockSpec(memory_space=pltpu.HBM if home else pltpu.VMEM) for home in homes
         ],
         scratch_shapes=loads + stores + sems + list(scratch),
-        input_output_aliases={1: 0} if alias else {},
+        input_output_aliases={4: 0} if alias else {},
         compiler_params=pltpu.CompilerParams(vmem_limit_bytes=24 << 20),
     )(
-        flags,
+        *flags,
         *[
             a if alias and i == 0 else pltpu.with_memory_space_constraint(a, space)
             for i, (a, space) in enumerate(zip(args, spaces))
@@ -537,9 +540,10 @@
 
 def on_device(state, courant, remesh, shell_dest, shell_row, return_dest, return_row, return_block):
     dev = lax.axis_index(DEV)
-    flags = jnp.stack(
-        [lax.axis_index("grp"), lax.axis_index("core"), dev, lax.axis_index("z")]
-    ).astype(i32)
+    flags = [
+        v.astype(i32).reshape(1)
+        for v in (lax.axis_index("grp"), lax.axis_index("core"), dev, lax.axis_index("z"))
+    ]
     field = state.reshape(3, RPB, NZ)
     speed = courant.reshape(RPB, NK)
     sy, sz, line = sines(NY), sines(NZ), line_table()
@@ -551,11 +555,10 @@
     lamx = eigen(NX).astype(np.float32)[:, None]
     mu = (eigen(NY)[:, None] + eigen(NZ)[None, :]).astype(np.float32)
 
-    group = lax.axis_index("grp").astype(i32).reshape(1)
     (blocks,) = call(
         shell_kernel,
         [((3, NJ, NI // 4, NK), f32)],
-        group,
+        flags,
         field.reshape(3, NJ, NI, NK),
         far=1,
         scratch=[pltpu.SemaphoreType.DMA],
@@ -675,7 +678,7 @@
             pltpu.VMEM((RPB, NK), f32),
             halo,
             halo,
-            pltpu.SemaphoreType.DMA((5,)),
+            pltpu.SemaphoreType.DMA((11,)),
         ],
     )
     returned = lax.all_to_all(
@@ -685,7 +688,7 @@
         cell_kernel, [((3 * NJ, NZ), f32)] * CZ, flags, returned.reshape(TARGETS * BACK, NZ)
     )
     parts = []
-    for k in range(CZ):
+    for k in (0, 1, 3, 2):
         pairs = [
             (place_of(1, y, z, x, c), place_of(0, y, (z + k) % CZ, x, c)) for y, z, x, c in chips()
         ]

time: 152 us -> 148 us (0.974)
  Pallas kernels: 17.1 us -> 12 us
    pallas_call x10, Pallas kernels: 17.1 us -> 12 us  [call(): pl.pallas_call(body, out_shape=[(pltpu.HBM if home else pltpu.VMEM)(*o[:2...]
  transfers between devices with their start and end apart: 11 -> 11, of which waited for: 9 -> 9; matrix products, arithmetic and copies ran while one was open for 0% -> 0% of each run, Pallas kernels for 4% -> 3%
where the time goes in v6:
time: 148 us; the launch traced here: 147 us
  blocking collectives  55 us (37%)
  starting transfers between devices  42.8 us (29%)
  waiting for transfers between devices  36.7 us (25%)
  Pallas kernels  12 us (8%)
    all_to_all x1, starting transfers between devices, on_device(): lax.all_to_all(bundle.reshape(BRICKS, CHUNK, 1, NZ), DEV, 0, 0, tiled=True)  19.1 us
    all_to_all x1, blocking collectives, on_device(): lax.all_to_all(solved.reshape(CHIPS, 3, 4, NZ), same, 0, 0, tiled=True)  18.5 us
    all_to_all x1, blocking collectives, on_device(): lax.all_to_all(share.reshape(CHIPS, 3, 4, NZ), same, 0, 0, tiled=True)  18.5 us
    all_to_all x1, blocking collectives, on_device(): lax.all_to_all(send.reshape(TARGETS, BACK, 1, NZ), ('y', 'x', 'core'), 0,...  18 us
    all_to_all x1, waiting for transfers between devices, on_device(): lax.all_to_all(bundle.reshape(BRICKS, CHUNK, 1, NZ), DEV, 0, 0, tiled=True)  14 us
    pallas_call x10, Pallas kernels, call(): pl.pallas_call(body, out_shape=[(pltpu.HBM if home else pltpu.VMEM)(*o[:2...  12 us
    ppermute x1, starting transfers between devices, on_device(): blocks = lax.ppermute(blocks.reshape(3, SB, NK), ALL, across)  8.66 us
    ppermute x1, waiting for transfers between devices, on_device(): up = lax.ppermute(last, ALL, ahead)  7.49 us
  transfers between devices with their start and end apart: 11, of which 9 were waited for; matrix products, arithmetic and copies ran while one was open for 0% of the time, Pallas kernels for 3%

profile of v6, /device:TPU:1, one launch (start us, length us, event | category | flops | bytes accessed | tf_op | source)
XLA Modules:
  0.0 146.9 jit_solution(3275031525151127610)
XLA Ops:
  0.0 1.0 shard_map.163
  1.0 8.7 %collective-permute-start = (f32[3,256,128]{2,1,0:T(8,128)S(1)}, f32[3,256,128]{2,1,0:T(8,128)S(1)}, u32[]{:S(2)}, u32[]{:S(2)}) collective-permute-start(f32[3,256,128]{2,1,0:T(8,128)S(1)} %bitcast.31), channel_id=1, source_target_pairs={{0,128},{1,129},{2,130},{3,131},{4,132},{5,133},{6,134},{7,135},{8... | collective-permute-start | bytes 1179656 | tf_op jit(solution)/shard_map/ppermute | solution.py:567
  9.7 1.6 %shard_map.165 = (bf16[512,256]{1,0:T(8,128)(2,1)S(1)}, f32[128,128]{1,0:T(8,128)S(1)}, bf16[256,256]{1,0:T(8,128)(2,1)S(1)}) custom-call(s32[1]{0:T(128)} %bitcast.refs_0_, s32[1]{0:T(128)} %bitcast.1.refs_1_, s32[1]{0:T(128)} %bitcast.2.refs_2_, s32[1]{0:T(128)} %bitcast.3.refs_3_, s32[1,256]{1,0:T(1,128)} %bitcast.38, s32[1,256]{1,0:T(1,128)} %bitcast.39, ...), custom_call_target="tpu_custom_call" | custom-call | tf_op jit(solution)/shard_map/pallas_call | solution.py:511
  11.3 3.0 %shard_map.164 = (f32[3,1024,128]{2,1,0:T(8,128)S(1)}, bf16[512,1024]{1,0:T(8,128)(2,1)}, f32[32,128]{1,0:T(8,128)}, f32[896,128]{1,0:T(8,128)}, f32[896,128]{1,0:T(8,128)}) custom-call(s32[1]{0:T(128)} %bitcast.refs_0_, s32[1]{0:T(128)} %bitcast.1.refs_1_, s32[1]{0:T(128)} %bitcast.2.refs_2_, s32[1]{0:T(128)} %bitcast.3.refs_3_, f32[3,1024,128]{2,1,0:T(8,128)} %bitcast.33, ...), custom_call_target="tpu_custom_call" | custom-call | tf_op jit(solution)/shard_map/pallas_call | solution.py:511
  14.2 3.2 %collective-permute-done.refs_4_ = f32[3,256,128]{2,1,0:T(8,128)S(1)} collective-permute-done((f32[3,256,128]{2,1,0:T(8,128)S(1)}, f32[3,256,128]{2,1,0:T(8,128)S(1)}, u32[]{:S(2)}, u32[]{:S(2)}) %collective-permute-start) | collective-permute-done | bytes 393248 | tf_op jit(solution)/shard_map/ppermute | solution.py:567
  17.4 0.9 shard_map.166
  18.4 19.1 %all-to-all-start = ((f32[128,13,1,128]{3,2,1,0:T(1,128)}), f32[128,13,1,128]{3,2,1,0:T(1,128)S(1)}, u32[]{:S(2)}, u32[]{:S(2)}) async-start(f32[128,13,1,128]{3,2,1,0:T(1,128)} %bitcast.13), calls=%async_computation | async-start | bytes 1703936 | tf_op jit(solution)/shard_map/all_to_all | solution.py:605
  37.5 3.5 %collective-permute-start.1 = (f32[896,128]{1,0:T(8,128)}, f32[896,128]{1,0:T(8,128)S(1)}, u32[]{:S(2)}, u32[]{:S(2)}) collective-permute-start(f32[896,128]{1,0:T(8,128)} %get-tuple-element.42), channel_id=1, source_target_pairs={{0,1},{1,2},{2,3},{3,4},{4,5},{5,6},{6,7},{7,8},{8,9},{9,10},{10,1... | collective-permute-start | bytes 1376264 | tf_op jit(solution)/shard_map/ppermute | solution.py:607
  41.1 1.9 %collective-permute-start.2 = (f32[896,128]{1,0:T(8,128)}, f32[896,128]{1,0:T(8,128)}, u32[]{:S(2)}, u32[]{:S(2)}) collective-permute-start(f32[896,128]{1,0:T(8,128)} %get-tuple-element.43), channel_id=1, source_target_pairs={{1,0},{2,1},{3,2},{4,3},{5,4},{6,5},{7,6},{8,7},{9,8},{10,9},{11,1... | collective-permute-start | bytes 1376264 | tf_op jit(solution)/shard_map/ppermute | solution.py:608
  43.0 7.5 %collective-permute-done.1.refs_17_ = f32[896,128]{1,0:T(8,128)S(1)} collective-permute-done((f32[896,128]{1,0:T(8,128)}, f32[896,128]{1,0:T(8,128)S(1)}, u32[]{:S(2)}, u32[]{:S(2)}) %collective-permute-start.1) | collective-permute-done | bytes 458784 | tf_op jit(solution)/shard_map/ppermute | solution.py:607
  50.5 3.4 %collective-permute-done.2.refs_18_ = f32[896,128]{1,0:T(8,128)} collective-permute-done((f32[896,128]{1,0:T(8,128)}, f32[896,128]{1,0:T(8,128)}, u32[]{:S(2)}, u32[]{:S(2)}) %collective-permute-start.2) | collective-permute-done | bytes 458784 | tf_op jit(solution)/shard_map/ppermute | solution.py:608
  53.8 14.0 %all-to-all-done = f32[128,13,1,128]{3,2,1,0:T(1,128)S(1)} async-done(((f32[128,13,1,128]{3,2,1,0:T(1,128)}), f32[128,13,1,128]{3,2,1,0:T(1,128)S(1)}, u32[]{:S(2)}, u32[]{:S(2)}) %all-to-all-start) | async-done | bytes 852000 | tf_op jit(solution)/shard_map/all_to_all | solution.py:605
  67.8 0.0 copy-start.6
  67.8 0.0 copy-start.7
  67.9 0.0 copy-start.9
  67.9 0.0 copy-start.10
  67.9 1.3 collective-permute-start.3
  69.3 1.3 collective-permute-done.3.refs_4_
  70.6 18.5 %all_to_all.20 = f32[64,3,4,128]{3,2,1,0:T(4,128)S(1)} all-to-all(f32[64,3,4,128]{3,2,1,0:T(4,128)S(1)} %bitcast.30), channel_id=1, replica_groups=mesh['grp'=2,'y'=4,'z'=4,'x'=4,'core'=2] {'y','z','x'}, dimensions={0} | all-to-all | bytes 786432 | tf_op jit(solution)/shard_map/all_to_all | solution.py:632
  89.2 18.5 %all_to_all.21 = f32[64,3,4,128]{3,2,1,0:T(4,128)S(1)} all-to-all(f32[64,3,4,128]{3,2,1,0:T(4,128)S(1)} %bitcast.26), channel_id=1, replica_groups=mesh['grp'=2,'y'=4,'z'=4,'x'=4,'core'=2] {'y','z','x'}, dimensions={0} | all-to-all | bytes 786432 | tf_op jit(solution)/shard_map/all_to_all | solution.py:644
  107.7 3.0 %collective-permute-start.5 = (f32[768,128]{1,0:T(8,128)S(1)}, f32[768,128]{1,0:T(8,128)S(1)}, u32[]{:S(2)}, u32[]{:S(2)}) collective-permute-start(f32[768,128]{1,0:T(8,128)S(1)} %bitcast.27), channel_id=1, source_target_pairs={{0,1},{1,0},{2,3},{3,2},{4,5},{5,4},{6,7},{7,6},{8,9},{9,8},{10,11... | collective-permute-start | bytes 1179656 | tf_op jit(solution)/shard_map/ppermute | solution.py:646
  110.8 1.6 %collective-permute-done.4.refs_6_ = f32[384,128]{1,0:T(8,128)S(1)} collective-permute-done((f32[384,128]{1,0:T(8,128)S(1)}, f32[384,128]{1,0:T(8,128)S(1)}, u32[]{:S(2)}, u32[]{:S(2)}) %collective-permute-start.4) | collective-permute-done | bytes 196640 | tf_op jit(solution)/shard_map/ppermute | solution.py:631
  112.4 4.6 %shard_map.170 = (f32[1568,128]{1,0:T(8,128)S(1)}, f32[3,1024,128]{2,1,0:T(8,128)}, f32[3,16,8,128]{3,2,1,0:T(8,128)}, f32[3,16,128]{2,1,0:T(8,128)}) custom-call(s32[1]{0:T(128)} %bitcast.refs_0_, s32[1]{0:T(128)} %bitcast.1.refs_1_, s32[1]{0:T(128)} %bitcast.2.refs_2_, s32[1]{0:T(128)} %bitcast.3.refs_3_, ...), custom_call_target="tpu_custom_call" | custom-call | tf_op jit(solution)/shard_map/pallas_call | solution.py:511
  117.0 18.0 %all_to_all.22 = f32[32,49,1,128]{3,2,1,0:T(1,128)S(1)} all-to-all(f32[32,49,1,128]{3,2,1,0:T(1,128)S(1)} %bitcast.29), channel_id=1, replica_groups=mesh['grp'=2,'y'=4,'z'=4,'x'=4,'core'=2] {'y','x','core'}, dimensions={0} | all-to-all | bytes 1605632 | tf_op jit(solution)/shard_map/all_to_all | solution.py:684
  135.0 1.3 collective-permute-start.6
  136.3 1.3 collective-permute-start.7
  137.6 1.3 collective-permute-start.8
  138.9 1.3 collective-permute-start.9
  140.2 3.3 %collective-permute-done.6.refs_8_ = f32[48,128]{1,0:T(8,128)S(1)} collective-permute-done((f32[48,128]{1,0:T(8,128)S(1)}, f32[48,128]{1,0:T(8,128)S(1)}, u32[]{:S(2)}, u32[]{:S(2)}) %collective-permute-start.6) | collective-permute-done | bytes 24608 | tf_op jit(solution)/shard_map/ppermute | solution.py:695
  143.5 1.9 %collective-permute-done.8.refs_10_ = f32[48,128]{1,0:T(8,128)S(1)} collective-permute-done((f32[48,128]{1,0:T(8,128)S(1)}, f32[48,128]{1,0:T(8,128)S(1)}, u32[]{:S(2)}, u32[]{:S(2)}) %collective-permute-start.8) | collective-permute-done | bytes 24608 | tf_op jit(solution)/shard_map/ppermute | solution.py:695
  145.3 0.5 collective-permute-done.9.refs_11_
  145.8 0.9 shard_map.172
  (31 shorter events, 0.1 us)
Async XLA Ops:
  1.0 16.4 %collective-permute-start = (f32[3,256,128]{2,1,0:T(8,128)S(1)}, f32[3,256,128]{2,1,0:T(8,128)S(1)}, u32[]{:S(2)}, u32[]{:S(2)}) collective-permute-start(f32[3,256,128]{2,1,0:T(8,128)S(1)} %bitcast.31), channel_id=1, source_target_pairs={{0,128},{1,129},{2,130},{3,131},{4,132},{5,133},{6,134},{7,135},{8... | collective-permute-start | bytes 1179656 | tf_op jit(solution)/shard_map/ppermute | solution.py:567
  17.4 50.4 %copy-start = (f32[256,128]{1,0:T(8,128)S(1)}, f32[256,128]{1,0:T(8,128)}, u32[]{:S(2)}) copy-start(f32[256,128]{1,0:T(8,128)} %constant.47.clone.refs_8_.refs_6_.refs_9_.refs_14_) | copy-start | bytes 393220
  17.4 50.4 %copy-start.3 = (bf16[256,256]{1,0:T(8,128)(2,1)S(1)}, bf16[256,256]{1,0:T(8,128)(2,1)}, u32[]{:S(2)}) copy-start(bf16[256,256]{1,0:T(8,128)(2,1)} %constant.46.clone.refs_7_.refs_13_) | copy-start | bytes 393220
  17.4 50.4 %copy-start.4 = (bf16[256,256]{1,0:T(8,128)(2,1)S(1)}, bf16[256,256]{1,0:T(8,128)(2,1)}, u32[]{:S(2)}) copy-start(bf16[256,256]{1,0:T(8,128)(2,1)} %constant.45.clone.refs_6_.refs_12_) | copy-start | bytes 393220
  18.4 49.5 %all-to-all-start = ((f32[128,13,1,128]{3,2,1,0:T(1,128)}), f32[128,13,1,128]{3,2,1,0:T(1,128)S(1)}, u32[]{:S(2)}, u32[]{:S(2)}) async-start(f32[128,13,1,128]{3,2,1,0:T(1,128)} %bitcast.13), calls=%async_computation | async-start | bytes 1703936 | tf_op jit(solution)/shard_map/all_to_all | solution.py:605
  37.5 13.0 %collective-permute-start.1 = (f32[896,128]{1,0:T(8,128)}, f32[896,128]{1,0:T(8,128)S(1)}, u32[]{:S(2)}, u32[]{:S(2)}) collective-permute-start(f32[896,128]{1,0:T(8,128)} %get-tuple-element.42), channel_id=1, source_target_pairs={{0,1},{1,2},{2,3},{3,4},{4,5},{5,6},{6,7},{7,8},{8,9},{9,10},{10,1... | collective-permute-start | bytes 1376264 | tf_op jit(solution)/shard_map/ppermute | solution.py:607
  41.1 12.8 %collective-permute-start.2 = (f32[896,128]{1,0:T(8,128)}, f32[896,128]{1,0:T(8,128)}, u32[]{:S(2)}, u32[]{:S(2)}) collective-permute-start(f32[896,128]{1,0:T(8,128)} %get-tuple-element.43), channel_id=1, source_target_pairs={{1,0},{2,1},{3,2},{4,3},{5,4},{6,5},{7,6},{8,7},{9,8},{10,9},{11,1... | collective-permute-start | bytes 1376264 | tf_op jit(solution)/shard_map/ppermute | solution.py:608
  50.5 20.1 %copy-start.13 = (f32[896,128]{1,0:T(8,128)}, f32[896,128]{1,0:T(8,128)S(1)}, u32[]{:S(2)}) copy-start(f32[896,128]{1,0:T(8,128)S(1)} %collective-permute-done.1.refs_17_) | copy-start | bytes 1376260
  67.8 21.3 %copy-start.6 = (f32[512,1]{1,0:T(8,128)S(1)}, f32[512,1]{1,0:T(8,128)}, u32[]{:S(2)}) copy-start(f32[512,1]{1,0:T(8,128)} %constant.51.clone.refs_8_) | copy-start | bytes 6148
  67.8 21.3 %copy-start.7 = (bf16[512,192]{1,0:T(8,128)(2,1)S(1)}, bf16[512,192]{1,0:T(8,128)(2,1)}, u32[]{:S(2)}) copy-start(bf16[512,192]{1,0:T(8,128)(2,1)} %constant.48.clone.refs_5_) | copy-start | bytes 589828
  67.9 21.3 %copy-start.9 = (bf16[64,512]{1,0:T(8,128)(2,1)S(1)}, bf16[64,512]{1,0:T(8,128)(2,1)}, u32[]{:S(2)}) copy-start(bf16[64,512]{1,0:T(8,128)(2,1)} %constant.50.clone.refs_7_) | copy-start | bytes 196612
  67.9 21.3 %copy-start.10 = (bf16[64,512]{1,0:T(8,128)(2,1)S(1)}, bf16[64,512]{1,0:T(8,128)(2,1)}, u32[]{:S(2)}) copy-start(bf16[64,512]{1,0:T(8,128)(2,1)} %constant.49.clone.refs_6_) | copy-start | bytes 196612
  67.9 2.7 %collective-permute-start.3 = (f32[768,128]{1,0:T(8,128)S(1)}, f32[768,128]{1,0:T(8,128)S(1)}, u32[]{:S(2)}, u32[]{:S(2)}) collective-permute-start(f32[768,128]{1,0:T(8,128)S(1)} %get-tuple-element.47), channel_id=1, source_target_pairs={{0,1},{1,0},{2,3},{3,2},{4,5},{5,4},{6,7},{7,6},{8,9},{9,8},{10,11... | collective-permute-start | bytes 1179656 | tf_op jit(solution)/shard_map/ppermute | solution.py:622
  70.6 41.8 %copy-start.1 = (bf16[512,1024]{1,0:T(8,128)(2,1)S(1)}, bf16[512,1024]{1,0:T(8,128)(2,1)}, u32[]{:S(2)}) copy-start(bf16[512,1024]{1,0:T(8,128)(2,1)} %get-tuple-element.51.refs_9_) | copy-start | bytes 3145732
  70.6 41.8 %copy-start.2 = (bf16[256,256]{1,0:T(8,128)(2,1)S(1)}, bf16[256,256]{1,0:T(8,128)(2,1)}, u32[]{:S(2)}) copy-start(bf16[256,256]{1,0:T(8,128)(2,1)} %constant.44.clone.refs_6_.refs_11_) | copy-start | bytes 393220
  70.6 41.8 %copy-start.12 = (f32[32,128]{1,0:T(8,128)S(1)}, f32[32,128]{1,0:T(8,128)}, u32[]{:S(2)}) copy-start(f32[32,128]{1,0:T(8,128)} %get-tuple-element.52.refs_10_) | copy-start | bytes 49156
  107.7 4.7 %collective-permute-start.5 = (f32[768,128]{1,0:T(8,128)S(1)}, f32[768,128]{1,0:T(8,128)S(1)}, u32[]{:S(2)}, u32[]{:S(2)}) collective-permute-start(f32[768,128]{1,0:T(8,128)S(1)} %bitcast.27), channel_id=1, source_target_pairs={{0,1},{1,0},{2,3},{3,2},{4,5},{5,4},{6,7},{7,6},{8,9},{9,8},{10,11... | collective-permute-start | bytes 1179656 | tf_op jit(solution)/shard_map/ppermute | solution.py:646
  110.8 1.6 %collective-permute-start.4 = (f32[384,128]{1,0:T(8,128)S(1)}, f32[384,128]{1,0:T(8,128)S(1)}, u32[]{:S(2)}, u32[]{:S(2)}) collective-permute-start(f32[384,128]{1,0:T(8,128)S(1)} %get-tuple-element.49.refs_5_), channel_id=1, source_target_pairs={{0,1},{1,0},{2,3},{3,2},{4,5},{5,4},{6,7},{7,6},{8,9},{9,8},{10,11... | collective-permute-start | bytes 589832 | tf_op jit(solution)/shard_map/ppermute | solution.py:631
  117.0 28.8 %copy-start.5 = (f32[128,128]{1,0:T(8,128)S(1)}, f32[128,128]{1,0:T(8,128)}, u32[]{:S(2)}) copy-start(f32[128,128]{1,0:T(8,128)} %refs_7_.4) | copy-start | bytes 196612
  117.0 28.8 %copy-start.8 = (f32[3,16,8,128]{3,2,1,0:T(8,128)S(1)}, f32[3,16,8,128]{3,2,1,0:T(8,128)}, u32[]{:S(2)}) copy-start(f32[3,16,8,128]{3,2,1,0:T(8,128)} %get-tuple-element.56.refs_5_) | copy-start | bytes 589828
  117.0 28.8 %copy-start.11 = (f32[3,16,128]{2,1,0:T(8,128)S(1)}, f32[3,16,128]{2,1,0:T(8,128)}, u32[]{:S(2)}) copy-start(f32[3,16,128]{2,1,0:T(8,128)} %get-tuple-element.57.refs_6_) | copy-start | bytes 73732
  135.0 8.5 %collective-permute-start.6 = (f32[48,128]{1,0:T(8,128)S(1)}, f32[48,128]{1,0:T(8,128)S(1)}, u32[]{:S(2)}, u32[]{:S(2)}) collective-permute-start(f32[48,128]{1,0:T(8,128)S(1)} %get-tuple-element.59), channel_id=1, source_target_pairs={{128,0},{129,1},{130,2},{131,3},{132,4},{133,5},{134,6},{135,7},{1... | collective-permute-start | bytes 73736 | tf_op jit(solution)/shard_map/ppermute | solution.py:695
  136.3 7.2 %collective-permute-start.7 = (f32[48,128]{1,0:T(8,128)S(1)}, f32[48,128]{1,0:T(8,128)S(1)}, u32[]{:S(2)}, u32[]{:S(2)}) collective-permute-start(f32[48,128]{1,0:T(8,128)S(1)} %get-tuple-element.60), channel_id=1, source_target_pairs={{128,8},{129,9},{130,10},{131,11},{132,12},{133,13},{134,14},{135,... | collective-permute-start | bytes 73736 | tf_op jit(solution)/shard_map/ppermute | solution.py:695
  137.6 7.7 %collective-permute-start.8 = (f32[48,128]{1,0:T(8,128)S(1)}, f32[48,128]{1,0:T(8,128)S(1)}, u32[]{:S(2)}, u32[]{:S(2)}) collective-permute-start(f32[48,128]{1,0:T(8,128)S(1)} %get-tuple-element.61), channel_id=1, source_target_pairs={{128,24},{129,25},{130,26},{131,27},{132,28},{133,29},{134,30},{13... | collective-permute-start | bytes 73736 | tf_op jit(solution)/shard_map/ppermute | solution.py:695
  138.9 7.0 %collective-permute-start.9 = (f32[48,128]{1,0:T(8,128)S(1)}, f32[48,128]{1,0:T(8,128)S(1)}, u32[]{:S(2)}, u32[]{:S(2)}) collective-permute-start(f32[48,128]{1,0:T(8,128)S(1)} %get-tuple-element.62), channel_id=1, source_target_pairs={{128,16},{129,17},{130,18},{131,19},{132,20},{133,21},{134,22},{13... | collective-permute-start | bytes 73736 | tf_op jit(solution)/shard_map/ppermute | solution.py:695

commit v7 on v6

--- a/solution.py
+++ b/solution.py
@@ -140,7 +140,7 @@
 
 
 def ready_kernel(
-    flags, state, speed, sz, rd, rr, rb, out, gather, codes, last, lead
+    flags, state, speed, sz, rd, rr, rb, out, gather, spots, codes, last, lead
 ):
     @pl.when(flags[0] == 0)
     def _():
@@ -156,12 +156,8 @@
             out[c] = times_paired(state[c], sz[...])
         y, z, x, core, lane = owners(rd[...])
         target = (y * CX + x) * CC + core
-        gather[...] = lax.dot_general(
-            onehot(iota((SLOTS, SB), 0) == lane * TARGETS + target),
-            onehot(iota((RPB, SB), 0) == rr[...]),
-            NT,
-            preferred_element_type=f32,
-        ).astype(bf16)
+        spots[...] = onehot(iota((SLOTS, SB), 0) == lane * TARGETS + target)
+        gather[...] = jnp.where(iota((RPB, SB), 0) == rr[...], 1.0, 0.0).T.astype(bf16)
         code = ((z - flags[3]) & (CZ - 1)) * NJ + rb[...] + 1
         tagged = jnp.where(iota((NZ, SB), 0) == lane, code.astype(f32), 0.0)
         sent = onehot(iota((TARGETS, SB), 0) == target)
@@ -189,17 +185,26 @@
         copy.wait()
 
 
-def bucket_kernel(flags, blocks, codes, place, merged, out):
+def bucket_kernel(flags, blocks, codes, place, merged, out, held, sems):
     @pl.when(flags[0] != 0)
     def _():
-        out[pl.ds(3 * CAP, BRICKS, stride=CHUNK), :] = codes[...]
-        for c in range(3):
-            moved = times_paired(blocks[c], merged[...])
-            slots = pick(place[...], moved)
-            for rank in range(CAP):
-                out[pl.ds(c * CAP + rank, BRICKS, stride=CHUNK), :] = slots[
-                    rank * BRICKS : (rank + 1) * BRICKS
-                ]
+        slots = [pick(place[...], times_paired(blocks[c], merged[...])) for c in range(3)]
+        part = BRICKS // 4
+        copies = []
+        for i in range(4):
+            first = i * part * CHUNK
+            held[pl.ds(first + 3 * CAP, part, stride=CHUNK), :] = codes[i * part : (i + 1) * part]
+            for c in range(3):
+                for rank in range(CAP):
+                    row = rank * BRICKS + i * part
+                    held[pl.ds(first + c * CAP + rank, part, stride=CHUNK), :] = slots[c][
+                        row : row + part
+                    ]
+            block = pl.ds(first, part * CHUNK)
+            copies.append(pltpu.make_async_copy(held.at[block, :], out.at[block, :], sems.at[i]))
+            copies[-1].start()
+        for copy in copies:
+            copy.wait()
 
 
 def weights(beta):
@@ -302,15 +307,16 @@
     own,
     other,
     gather,
+    spots,
     codes,
     sz,
     syh,
     syl,
     mu,
-    state_home,
-    speed_home,
-    up_home,
-    down_home,
+    state,
+    speed,
+    up,
+    down,
     send,
     out,
     edge_home,
@@ -318,26 +324,14 @@
     held,
     edge,
     layer,
-    state,
-    speed,
-    up,
-    down,
     sems,
 ):
     @pl.when(flags[0] == 0)
     def _():
-        pairs = [(speed_home, speed), (up_home, up), (down_home, down)]
-        pairs += [(state_home.at[c], state.at[c]) for c in range(3)]
-        loads = [pltpu.make_async_copy(a, b, sems.at[i]) for i, (a, b) in enumerate(pairs)]
-        for copy in loads:
-            copy.start()
-        for copy in loads[:3]:
-            copy.wait()
         wide = jnp.concatenate([up[768:896, :], speed[...], down[768:896, :]], axis=0)
         copies = []
         for c in range(3):
             block = slice(c * 256, (c + 1) * 256)
-            loads[3 + c].wait()
             field = jnp.concatenate([up[block, :], state[c], down[block, :]], axis=0)
             field = near_step(near_step(field, wide), speed[...])
             held[c] = field
@@ -422,7 +416,7 @@
             copies[-1].start()
         send[pl.ds(3 * GROUP, TARGETS, stride=BACK), :] = codes[...]
         for c in range(3):
-            rows_out = pick(gather[...], velocity[c])
+            rows_out = pick(spots[...], pick(gather[...], velocity[c]))
             for lane in range(GROUP):
                 send[pl.ds(c * GROUP + lane, TARGETS, stride=BACK), :] = rows_out[
                     lane * TARGETS : (lane + 1) * TARGETS
@@ -579,11 +573,12 @@
         sz.astype(np.float32),
         fetch=True,
     )
-    turned, gather, codes, last, lead = call(
+    turned, gather, spots, codes, last, lead = call(
         ready_kernel,
         [
             ((3, RPB, NZ), f32),
-            ((SLOTS, RPB), bf16, "home"),
+            ((SB, RPB), bf16, "home"),
+        ((SLOTS, SB), bf16, "home"),
             ((TARGETS, NZ), f32, "home"),
             ((896, NK), f32, "home"),
             ((896, NK), f32, "home"),
@@ -599,7 +594,14 @@
     )
     blocks, turned = lax.optimization_barrier((blocks, turned))
     (bundle,) = call(
-        bucket_kernel, [((BRICKS * CHUNK, NZ), f32)], flags, blocks, rows, place, merged
+        bucket_kernel,
+        [((BRICKS * CHUNK, NZ), f32, "raw")],
+        flags,
+        blocks,
+        rows,
+        place,
+        merged,
+        scratch=[pltpu.VMEM((BRICKS * CHUNK, NZ), f32), pltpu.SemaphoreType.DMA((4,))],
     )
     bundle, last, lead = lax.optimization_barrier((bundle, last, lead))
     bundle = lax.all_to_all(bundle.reshape(BRICKS, CHUNK, 1, NZ), DEV, 0, 0, tiled=True)
@@ -644,7 +646,6 @@
     own = lax.all_to_all(solved.reshape(CHIPS, 3, 4, NZ), same, 0, 0, tiled=True)
     own = own.reshape(CHIPS * 12, NZ)
     other = lax.ppermute(own, "core", swap)
-    halo = pltpu.VMEM((896, NK), f32)
     send, result, edge, layer = call(
         inverse_kernel,
         [
@@ -660,6 +661,7 @@
         own,
         other,
         gather,
+        spots,
         codes,
         szp,
         syh,
@@ -669,15 +671,10 @@
         speed,
         up,
         down,
-        far=4,
         scratch=[
             pltpu.VMEM((3, RPB, NZ), f32),
             pltpu.VMEM((3, NJ, 8, NK), f32),
             pltpu.VMEM((3, NJ, NK), f32),
-            pltpu.VMEM((3, RPB, NK), f32),
-            pltpu.VMEM((RPB, NK), f32),
-            halo,
-            halo,
             pltpu.SemaphoreType.DMA((11,)),
         ],
     )

time: 148 us -> 148 us (level)
  Pallas kernels: 12 us -> 9.57 us
  waiting for transfers between devices: 36.7 us -> 38.3 us
    pallas_call x10, Pallas kernels: 12 us -> 9.57 us  [call(): pl.pallas_call(body, out_shape=[(pltpu.HBM if home else pltpu.VMEM)(*o[:2...]
    ppermute x4, waiting for transfers between devices: 5.65 us -> 8.01 us  [on_device(): parts.append(lax.ppermute(sums[k], ALL, pairs))]
where the time goes in v7:
time: 148 us; the launch traced here: 147 us
  blocking collectives  55.2 us (37%)
  starting transfers between devices  42.9 us (29%)
  waiting for transfers between devices  38.3 us (26%)
  Pallas kernels  9.57 us (6%)
    all_to_all x1, starting transfers between devices, on_device(): lax.all_to_all(bundle.reshape(BRICKS, CHUNK, 1, NZ), DEV, 0, 0, tiled=True)  19.3 us
    all_to_all x1, blocking collectives, on_device(): lax.all_to_all(share.reshape(CHIPS, 3, 4, NZ), same, 0, 0, tiled=True)  18.7 us
    all_to_all x1, blocking collectives, on_device(): lax.all_to_all(solved.reshape(CHIPS, 3, 4, NZ), same, 0, 0, tiled=True)  18.5 us
    all_to_all x1, blocking collectives, on_device(): lax.all_to_all(send.reshape(TARGETS, BACK, 1, NZ), ('y', 'x', 'core'), 0,...  18 us
    all_to_all x1, waiting for transfers between devices, on_device(): lax.all_to_all(bundle.reshape(BRICKS, CHUNK, 1, NZ), DEV, 0, 0, tiled=True)  13.2 us
    pallas_call x10, Pallas kernels, call(): pl.pallas_call(body, out_shape=[(pltpu.HBM if home else pltpu.VMEM)(*o[:2...  9.57 us
    ppermute x1, starting transfers between devices, on_device(): blocks = lax.ppermute(blocks.reshape(3, SB, NK), ALL, across)  8.66 us
    ppermute x4, waiting for transfers between devices, on_device(): parts.append(lax.ppermute(sums[k], ALL, pairs))  8.01 us
  transfers between devices with their start and end apart: 11, of which 9 were waited for; matrix products, arithmetic and copies ran while one was open for 0% of the time, Pallas kernels for 3%

profile of v7, /device:TPU:1, one launch (start us, length us, event | category | flops | bytes accessed | tf_op | source)
XLA Modules:
  0.0 147.3 jit_solution(7951692082640741069)
XLA Ops:
  0.0 1.0 shard_map.163
  1.0 8.7 %collective-permute-start = (f32[3,256,128]{2,1,0:T(8,128)S(1)}, f32[3,256,128]{2,1,0:T(8,128)S(1)}, u32[]{:S(2)}, u32[]{:S(2)}) collective-permute-start(f32[3,256,128]{2,1,0:T(8,128)S(1)} %bitcast.36), channel_id=1, source_target_pairs={{0,128},{1,129},{2,130},{3,131},{4,132},{5,133},{6,134},{7,135},{8... | collective-permute-start | bytes 1179656 | tf_op jit(solution)/shard_map/ppermute | solution.py:561
  9.7 1.6 %shard_map.165 = (bf16[512,256]{1,0:T(8,128)(2,1)S(1)}, f32[128,128]{1,0:T(8,128)S(1)}, bf16[256,256]{1,0:T(8,128)(2,1)S(1)}) custom-call(s32[1]{0:T(128)} %bitcast.refs_0_, s32[1]{0:T(128)} %bitcast.1.refs_1_, s32[1]{0:T(128)} %bitcast.2.refs_2_, s32[1]{0:T(128)} %bitcast.3.refs_3_, s32[1,256]{1,0:T(1,128)} %bitcast.39, s32[1,256]{1,0:T(1,128)} %bitcast.40, ...), custom_call_target="tpu_custom_call" | custom-call | tf_op jit(solution)/shard_map/pallas_call | solution.py:505
  11.3 2.9 %shard_map.164 = (f32[3,1024,128]{2,1,0:T(8,128)S(1)}, bf16[256,1024]{1,0:T(8,128)(2,1)}, bf16[512,256]{1,0:T(8,128)(2,1)}, f32[32,128]{1,0:T(8,128)}, f32[896,128]{1,0:T(8,128)}, /*index=5*/f32[896,128]{1,0:T(8,128)}) custom-call(s32[1]{0:T(128)} %bitcast.refs_0_, s32[1]{0:T(128)} %bitcast.1.refs_1_, s32[1]{0:T(128)} %bitcast.2.refs_2_, s32[1]{0:T(128)} %bitcast.3.refs_3_, ...), custom_call_target="tpu_custom_call" | custom-call | tf_op jit(solution)/shard_map/pallas_call | solution.py:505
  14.2 3.2 %collective-permute-done.refs_4_ = f32[3,256,128]{2,1,0:T(8,128)S(1)} collective-permute-done((f32[3,256,128]{2,1,0:T(8,128)S(1)}, f32[3,256,128]{2,1,0:T(8,128)S(1)}, u32[]{:S(2)}, u32[]{:S(2)}) %collective-permute-start) | collective-permute-done | bytes 393248 | tf_op jit(solution)/shard_map/ppermute | solution.py:561
  17.5 19.3 %all-to-all-start = ((f32[128,13,1,128]{3,2,1,0:T(1,128)}), f32[128,13,1,128]{3,2,1,0:T(1,128)S(1)}, u32[]{:S(2)}, u32[]{:S(2)}) async-start(f32[128,13,1,128]{3,2,1,0:T(1,128)} %bitcast.37), calls=%async_computation | async-start | bytes 1703936 | tf_op jit(solution)/shard_map/all_to_all | solution.py:607
  36.8 3.5 %collective-permute-start.1 = (f32[896,128]{1,0:T(8,128)}, f32[896,128]{1,0:T(8,128)S(1)}, u32[]{:S(2)}, u32[]{:S(2)}) collective-permute-start(f32[896,128]{1,0:T(8,128)} %get-tuple-element.43), channel_id=1, source_target_pairs={{0,1},{1,2},{2,3},{3,4},{4,5},{5,6},{6,7},{7,8},{8,9},{9,10},{10,1... | collective-permute-start | bytes 1376264 | tf_op jit(solution)/shard_map/ppermute | solution.py:609
  40.3 1.9 %collective-permute-start.2 = (f32[896,128]{1,0:T(8,128)}, f32[896,128]{1,0:T(8,128)S(1)}, u32[]{:S(2)}, u32[]{:S(2)}) collective-permute-start(f32[896,128]{1,0:T(8,128)} %get-tuple-element.44), channel_id=1, source_target_pairs={{1,0},{2,1},{3,2},{4,3},{5,4},{6,5},{7,6},{8,7},{9,8},{10,9},{11,1... | collective-permute-start | bytes 1376264 | tf_op jit(solution)/shard_map/ppermute | solution.py:610
  42.2 7.5 %collective-permute-done.1.refs_18_ = f32[896,128]{1,0:T(8,128)S(1)} collective-permute-done((f32[896,128]{1,0:T(8,128)}, f32[896,128]{1,0:T(8,128)S(1)}, u32[]{:S(2)}, u32[]{:S(2)}) %collective-permute-start.1) | collective-permute-done | bytes 458784 | tf_op jit(solution)/shard_map/ppermute | solution.py:609
  49.7 3.4 %collective-permute-done.2.refs_19_ = f32[896,128]{1,0:T(8,128)S(1)} collective-permute-done((f32[896,128]{1,0:T(8,128)}, f32[896,128]{1,0:T(8,128)S(1)}, u32[]{:S(2)}, u32[]{:S(2)}) %collective-permute-start.2) | collective-permute-done | bytes 458784 | tf_op jit(solution)/shard_map/ppermute | solution.py:610
  53.1 0.8 copy-done.7
  53.9 13.2 %all-to-all-done = f32[128,13,1,128]{3,2,1,0:T(1,128)S(1)} async-done(((f32[128,13,1,128]{3,2,1,0:T(1,128)}), f32[128,13,1,128]{3,2,1,0:T(1,128)S(1)}, u32[]{:S(2)}, u32[]{:S(2)}) %all-to-all-start) | async-done | bytes 852000 | tf_op jit(solution)/shard_map/all_to_all | solution.py:607
  67.1 0.0 copy-start.10
  67.1 0.0 copy-start.11
  67.1 0.0 copy-start.14
  67.1 0.0 copy-start.15
  67.2 1.3 collective-permute-start.3
  68.5 1.3 collective-permute-done.3.refs_4_
  69.9 18.7 %all_to_all.20 = f32[64,3,4,128]{3,2,1,0:T(4,128)S(1)} all-to-all(f32[64,3,4,128]{3,2,1,0:T(4,128)S(1)} %bitcast.35), channel_id=1, replica_groups=mesh['grp'=2,'y'=4,'z'=4,'x'=4,'core'=2] {'y','z','x'}, dimensions={0} | all-to-all | bytes 786432 | tf_op jit(solution)/shard_map/all_to_all | solution.py:634
  88.6 18.5 %all_to_all.21 = f32[64,3,4,128]{3,2,1,0:T(4,128)S(1)} all-to-all(f32[64,3,4,128]{3,2,1,0:T(4,128)S(1)} %bitcast.31), channel_id=1, replica_groups=mesh['grp'=2,'y'=4,'z'=4,'x'=4,'core'=2] {'y','z','x'}, dimensions={0} | all-to-all | bytes 786432 | tf_op jit(solution)/shard_map/all_to_all | solution.py:646
  107.2 3.0 %collective-permute-start.5 = (f32[768,128]{1,0:T(8,128)S(1)}, f32[768,128]{1,0:T(8,128)S(1)}, u32[]{:S(2)}, u32[]{:S(2)}) collective-permute-start(f32[768,128]{1,0:T(8,128)S(1)} %bitcast.32), channel_id=1, source_target_pairs={{0,1},{1,0},{2,3},{3,2},{4,5},{5,4},{6,7},{7,6},{8,9},{9,8},{10,11... | collective-permute-start | bytes 1179656 | tf_op jit(solution)/shard_map/ppermute | solution.py:648
  110.2 1.6 %collective-permute-done.4.refs_6_ = f32[384,128]{1,0:T(8,128)S(1)} collective-permute-done((f32[384,128]{1,0:T(8,128)S(1)}, f32[384,128]{1,0:T(8,128)S(1)}, u32[]{:S(2)}, u32[]{:S(2)}) %collective-permute-start.4) | collective-permute-done | bytes 196640 | tf_op jit(solution)/shard_map/ppermute | solution.py:633
  111.9 3.1 %shard_map.170 = (f32[1568,128]{1,0:T(8,128)S(1)}, f32[3,1024,128]{2,1,0:T(8,128)}, f32[3,16,8,128]{3,2,1,0:T(8,128)}, f32[3,16,128]{2,1,0:T(8,128)}) custom-call(s32[1]{0:T(128)} %bitcast.refs_0_, s32[1]{0:T(128)} %bitcast.1.refs_1_, s32[1]{0:T(128)} %bitcast.2.refs_2_, s32[1]{0:T(128)} %bitcast.3.refs_3_, ...), custom_call_target="tpu_custom_call" | custom-call | tf_op jit(solution)/shard_map/pallas_call | solution.py:505
  115.0 18.0 %all_to_all.22 = f32[32,49,1,128]{3,2,1,0:T(1,128)S(1)} all-to-all(f32[32,49,1,128]{3,2,1,0:T(1,128)S(1)} %bitcast.34), channel_id=1, replica_groups=mesh['grp'=2,'y'=4,'z'=4,'x'=4,'core'=2] {'y','x','core'}, dimensions={0} | all-to-all | bytes 1605632 | tf_op jit(solution)/shard_map/all_to_all | solution.py:681
  133.0 1.3 collective-permute-start.6
  134.2 1.3 collective-permute-start.7
  135.5 1.3 collective-permute-start.8
  136.8 1.3 collective-permute-start.9
  138.1 5.6 %collective-permute-done.6.refs_8_ = f32[48,128]{1,0:T(8,128)S(1)} collective-permute-done((f32[48,128]{1,0:T(8,128)S(1)}, f32[48,128]{1,0:T(8,128)S(1)}, u32[]{:S(2)}, u32[]{:S(2)}) %collective-permute-start.6) | collective-permute-done | bytes 24608 | tf_op jit(solution)/shard_map/ppermute | solution.py:692
  143.8 1.9 %collective-permute-done.8.refs_10_ = f32[48,128]{1,0:T(8,128)S(1)} collective-permute-done((f32[48,128]{1,0:T(8,128)S(1)}, f32[48,128]{1,0:T(8,128)S(1)}, u32[]{:S(2)}, u32[]{:S(2)}) %collective-permute-start.8) | collective-permute-done | bytes 24608 | tf_op jit(solution)/shard_map/ppermute | solution.py:692
  145.6 0.5 collective-permute-done.9.refs_11_
  146.2 0.9 shard_map.172
  (39 shorter events, 0.1 us)
Async XLA Ops:
  1.0 16.4 %collective-permute-start = (f32[3,256,128]{2,1,0:T(8,128)S(1)}, f32[3,256,128]{2,1,0:T(8,128)S(1)}, u32[]{:S(2)}, u32[]{:S(2)}) collective-permute-start(f32[3,256,128]{2,1,0:T(8,128)S(1)} %bitcast.36), channel_id=1, source_target_pairs={{0,128},{1,129},{2,130},{3,131},{4,132},{5,133},{6,134},{7,135},{8... | collective-permute-start | bytes 1179656 | tf_op jit(solution)/shard_map/ppermute | solution.py:561
  17.4 49.7 %copy-start.2 = (f32[256,128]{1,0:T(8,128)S(1)}, f32[256,128]{1,0:T(8,128)}, u32[]{:S(2)}) copy-start(f32[256,128]{1,0:T(8,128)} %constant.47.clone.refs_8_.refs_6_.refs_9_.refs_15_) | copy-start | bytes 393220
  17.4 49.7 %copy-start.5 = (bf16[256,256]{1,0:T(8,128)(2,1)S(1)}, bf16[256,256]{1,0:T(8,128)(2,1)}, u32[]{:S(2)}) copy-start(bf16[256,256]{1,0:T(8,128)(2,1)} %constant.46.clone.refs_7_.refs_14_) | copy-start | bytes 393220
  17.4 49.7 %copy-start.6 = (bf16[256,256]{1,0:T(8,128)(2,1)S(1)}, bf16[256,256]{1,0:T(8,128)(2,1)}, u32[]{:S(2)}) copy-start(bf16[256,256]{1,0:T(8,128)(2,1)} %constant.45.clone.refs_6_.refs_13_) | copy-start | bytes 393220
  17.5 49.6 %all-to-all-start = ((f32[128,13,1,128]{3,2,1,0:T(1,128)}), f32[128,13,1,128]{3,2,1,0:T(1,128)S(1)}, u32[]{:S(2)}, u32[]{:S(2)}) async-start(f32[128,13,1,128]{3,2,1,0:T(1,128)} %bitcast.37), calls=%async_computation | async-start | bytes 1703936 | tf_op jit(solution)/shard_map/all_to_all | solution.py:607
  36.8 13.0 %collective-permute-start.1 = (f32[896,128]{1,0:T(8,128)}, f32[896,128]{1,0:T(8,128)S(1)}, u32[]{:S(2)}, u32[]{:S(2)}) collective-permute-start(f32[896,128]{1,0:T(8,128)} %get-tuple-element.43), channel_id=1, source_target_pairs={{0,1},{1,2},{2,3},{3,4},{4,5},{5,6},{6,7},{7,8},{8,9},{9,10},{10,1... | collective-permute-start | bytes 1376264 | tf_op jit(solution)/shard_map/ppermute | solution.py:609
  40.3 12.8 %collective-permute-start.2 = (f32[896,128]{1,0:T(8,128)}, f32[896,128]{1,0:T(8,128)S(1)}, u32[]{:S(2)}, u32[]{:S(2)}) collective-permute-start(f32[896,128]{1,0:T(8,128)} %get-tuple-element.44), channel_id=1, source_target_pairs={{1,0},{2,1},{3,2},{4,3},{5,4},{6,5},{7,6},{8,7},{9,8},{10,9},{11,1... | collective-permute-start | bytes 1376264 | tf_op jit(solution)/shard_map/ppermute | solution.py:610
  53.1 0.8 copy-start.7
  67.1 21.5 %copy-start.10 = (f32[512,1]{1,0:T(8,128)S(1)}, f32[512,1]{1,0:T(8,128)}, u32[]{:S(2)}) copy-start(f32[512,1]{1,0:T(8,128)} %constant.51.clone.refs_8_) | copy-start | bytes 6148
  67.1 21.5 %copy-start.11 = (bf16[512,192]{1,0:T(8,128)(2,1)S(1)}, bf16[512,192]{1,0:T(8,128)(2,1)}, u32[]{:S(2)}) copy-start(bf16[512,192]{1,0:T(8,128)(2,1)} %constant.48.clone.refs_5_) | copy-start | bytes 589828
  67.1 21.5 %copy-start.14 = (bf16[64,512]{1,0:T(8,128)(2,1)S(1)}, bf16[64,512]{1,0:T(8,128)(2,1)}, u32[]{:S(2)}) copy-start(bf16[64,512]{1,0:T(8,128)(2,1)} %constant.50.clone.refs_7_) | copy-start | bytes 196612
  67.1 21.5 %copy-start.15 = (bf16[64,512]{1,0:T(8,128)(2,1)S(1)}, bf16[64,512]{1,0:T(8,128)(2,1)}, u32[]{:S(2)}) copy-start(bf16[64,512]{1,0:T(8,128)(2,1)} %constant.49.clone.refs_6_) | copy-start | bytes 196612
  67.2 2.7 %collective-permute-start.3 = (f32[768,128]{1,0:T(8,128)S(1)}, f32[768,128]{1,0:T(8,128)S(1)}, u32[]{:S(2)}, u32[]{:S(2)}) collective-permute-start(f32[768,128]{1,0:T(8,128)S(1)} %get-tuple-element.48), channel_id=1, source_target_pairs={{0,1},{1,0},{2,3},{3,2},{4,5},{5,4},{6,7},{7,6},{8,9},{9,8},{10,11... | collective-permute-start | bytes 1179656 | tf_op jit(solution)/shard_map/ppermute | solution.py:624
  69.9 42.0 %copy-start.8 = (f32[896,128]{1,0:T(8,128)S(1)}, f32[896,128]{1,0:T(8,128)}, u32[]{:S(2)}) copy-start(f32[896,128]{1,0:T(8,128)} %copy-done.7) | copy-start | bytes 1376260
  69.9 42.0 %copy-start = (f32[1,3,131072]{2,0,1:T(1,128)S(1)}, f32[1,3,131072]{2,0,1:T(1,128)}, u32[]{:S(2)}) copy-start(f32[1,3,131072]{2,0,1:T(1,128)} %param.17) | copy-start | bytes 4718596
  69.9 42.0 %copy-start.1 = (f32[131072]{0:T(1024)S(1)}, f32[131072]{0:T(1024)}, u32[]{:S(2)}) copy-start(f32[131072]{0:T(1024)} %param.18) | copy-start | bytes 1572868
  69.9 42.0 %copy-start.3 = (bf16[256,1024]{1,0:T(8,128)(2,1)S(1)}, bf16[256,1024]{1,0:T(8,128)(2,1)}, u32[]{:S(2)}) copy-start(bf16[256,1024]{1,0:T(8,128)(2,1)} %get-tuple-element.52.refs_9_) | copy-start | bytes 1572868
  69.9 42.0 %copy-start.4 = (bf16[256,256]{1,0:T(8,128)(2,1)S(1)}, bf16[256,256]{1,0:T(8,128)(2,1)}, u32[]{:S(2)}) copy-start(bf16[256,256]{1,0:T(8,128)(2,1)} %constant.44.clone.refs_6_.refs_12_) | copy-start | bytes 393220
  69.9 42.0 %copy-start.12 = (bf16[512,256]{1,0:T(8,128)(2,1)S(1)}, bf16[512,256]{1,0:T(8,128)(2,1)}, u32[]{:S(2)}) copy-start(bf16[512,256]{1,0:T(8,128)(2,1)} %get-tuple-element.53.refs_10_) | copy-start | bytes 786436
  69.9 42.0 %copy-start.17 = (f32[32,128]{1,0:T(8,128)S(1)}, f32[32,128]{1,0:T(8,128)}, u32[]{:S(2)}) copy-start(f32[32,128]{1,0:T(8,128)} %get-tuple-element.54.refs_11_) | copy-start | bytes 49156
  107.2 4.7 %collective-permute-start.5 = (f32[768,128]{1,0:T(8,128)S(1)}, f32[768,128]{1,0:T(8,128)S(1)}, u32[]{:S(2)}, u32[]{:S(2)}) collective-permute-start(f32[768,128]{1,0:T(8,128)S(1)} %bitcast.32), channel_id=1, source_target_pairs={{0,1},{1,0},{2,3},{3,2},{4,5},{5,4},{6,7},{7,6},{8,9},{9,8},{10,11... | collective-permute-start | bytes 1179656 | tf_op jit(solution)/shard_map/ppermute | solution.py:648
  110.2 1.6 %collective-permute-start.4 = (f32[384,128]{1,0:T(8,128)S(1)}, f32[384,128]{1,0:T(8,128)S(1)}, u32[]{:S(2)}, u32[]{:S(2)}) collective-permute-start(f32[384,128]{1,0:T(8,128)S(1)} %get-tuple-element.50.refs_5_), channel_id=1, source_target_pairs={{0,1},{1,0},{2,3},{3,2},{4,5},{5,4},{6,7},{7,6},{8,9},{9,8},{10,11... | collective-permute-start | bytes 589832 | tf_op jit(solution)/shard_map/ppermute | solution.py:633
  115.0 31.2 %copy-start.9 = (f32[128,128]{1,0:T(8,128)S(1)}, f32[128,128]{1,0:T(8,128)}, u32[]{:S(2)}) copy-start(f32[128,128]{1,0:T(8,128)} %refs_7_.4) | copy-start | bytes 196612
  115.0 31.2 %copy-start.13 = (f32[3,16,8,128]{3,2,1,0:T(8,128)S(1)}, f32[3,16,8,128]{3,2,1,0:T(8,128)}, u32[]{:S(2)}) copy-start(f32[3,16,8,128]{3,2,1,0:T(8,128)} %get-tuple-element.58.refs_5_) | copy-start | bytes 589828
  115.0 31.2 %copy-start.16 = (f32[3,16,128]{2,1,0:T(8,128)S(1)}, f32[3,16,128]{2,1,0:T(8,128)}, u32[]{:S(2)}) copy-start(f32[3,16,128]{2,1,0:T(8,128)} %get-tuple-element.59.refs_6_) | copy-start | bytes 73732
  133.0 10.8 %collective-permute-start.6 = (f32[48,128]{1,0:T(8,128)S(1)}, f32[48,128]{1,0:T(8,128)S(1)}, u32[]{:S(2)}, u32[]{:S(2)}) collective-permute-start(f32[48,128]{1,0:T(8,128)S(1)} %get-tuple-element.61), channel_id=1, source_target_pairs={{128,0},{129,1},{130,2},{131,3},{132,4},{133,5},{134,6},{135,7},{1... | collective-permute-start | bytes 73736 | tf_op jit(solution)/shard_map/ppermute | solution.py:692
  134.2 9.5 %collective-permute-start.7 = (f32[48,128]{1,0:T(8,128)S(1)}, f32[48,128]{1,0:T(8,128)S(1)}, u32[]{:S(2)}, u32[]{:S(2)}) collective-permute-start(f32[48,128]{1,0:T(8,128)S(1)} %get-tuple-element.62), channel_id=1, source_target_pairs={{128,8},{129,9},{130,10},{131,11},{132,12},{133,13},{134,14},{135,... | collective-permute-start | bytes 73736 | tf_op jit(solution)/shard_map/ppermute | solution.py:692
  135.5 10.1 %collective-permute-start.8 = (f32[48,128]{1,0:T(8,128)S(1)}, f32[48,128]{1,0:T(8,128)S(1)}, u32[]{:S(2)}, u32[]{:S(2)}) collective-permute-start(f32[48,128]{1,0:T(8,128)S(1)} %get-tuple-element.63), channel_id=1, source_target_pairs={{128,24},{129,25},{130,26},{131,27},{132,28},{133,29},{134,30},{13... | collective-permute-start | bytes 73736 | tf_op jit(solution)/shard_map/ppermute | solution.py:692
  136.8 9.3 %collective-permute-start.9 = (f32[48,128]{1,0:T(8,128)S(1)}, f32[48,128]{1,0:T(8,128)S(1)}, u32[]{:S(2)}, u32[]{:S(2)}) collective-permute-start(f32[48,128]{1,0:T(8,128)S(1)} %get-tuple-element.64), channel_id=1, source_target_pairs={{128,16},{129,17},{130,18},{131,19},{132,20},{133,21},{134,22},{13... | collective-permute-start | bytes 73736 | tf_op jit(solution)/shard_map/ppermute | solution.py:692

commit v8 on v7

--- a/solution.py
+++ b/solution.py
@@ -140,7 +140,7 @@
 
 
 def ready_kernel(
-    flags, state, speed, sz, rd, rr, rb, out, gather, spots, codes, last, lead
+    flags, state, speed, sz, rd, rr, rb, out, gather, codes, last, lead
 ):
     @pl.when(flags[0] == 0)
     def _():
@@ -156,8 +156,12 @@
             out[c] = times_paired(state[c], sz[...])
         y, z, x, core, lane = owners(rd[...])
         target = (y * CX + x) * CC + core
-        spots[...] = onehot(iota((SLOTS, SB), 0) == lane * TARGETS + target)
-        gather[...] = jnp.where(iota((RPB, SB), 0) == rr[...], 1.0, 0.0).T.astype(bf16)
+        gather[...] = lax.dot_general(
+            onehot(iota((SLOTS, SB), 0) == lane * TARGETS + target),
+            onehot(iota((RPB, SB), 0) == rr[...]),
+            NT,
+            preferred_element_type=f32,
+        ).astype(bf16)
         code = ((z - flags[3]) & (CZ - 1)) * NJ + rb[...] + 1
         tagged = jnp.where(iota((NZ, SB), 0) == lane, code.astype(f32), 0.0)
         sent = onehot(iota((TARGETS, SB), 0) == target)
@@ -186,7 +190,7 @@
 
 
 def bucket_kernel(flags, blocks, codes, place, merged, out, held, sems):
-    @pl.when(flags[0] != 0)
+    @pl.when(flags[0] == 0)
     def _():
         slots = [pick(place[...], times_paired(blocks[c], merged[...])) for c in range(3)]
         part = BRICKS // 4
@@ -201,7 +205,8 @@
                         row : row + part
                     ]
             block = pl.ds(first, part * CHUNK)
-            copies.append(pltpu.make_async_copy(held.at[block, :], out.at[block, :], sems.at[i]))
+            target = out.at[pl.ds(BRICKS * CHUNK + first, part * CHUNK), :]
+            copies.append(pltpu.make_async_copy(held.at[block, :], target, sems.at[i]))
             copies[-1].start()
         for copy in copies:
             copy.wait()
@@ -307,7 +312,6 @@
     own,
     other,
     gather,
-    spots,
     codes,
     sz,
     syh,
@@ -416,7 +420,7 @@
             copies[-1].start()
         send[pl.ds(3 * GROUP, TARGETS, stride=BACK), :] = codes[...]
         for c in range(3):
-            rows_out = pick(spots[...], pick(gather[...], velocity[c]))
+            rows_out = pick(gather[...], velocity[c])
             for lane in range(GROUP):
                 send[pl.ds(c * GROUP + lane, TARGETS, stride=BACK), :] = rows_out[
                     lane * TARGETS : (lane + 1) * TARGETS
@@ -557,9 +561,6 @@
         far=1,
         scratch=[pltpu.SemaphoreType.DMA],
     )
-    across = [(place_of(0, *q), place_of(1, *q)) for q in chips()]
-    blocks = lax.ppermute(blocks.reshape(3, SB, NK), ALL, across)
-
     sd, sr, rd, rr, rb = (
         v.reshape(1, SB) for v in (shell_dest, shell_row, return_dest, return_row, return_block)
     )
@@ -573,12 +574,22 @@
         sz.astype(np.float32),
         fetch=True,
     )
-    turned, gather, spots, codes, last, lead = call(
+    (bundle,) = call(
+        bucket_kernel,
+        [((2 * BRICKS * CHUNK, NZ), f32, "raw")],
+        flags,
+        blocks.reshape(3, SB, NK),
+        rows,
+        place,
+        merged,
+        scratch=[pltpu.VMEM((BRICKS * CHUNK, NZ), f32), pltpu.SemaphoreType.DMA((4,))],
+    )
+    bundle = lax.all_to_all(bundle.reshape(2 * BRICKS, CHUNK, 1, NZ), ALL, 0, 0, tiled=True)
+    turned, gather, codes, last, lead = call(
         ready_kernel,
         [
             ((3, RPB, NZ), f32),
-            ((SB, RPB), bf16, "home"),
-        ((SLOTS, SB), bf16, "home"),
+            ((SLOTS, RPB), bf16, "home"),
             ((TARGETS, NZ), f32, "home"),
             ((896, NK), f32, "home"),
             ((896, NK), f32, "home"),
@@ -592,19 +603,6 @@
         rb,
         fetch=True,
     )
-    blocks, turned = lax.optimization_barrier((blocks, turned))
-    (bundle,) = call(
-        bucket_kernel,
-        [((BRICKS * CHUNK, NZ), f32, "raw")],
-        flags,
-        blocks,
-        rows,
-        place,
-        merged,
-        scratch=[pltpu.VMEM((BRICKS * CHUNK, NZ), f32), pltpu.SemaphoreType.DMA((4,))],
-    )
-    bundle, last, lead = lax.optimization_barrier((bundle, last, lead))
-    bundle = lax.all_to_all(bundle.reshape(BRICKS, CHUNK, 1, NZ), DEV, 0, 0, tiled=True)
     ahead = [(d, (d + 1) % BRICKS) for d in range(BRICKS)]
     up = lax.ppermute(last, ALL, ahead)
     down = lax.ppermute(lead, ALL, [(b, a) for a, b in ahead])
@@ -613,7 +611,7 @@
         forward_kernel,
         [((3, 4, NY, NZ), f32), ((3 * NY, NZ), f32), ((3 * NY, NZ), f32)],
         flags,
-        bundle.reshape(BRICKS * CHUNK, NZ),
+        bundle.reshape(2 * BRICKS * CHUNK, NZ),
         turned,
         syh,
         syl,
@@ -661,7 +659,6 @@
         own,
         other,
         gather,
-        spots,
         codes,
         szp,
         syh,

time: 148 us -> 147 us (level)
  starting transfers between devices: 42.9 us -> 33.8 us
  waiting for transfers between devices: 38.3 us -> 42.7 us
  Pallas kernels: 9.57 us -> 11.3 us
  local copies, waits for them, and re-layouts: 0.88 us -> 2.55 us
    all_to_all x1, waiting for transfers between devices: 13.2 us -> 23.5 us  [on_device(): lax.all_to_all(bundle.reshape(2 * BRICKS, CHUNK, 1, NZ), ALL, 0, 0, tiled...]
    ppermute x1 -> x0, starting transfers between devices: 8.66 us -> none  [on_device(): blocks = lax.ppermute(blocks.reshape(3, SB, NK), ALL, across)]
    all_to_all x1, starting transfers between devices: 19.3 us -> 13.1 us  [on_device(): lax.all_to_all(bundle.reshape(2 * BRICKS, CHUNK, 1, NZ), ALL, 0, 0, tiled...]
    ppermute x1, starting transfers between devices: 1.35 us -> 6.7 us  [on_device(): incoming = lax.ppermute(outgoing, 'core', swap)]
    ppermute x1 -> x0, waiting for transfers between devices: 3.24 us -> none  [on_device(): blocks = lax.ppermute(blocks.reshape(3, SB, NK), ALL, across)]
    ppermute x4, waiting for transfers between devices: 8.01 us -> 5.65 us  [on_device(): parts.append(lax.ppermute(sums[k], ALL, pairs))]
    pallas_call x10, Pallas kernels: 9.57 us -> 11.3 us  [call(): pl.pallas_call(body, out_shape=[(pltpu.HBM if home else pltpu.VMEM)(*o[:2...]
    unnamed x36 -> x40, local copies, waits for them, and re-layouts: 0.88 us -> 2.55 us
  transfers between devices with their start and end apart: 11 -> 10, of which waited for: 9 -> 8; matrix products, arithmetic and copies ran while one was open for 0% -> 0% of each run, Pallas kernels for 3% -> 2%
where the time goes in v8:
time: 147 us; the launch traced here: 146 us
  blocking collectives  55.4 us (38%)
  waiting for transfers between devices  42.7 us (29%)
  starting transfers between devices  33.8 us (23%)
  Pallas kernels  11.3 us (8%)
  local copies, waits for them, and re-layouts  2.55 us (2%)
    all_to_all x1, waiting for transfers between devices, on_device(): lax.all_to_all(bundle.reshape(2 * BRICKS, CHUNK, 1, NZ), ALL, 0, 0, tiled...  23.5 us
    all_to_all x1, blocking collectives, on_device(): lax.all_to_all(share.reshape(CHIPS, 3, 4, NZ), same, 0, 0, tiled=True)  19 us
    all_to_all x1, blocking collectives, on_device(): lax.all_to_all(solved.reshape(CHIPS, 3, 4, NZ), same, 0, 0, tiled=True)  18.5 us
    all_to_all x1, blocking collectives, on_device(): lax.all_to_all(send.reshape(TARGETS, BACK, 1, NZ), ('y', 'x', 'core'), 0,...  18 us
    all_to_all x1, starting transfers between devices, on_device(): lax.all_to_all(bundle.reshape(2 * BRICKS, CHUNK, 1, NZ), ALL, 0, 0, tiled...  13.1 us
    pallas_call x10, Pallas kernels, call(): pl.pallas_call(body, out_shape=[(pltpu.HBM if home else pltpu.VMEM)(*o[:2...  11.3 us
    ppermute x1, starting transfers between devices, on_device(): incoming = lax.ppermute(outgoing, 'core', swap)  6.7 us
    ppermute x1, waiting for transfers between devices, on_device(): up = lax.ppermute(last, ALL, ahead)  6.59 us
  transfers between devices with their start and end apart: 10, of which 8 were waited for; matrix products, arithmetic and copies ran while one was open for 0% of the time, Pallas kernels for 2%

profile of v8, /device:TPU:1, one launch (start us, length us, event | category | flops | bytes accessed | tf_op | source)
XLA Modules:
  0.0 146.2 jit_solution(10115362248669142657)
XLA Ops:
  0.0 1.0 shard_map.163
  1.0 1.6 %shard_map.164 = (bf16[512,256]{1,0:T(8,128)(2,1)S(1)}, f32[128,128]{1,0:T(8,128)S(1)}, bf16[256,256]{1,0:T(8,128)(2,1)S(1)}) custom-call(s32[1]{0:T(128)} %bitcast.refs_0_, s32[1]{0:T(128)} %bitcast.1.refs_1_, s32[1]{0:T(128)} %bitcast.2.refs_2_, s32[1]{0:T(128)} %bitcast.3.refs_3_, s32[1,256]{1,0:T(1,128)} %bitcast.39, s32[1,256]{1,0:T(1,128)} %bitcast.40, ...), custom_call_target="tpu_custom_call" | custom-call | tf_op jit(solution)/shard_map/pallas_call | solution.py:509
  2.6 1.7 %shard_map.165 = f32[3328,128]{1,0:T(8,128)} custom-call(s32[1]{0:T(128)} %bitcast.refs_0_, s32[1]{0:T(128)} %bitcast.1.refs_1_, s32[1]{0:T(128)} %bitcast.2.refs_2_, s32[1]{0:T(128)} %bitcast.3.refs_3_, f32[3,256,128]{2,1,0:T(8,128)S(1)} %bitcast.32, f32[128,128]{1,0:T(8,128)S(1)} %get-tuple-element.29.refs_5_, ...), custom_call_target="tpu_custom_call" | custom-call | tf_op jit(solution)/shard_map/pallas_call | solution.py:509
  4.3 13.1 %all-to-all-start = ((f32[256,13,1,128]{3,2,1,0:T(1,128)}), f32[256,13,1,128]{3,2,1,0:T(1,128)S(1)}, u32[]{:S(2)}, u32[]{:S(2)}) async-start(f32[256,13,1,128]{3,2,1,0:T(1,128)} %bitcast.37), calls=%async_computation | async-start | bytes 3407872 | tf_op jit(solution)/shard_map/all_to_all | solution.py:587
  17.4 0.0 copy-start.1
  17.4 0.0 copy-start.5
  17.4 3.0 %shard_map.166 = (f32[3,1024,128]{2,1,0:T(8,128)S(1)}, bf16[512,1024]{1,0:T(8,128)(2,1)}, f32[32,128]{1,0:T(8,128)}, f32[896,128]{1,0:T(8,128)}, f32[896,128]{1,0:T(8,128)}) custom-call(s32[1]{0:T(128)} %bitcast.refs_0_, s32[1]{0:T(128)} %bitcast.1.refs_1_, s32[1]{0:T(128)} %bitcast.2.refs_2_, s32[1]{0:T(128)} %bitcast.3.refs_3_, f32[3,1024,128]{2,1,0:T(8,128)} %bitcast.24, ...), custom_call_target="tpu_custom_call" | custom-call | tf_op jit(solution)/shard_map/pallas_call | solution.py:509
  20.5 3.5 %collective-permute-start = (f32[896,128]{1,0:T(8,128)}, f32[896,128]{1,0:T(8,128)S(1)}, u32[]{:S(2)}, u32[]{:S(2)}) collective-permute-start(f32[896,128]{1,0:T(8,128)} %get-tuple-element.32), channel_id=1, source_target_pairs={{0,1},{1,2},{2,3},{3,4},{4,5},{5,6},{6,7},{7,8},{8,9},{9,10},{10,1... | collective-permute-start | bytes 1376264 | tf_op jit(solution)/shard_map/ppermute | solution.py:607
  24.0 2.4 %collective-permute-start.1 = (f32[896,128]{1,0:T(8,128)}, f32[896,128]{1,0:T(8,128)S(1)}, u32[]{:S(2)}, u32[]{:S(2)}) collective-permute-start(f32[896,128]{1,0:T(8,128)} %get-tuple-element.33), channel_id=1, source_target_pairs={{1,0},{2,1},{3,2},{4,3},{5,4},{6,5},{7,6},{8,7},{9,8},{10,9},{11,1... | collective-permute-start | bytes 1376264 | tf_op jit(solution)/shard_map/ppermute | solution.py:608
  26.5 6.6 %collective-permute-done.refs_17_ = f32[896,128]{1,0:T(8,128)S(1)} collective-permute-done((f32[896,128]{1,0:T(8,128)}, f32[896,128]{1,0:T(8,128)S(1)}, u32[]{:S(2)}, u32[]{:S(2)}) %collective-permute-start) | collective-permute-done | bytes 458784 | tf_op jit(solution)/shard_map/ppermute | solution.py:607
  33.1 0.8 copy-done.8
  33.8 4.0 %collective-permute-done.1.refs_18_ = f32[896,128]{1,0:T(8,128)S(1)} collective-permute-done((f32[896,128]{1,0:T(8,128)}, f32[896,128]{1,0:T(8,128)S(1)}, u32[]{:S(2)}, u32[]{:S(2)}) %collective-permute-start.1) | collective-permute-done | bytes 458784 | tf_op jit(solution)/shard_map/ppermute | solution.py:608
  37.8 0.8 copy-done.10
  38.6 23.5 %all-to-all-done = f32[256,13,1,128]{3,2,1,0:T(1,128)S(1)} async-done(((f32[256,13,1,128]{3,2,1,0:T(1,128)}), f32[256,13,1,128]{3,2,1,0:T(1,128)S(1)}, u32[]{:S(2)}, u32[]{:S(2)}) %all-to-all-start) | async-done | bytes 1703968 | tf_op jit(solution)/shard_map/all_to_all | solution.py:587
  62.1 0.9 copy-done.6
  63.0 0.0 copy-start.17
  63.0 6.7 %collective-permute-start.2 = (f32[768,128]{1,0:T(8,128)S(1)}, f32[768,128]{1,0:T(8,128)S(1)}, u32[]{:S(2)}, u32[]{:S(2)}) collective-permute-start(f32[768,128]{1,0:T(8,128)S(1)} %get-tuple-element.37), channel_id=1, source_target_pairs={{0,1},{1,0},{2,3},{3,2},{4,5},{5,4},{6,7},{7,6},{8,9},{9,8},{10,11... | collective-permute-start | bytes 1179656 | tf_op jit(solution)/shard_map/ppermute | solution.py:622
  69.7 1.3 collective-permute-done.2.refs_4_
  71.1 19.0 %all_to_all.20 = f32[64,3,4,128]{3,2,1,0:T(4,128)S(1)} all-to-all(f32[64,3,4,128]{3,2,1,0:T(4,128)S(1)} %bitcast.36), channel_id=1, replica_groups=mesh['grp'=2,'y'=4,'z'=4,'x'=4,'core'=2] {'y','z','x'}, dimensions={0} | all-to-all | bytes 786432 | tf_op jit(solution)/shard_map/all_to_all | solution.py:632
  90.1 18.5 %all_to_all.21 = f32[64,3,4,128]{3,2,1,0:T(4,128)S(1)} all-to-all(f32[64,3,4,128]{3,2,1,0:T(4,128)S(1)} %bitcast.31), channel_id=1, replica_groups=mesh['grp'=2,'y'=4,'z'=4,'x'=4,'core'=2] {'y','z','x'}, dimensions={0} | all-to-all | bytes 786432 | tf_op jit(solution)/shard_map/all_to_all | solution.py:644
  108.6 2.9 %collective-permute-start.4 = (f32[768,128]{1,0:T(8,128)S(1)}, f32[768,128]{1,0:T(8,128)S(1)}, u32[]{:S(2)}, u32[]{:S(2)}) collective-permute-start(f32[768,128]{1,0:T(8,128)S(1)} %bitcast.33), channel_id=1, source_target_pairs={{0,1},{1,0},{2,3},{3,2},{4,5},{5,4},{6,7},{7,6},{8,9},{9,8},{10,11... | collective-permute-start | bytes 1179656 | tf_op jit(solution)/shard_map/ppermute | solution.py:646
  111.5 1.6 %collective-permute-done.3.refs_6_ = f32[384,128]{1,0:T(8,128)S(1)} collective-permute-done((f32[384,128]{1,0:T(8,128)S(1)}, f32[384,128]{1,0:T(8,128)S(1)}, u32[]{:S(2)}, u32[]{:S(2)}) %collective-permute-start.3) | collective-permute-done | bytes 196640 | tf_op jit(solution)/shard_map/ppermute | solution.py:631
  113.2 3.1 %shard_map.170 = (f32[1568,128]{1,0:T(8,128)S(1)}, f32[3,1024,128]{2,1,0:T(8,128)}, f32[3,16,8,128]{3,2,1,0:T(8,128)}, f32[3,16,128]{2,1,0:T(8,128)}) custom-call(s32[1]{0:T(128)} %bitcast.refs_0_, s32[1]{0:T(128)} %bitcast.1.refs_1_, s32[1]{0:T(128)} %bitcast.2.refs_2_, s32[1]{0:T(128)} %bitcast.3.refs_3_, ...), custom_call_target="tpu_custom_call" | custom-call | tf_op jit(solution)/shard_map/pallas_call | solution.py:509
  116.3 18.0 %all_to_all.22 = f32[32,49,1,128]{3,2,1,0:T(1,128)S(1)} all-to-all(f32[32,49,1,128]{3,2,1,0:T(1,128)S(1)} %bitcast.35), channel_id=1, replica_groups=mesh['grp'=2,'y'=4,'z'=4,'x'=4,'core'=2] {'y','x','core'}, dimensions={0} | all-to-all | bytes 1605632 | tf_op jit(solution)/shard_map/all_to_all | solution.py:678
  134.2 1.3 collective-permute-start.5
  135.5 1.3 collective-permute-start.6
  136.8 1.3 collective-permute-start.7
  138.1 1.3 collective-permute-start.8
  139.4 3.3 %collective-permute-done.5.refs_8_ = f32[48,128]{1,0:T(8,128)S(1)} collective-permute-done((f32[48,128]{1,0:T(8,128)S(1)}, f32[48,128]{1,0:T(8,128)S(1)}, u32[]{:S(2)}, u32[]{:S(2)}) %collective-permute-start.5) | collective-permute-done | bytes 24608 | tf_op jit(solution)/shard_map/ppermute | solution.py:689
  142.7 1.9 %collective-permute-done.7.refs_10_ = f32[48,128]{1,0:T(8,128)S(1)} collective-permute-done((f32[48,128]{1,0:T(8,128)S(1)}, f32[48,128]{1,0:T(8,128)S(1)}, u32[]{:S(2)}, u32[]{:S(2)}) %collective-permute-start.7) | collective-permute-done | bytes 24608 | tf_op jit(solution)/shard_map/ppermute | solution.py:689
  144.5 0.5 collective-permute-done.8.refs_11_
  145.1 0.9 shard_map.172
  (41 shorter events, 0.1 us)
Async XLA Ops:
  4.3 57.7 %all-to-all-start = ((f32[256,13,1,128]{3,2,1,0:T(1,128)}), f32[256,13,1,128]{3,2,1,0:T(1,128)S(1)}, u32[]{:S(2)}, u32[]{:S(2)}) async-start(f32[256,13,1,128]{3,2,1,0:T(1,128)} %bitcast.37), calls=%async_computation | async-start | bytes 3407872 | tf_op jit(solution)/shard_map/all_to_all | solution.py:587
  17.4 44.7 %copy-start.1 = (f32[256,128]{1,0:T(8,128)S(1)}, f32[256,128]{1,0:T(8,128)}, u32[]{:S(2)}) copy-start(f32[256,128]{1,0:T(8,128)} %constant.47.clone.refs_8_.refs_6_.refs_9_.refs_14_) | copy-start | bytes 393220
  17.4 44.6 %copy-start.5 = (bf16[256,256]{1,0:T(8,128)(2,1)S(1)}, bf16[256,256]{1,0:T(8,128)(2,1)}, u32[]{:S(2)}) copy-start(bf16[256,256]{1,0:T(8,128)(2,1)} %constant.46.clone.refs_7_.refs_13_) | copy-start | bytes 393220
  20.5 12.6 %collective-permute-start = (f32[896,128]{1,0:T(8,128)}, f32[896,128]{1,0:T(8,128)S(1)}, u32[]{:S(2)}, u32[]{:S(2)}) collective-permute-start(f32[896,128]{1,0:T(8,128)} %get-tuple-element.32), channel_id=1, source_target_pairs={{0,1},{1,2},{2,3},{3,4},{4,5},{5,6},{6,7},{7,8},{8,9},{9,10},{10,1... | collective-permute-start | bytes 1376264 | tf_op jit(solution)/shard_map/ppermute | solution.py:607
  24.0 13.8 %collective-permute-start.1 = (f32[896,128]{1,0:T(8,128)}, f32[896,128]{1,0:T(8,128)S(1)}, u32[]{:S(2)}, u32[]{:S(2)}) collective-permute-start(f32[896,128]{1,0:T(8,128)} %get-tuple-element.33), channel_id=1, source_target_pairs={{1,0},{2,1},{3,2},{4,3},{5,4},{6,5},{7,6},{8,7},{9,8},{10,9},{11,1... | collective-permute-start | bytes 1376264 | tf_op jit(solution)/shard_map/ppermute | solution.py:608
  33.0 0.8 copy-start.8
  37.8 0.8 copy-start.10
  62.1 0.9 copy-start.6
  63.0 27.1 %copy-start.13 = (f32[512,1]{1,0:T(8,128)S(1)}, f32[512,1]{1,0:T(8,128)}, u32[]{:S(2)}) copy-start(f32[512,1]{1,0:T(8,128)} %constant.51.clone.refs_8_) | copy-start | bytes 6148
  63.0 27.1 %copy-start.14 = (bf16[512,192]{1,0:T(8,128)(2,1)S(1)}, bf16[512,192]{1,0:T(8,128)(2,1)}, u32[]{:S(2)}) copy-start(bf16[512,192]{1,0:T(8,128)(2,1)} %constant.48.clone.refs_5_) | copy-start | bytes 589828
  63.0 50.1 %copy-start.11 = (f32[896,128]{1,0:T(8,128)S(1)}, f32[896,128]{1,0:T(8,128)}, u32[]{:S(2)}) copy-start(f32[896,128]{1,0:T(8,128)} %copy-done.10) | copy-start | bytes 1376260
  63.0 27.1 %copy-start.16 = (bf16[64,512]{1,0:T(8,128)(2,1)S(1)}, bf16[64,512]{1,0:T(8,128)(2,1)}, u32[]{:S(2)}) copy-start(bf16[64,512]{1,0:T(8,128)(2,1)} %constant.50.clone.refs_7_) | copy-start | bytes 196612
  63.0 27.1 %copy-start.17 = (bf16[64,512]{1,0:T(8,128)(2,1)S(1)}, bf16[64,512]{1,0:T(8,128)(2,1)}, u32[]{:S(2)}) copy-start(bf16[64,512]{1,0:T(8,128)(2,1)} %constant.49.clone.refs_6_) | copy-start | bytes 196612
  63.0 8.0 %collective-permute-start.2 = (f32[768,128]{1,0:T(8,128)S(1)}, f32[768,128]{1,0:T(8,128)S(1)}, u32[]{:S(2)}, u32[]{:S(2)}) collective-permute-start(f32[768,128]{1,0:T(8,128)S(1)} %get-tuple-element.37), channel_id=1, source_target_pairs={{0,1},{1,0},{2,3},{3,2},{4,5},{5,4},{6,7},{7,6},{8,9},{9,8},{10,11... | collective-permute-start | bytes 1179656 | tf_op jit(solution)/shard_map/ppermute | solution.py:622
  71.1 42.0 %copy-start.4 = (bf16[256,256]{1,0:T(8,128)(2,1)S(1)}, bf16[256,256]{1,0:T(8,128)(2,1)}, u32[]{:S(2)}) copy-start(bf16[256,256]{1,0:T(8,128)(2,1)} %constant.44.clone.refs_6_.refs_11_) | copy-start | bytes 393220
  71.1 42.0 %copy-start.7 = (bf16[256,256]{1,0:T(8,128)(2,1)S(1)}, bf16[256,256]{1,0:T(8,128)(2,1)}, u32[]{:S(2)}) copy-start(bf16[256,256]{1,0:T(8,128)(2,1)} %constant.45.clone.refs_6_.refs_12_) | copy-start | bytes 393220
  71.1 42.0 %copy-start.9 = (f32[896,128]{1,0:T(8,128)S(1)}, f32[896,128]{1,0:T(8,128)}, u32[]{:S(2)}) copy-start(f32[896,128]{1,0:T(8,128)} %copy-done.8) | copy-start | bytes 1376260
  71.1 42.1 %copy-start.19 = (f32[32,128]{1,0:T(8,128)S(1)}, f32[32,128]{1,0:T(8,128)}, u32[]{:S(2)}) copy-start(f32[32,128]{1,0:T(8,128)} %get-tuple-element.42.refs_10_) | copy-start | bytes 49156
  71.1 42.1 %copy-start = (f32[1,3,131072]{2,0,1:T(1,128)S(1)}, f32[1,3,131072]{2,0,1:T(1,128)}, u32[]{:S(2)}) copy-start(f32[1,3,131072]{2,0,1:T(1,128)} %param.17) | copy-start | bytes 4718596
  71.1 42.1 %copy-start.2 = (f32[131072]{0:T(1024)S(1)}, f32[131072]{0:T(1024)}, u32[]{:S(2)}) copy-start(f32[131072]{0:T(1024)} %param.18) | copy-start | bytes 1572868
  71.1 42.1 %copy-start.3 = (bf16[512,1024]{1,0:T(8,128)(2,1)S(1)}, bf16[512,1024]{1,0:T(8,128)(2,1)}, u32[]{:S(2)}) copy-start(bf16[512,1024]{1,0:T(8,128)(2,1)} %get-tuple-element.41.refs_9_) | copy-start | bytes 3145732
  108.6 4.5 %collective-permute-start.4 = (f32[768,128]{1,0:T(8,128)S(1)}, f32[768,128]{1,0:T(8,128)S(1)}, u32[]{:S(2)}, u32[]{:S(2)}) collective-permute-start(f32[768,128]{1,0:T(8,128)S(1)} %bitcast.33), channel_id=1, source_target_pairs={{0,1},{1,0},{2,3},{3,2},{4,5},{5,4},{6,7},{7,6},{8,9},{9,8},{10,11... | collective-permute-start | bytes 1179656 | tf_op jit(solution)/shard_map/ppermute | solution.py:646
  111.5 1.6 %collective-permute-start.3 = (f32[384,128]{1,0:T(8,128)S(1)}, f32[384,128]{1,0:T(8,128)S(1)}, u32[]{:S(2)}, u32[]{:S(2)}) collective-permute-start(f32[384,128]{1,0:T(8,128)S(1)} %get-tuple-element.39.refs_5_), channel_id=1, source_target_pairs={{0,1},{1,0},{2,3},{3,2},{4,5},{5,4},{6,7},{7,6},{8,9},{9,8},{10,11... | collective-permute-start | bytes 589832 | tf_op jit(solution)/shard_map/ppermute | solution.py:631
  116.2 28.8 %copy-start.12 = (f32[128,128]{1,0:T(8,128)S(1)}, f32[128,128]{1,0:T(8,128)}, u32[]{:S(2)}) copy-start(f32[128,128]{1,0:T(8,128)} %refs_7_.4) | copy-start | bytes 196612
  116.2 28.8 %copy-start.15 = (f32[3,16,8,128]{3,2,1,0:T(8,128)S(1)}, f32[3,16,8,128]{3,2,1,0:T(8,128)}, u32[]{:S(2)}) copy-start(f32[3,16,8,128]{3,2,1,0:T(8,128)} %get-tuple-element.46.refs_5_) | copy-start | bytes 589828
  116.3 28.8 %copy-start.18 = (f32[3,16,128]{2,1,0:T(8,128)S(1)}, f32[3,16,128]{2,1,0:T(8,128)}, u32[]{:S(2)}) copy-start(f32[3,16,128]{2,1,0:T(8,128)} %get-tuple-element.47.refs_6_) | copy-start | bytes 73732
  134.2 8.5 %collective-permute-start.5 = (f32[48,128]{1,0:T(8,128)S(1)}, f32[48,128]{1,0:T(8,128)S(1)}, u32[]{:S(2)}, u32[]{:S(2)}) collective-permute-start(f32[48,128]{1,0:T(8,128)S(1)} %get-tuple-element.49), channel_id=1, source_target_pairs={{128,0},{129,1},{130,2},{131,3},{132,4},{133,5},{134,6},{135,7},{1... | collective-permute-start | bytes 73736 | tf_op jit(solution)/shard_map/ppermute | solution.py:689
  135.5 7.2 %collective-permute-start.6 = (f32[48,128]{1,0:T(8,128)S(1)}, f32[48,128]{1,0:T(8,128)S(1)}, u32[]{:S(2)}, u32[]{:S(2)}) collective-permute-start(f32[48,128]{1,0:T(8,128)S(1)} %get-tuple-element.50), channel_id=1, source_target_pairs={{128,8},{129,9},{130,10},{131,11},{132,12},{133,13},{134,14},{135,... | collective-permute-start | bytes 73736 | tf_op jit(solution)/shard_map/ppermute | solution.py:689
  136.8 7.7 %collective-permute-start.7 = (f32[48,128]{1,0:T(8,128)S(1)}, f32[48,128]{1,0:T(8,128)S(1)}, u32[]{:S(2)}, u32[]{:S(2)}) collective-permute-start(f32[48,128]{1,0:T(8,128)S(1)} %get-tuple-element.51), channel_id=1, source_target_pairs={{128,24},{129,25},{130,26},{131,27},{132,28},{133,29},{134,30},{13... | collective-permute-start | bytes 73736 | tf_op jit(solution)/shard_map/ppermute | solution.py:689
  138.1 7.0 %collective-permute-start.8 = (f32[48,128]{1,0:T(8,128)S(1)}, f32[48,128]{1,0:T(8,128)S(1)}, u32[]{:S(2)}, u32[]{:S(2)}) collective-permute-start(f32[48,128]{1,0:T(8,128)S(1)} %get-tuple-element.52), channel_id=1, source_target_pairs={{128,16},{129,17},{130,18},{131,19},{132,20},{133,21},{134,22},{13... | collective-permute-start | bytes 73736 | tf_op jit(solution)/shard_map/ppermute | solution.py:689

commit v9 on v8

--- a/solution.py
+++ b/solution.py
@@ -220,9 +220,17 @@
     return g11, g12, g13
 
 
-def forward_kernel(flags, received, work, syh, syl, mu, planes, outgoing, kept):
+def forward_kernel(
+    flags, received, work, mu, high_home, low_home, planes, outgoing, kept, syh, syl, sems
+):
     @pl.when(flags[0] != 0)
     def _():
+        copies = [
+            pltpu.make_async_copy(high_home, syh, sems.at[0]),
+            pltpu.make_async_copy(low_home, syl, sems.at[1]),
+        ]
+        for copy in copies:
+            copy.start()
         beta = mu[...] + 2.0
         g11, g12, g13 = weights(beta)
         first = flags[1] == 0
@@ -235,6 +243,9 @@
             )
             field = (pick(spread, rows) + work[c]) * (4.0 / ((NY + 1) * (NZ + 1)))
             field = jnp.concatenate([field[p * NY : (p + 1) * NY] for p in range(4)], axis=1)
+            if c == 0:
+                for copy in copies:
+                    copy.wait()
             field = table_times(syh[...], syl[...], field)
             f0, f1, f2, f3 = (field[:, p * NZ : (p + 1) * NZ] for p in range(4))
             for p, plane in enumerate((f0, f1, f2, f3)):
@@ -606,16 +617,21 @@
     ahead = [(d, (d + 1) % BRICKS) for d in range(BRICKS)]
     up = lax.ppermute(last, ALL, ahead)
     down = lax.ppermute(lead, ALL, [(b, a) for a, b in ahead])
-    bundle, up, down = lax.optimization_barrier((bundle, up, down))
     planes, outgoing, kept = call(
         forward_kernel,
         [((3, 4, NY, NZ), f32), ((3 * NY, NZ), f32), ((3 * NY, NZ), f32)],
         flags,
         bundle.reshape(2 * BRICKS * CHUNK, NZ),
         turned,
+        mu,
         syh,
         syl,
-        mu,
+        far=2,
+        scratch=[
+            pltpu.VMEM((NY, NY), bf16),
+            pltpu.VMEM((NY, NY), bf16),
+            pltpu.SemaphoreType.DMA((2,)),
+        ],
     )
     swap = [(0, 1), (1, 0)]
     same = ("y", "z", "x")

time: 147 us -> 155 us (1.054)
  blocking collectives: 55.4 us -> 38.3 us
  waiting for transfers between devices: 42.7 us -> 58.7 us
  starting transfers between devices: 33.8 us -> 38.8 us
  local copies, waits for them, and re-layouts: 2.55 us -> 4.76 us
  Pallas kernels: 11.3 us -> 12.9 us
    all_to_all x1 -> x0, blocking collectives: 18.5 us -> none  [on_device(): lax.all_to_all(solved.reshape(CHIPS, 3, 4, NZ), same, 0, 0, tiled=True)]
    all_to_all x1, waiting for transfers between devices: 23.5 us -> 41.6 us  [on_device(): lax.all_to_all(bundle.reshape(2 * BRICKS, CHUNK, 1, NZ), ALL, 0, 0, tiled...]
    all_to_all x0 -> x1, waiting for transfers between devices: none -> 6.84 us  [on_device(): lax.all_to_all(solved.reshape(CHIPS, 3, 4, NZ), same, 0, 0, tiled=True)]
    ppermute x1, waiting for transfers between devices: 6.59 us -> 0.01 us  [on_device(): up = lax.ppermute(last, ALL, ahead)]
    ppermute x1, starting transfers between devices: 6.7 us -> 1.16 us  [on_device(): incoming = lax.ppermute(outgoing, 'core', swap)]
    all_to_all x0 -> x1, starting transfers between devices: none -> 5.31 us  [on_device(): lax.all_to_all(solved.reshape(CHIPS, 3, 4, NZ), same, 0, 0, tiled=True)]
    ppermute x1, starting transfers between devices: 2.9 us -> 7.46 us  [on_device(): other = lax.ppermute(own, 'core', swap)]
    ppermute x1, waiting for transfers between devices: 3.98 us -> 0.01 us  [on_device(): down = lax.ppermute(lead, ALL, [(b, a) for a, b in ahead])]
  transfers between devices with their start and end apart: 10 -> 11, of which waited for: 8 -> 8; matrix products, arithmetic and copies ran while one was open for 0% -> 0% of each run, Pallas kernels for 2% -> 2%
where the time goes in v9:
time: 155 us; the launch traced here: 154 us
  waiting for transfers between devices  58.7 us (38%)
  starting transfers between devices  38.8 us (25%)
  blocking collectives  38.3 us (25%)
  Pallas kernels  12.9 us (8%)
  local copies, waits for them, and re-layouts  4.76 us (3%)
    all_to_all x1, waiting for transfers between devices, on_device(): lax.all_to_all(bundle.reshape(2 * BRICKS, CHUNK, 1, NZ), ALL, 0, 0, tiled...  41.6 us
    all_to_all x1, blocking collectives, on_device(): lax.all_to_all(share.reshape(CHIPS, 3, 4, NZ), same, 0, 0, tiled=True)  20.4 us
    all_to_all x1, blocking collectives, on_device(): lax.all_to_all(send.reshape(TARGETS, BACK, 1, NZ), ('y', 'x', 'core'), 0,...  17.9 us
    all_to_all x1, starting transfers between devices, on_device(): lax.all_to_all(bundle.reshape(2 * BRICKS, CHUNK, 1, NZ), ALL, 0, 0, tiled...  13.1 us
    pallas_call x10, Pallas kernels, call(): pl.pallas_call(body, out_shape=[(pltpu.HBM if home else pltpu.VMEM)(*o[:2...  12.9 us
    ppermute x1, starting transfers between devices, on_device(): other = lax.ppermute(own, 'core', swap)  7.46 us
    ppermute x4, waiting for transfers between devices, on_device(): parts.append(lax.ppermute(sums[k], ALL, pairs))  7.21 us
    all_to_all x1, waiting for transfers between devices, on_device(): lax.all_to_all(solved.reshape(CHIPS, 3, 4, NZ), same, 0, 0, tiled=True)  6.84 us
  transfers between devices with their start and end apart: 11, of which 8 were waited for; matrix products, arithmetic and copies ran while one was open for 0% of the time, Pallas kernels for 2%

profile of v9, /device:TPU:1, one launch (start us, length us, event | category | flops | bytes accessed | tf_op | source)
XLA Modules:
  0.0 153.8 jit_solution(885369739701115231)
XLA Ops:
  0.0 1.0 shard_map.163
  1.0 1.6 %shard_map.164 = (bf16[512,256]{1,0:T(8,128)(2,1)S(1)}, f32[128,128]{1,0:T(8,128)S(1)}, bf16[256,256]{1,0:T(8,128)(2,1)S(1)}) custom-call(s32[1]{0:T(128)} %bitcast.refs_0_, s32[1]{0:T(128)} %bitcast.1.refs_1_, s32[1]{0:T(128)} %bitcast.2.refs_2_, s32[1]{0:T(128)} %bitcast.3.refs_3_, s32[1,256]{1,0:T(1,128)} %bitcast.38, s32[1,256]{1,0:T(1,128)} %bitcast.39, ...), custom_call_target="tpu_custom_call" | custom-call | tf_op jit(solution)/shard_map/pallas_call | solution.py:520
  2.6 1.7 %shard_map.165 = f32[3328,128]{1,0:T(8,128)} custom-call(s32[1]{0:T(128)} %bitcast.refs_0_, s32[1]{0:T(128)} %bitcast.1.refs_1_, s32[1]{0:T(128)} %bitcast.2.refs_2_, s32[1]{0:T(128)} %bitcast.3.refs_3_, f32[3,256,128]{2,1,0:T(8,128)S(1)} %bitcast.31, f32[128,128]{1,0:T(8,128)S(1)} %get-tuple-element.26.refs_5_, ...), custom_call_target="tpu_custom_call" | custom-call | tf_op jit(solution)/shard_map/pallas_call | solution.py:520
  4.3 13.1 %all-to-all-start = ((f32[256,13,1,128]{3,2,1,0:T(1,128)}), f32[256,13,1,128]{3,2,1,0:T(1,128)S(1)}, u32[]{:S(2)}, u32[]{:S(2)}) async-start(f32[256,13,1,128]{3,2,1,0:T(1,128)} %bitcast.36), calls=%async_computation | async-start | bytes 3407872 | tf_op jit(solution)/shard_map/all_to_all | solution.py:598
  17.4 0.0 copy-start.1
  17.4 3.0 %shard_map.166 = (f32[3,1024,128]{2,1,0:T(8,128)S(1)}, bf16[512,1024]{1,0:T(8,128)(2,1)}, f32[32,128]{1,0:T(8,128)}, f32[896,128]{1,0:T(8,128)}, f32[896,128]{1,0:T(8,128)}) custom-call(s32[1]{0:T(128)} %bitcast.refs_0_, s32[1]{0:T(128)} %bitcast.1.refs_1_, s32[1]{0:T(128)} %bitcast.2.refs_2_, s32[1]{0:T(128)} %bitcast.3.refs_3_, f32[3,1024,128]{2,1,0:T(8,128)} %bitcast.24, ...), custom_call_target="tpu_custom_call" | custom-call | tf_op jit(solution)/shard_map/pallas_call | solution.py:520
  20.4 41.6 %all-to-all-done = f32[256,13,1,128]{3,2,1,0:T(1,128)S(1)} async-done(((f32[256,13,1,128]{3,2,1,0:T(1,128)}), f32[256,13,1,128]{3,2,1,0:T(1,128)S(1)}, u32[]{:S(2)}, u32[]{:S(2)}) %all-to-all-start) | async-done | bytes 1703968 | tf_op jit(solution)/shard_map/all_to_all | solution.py:598
  62.1 1.1 copy-done.3
  63.2 1.2 collective-permute-start
  64.4 1.3 collective-permute-done.refs_4_
  65.8 20.4 %all_to_all.20 = f32[64,3,4,128]{3,2,1,0:T(4,128)S(1)} all-to-all(f32[64,3,4,128]{3,2,1,0:T(4,128)S(1)} %bitcast.35), channel_id=1, replica_groups=mesh['grp'=2,'y'=4,'z'=4,'x'=4,'core'=2] {'y','z','x'}, dimensions={0} | all-to-all | bytes 786432 | tf_op jit(solution)/shard_map/all_to_all | solution.py:648
  86.2 0.8 shard_map.169
  87.0 5.3 %all-to-all-start.2 = ((f32[64,3,4,128]{3,2,1,0:T(4,128)}), f32[64,3,4,128]{3,2,1,0:T(4,128)S(1)}, u32[]{:S(2)}, u32[]{:S(2)}) async-start(f32[64,3,4,128]{3,2,1,0:T(4,128)} %bitcast.17), calls=%async_computation.2 | async-start | bytes 786432 | tf_op jit(solution)/shard_map/all_to_all | solution.py:660
  92.3 4.7 %collective-permute-start.3 = (f32[896,128]{1,0:T(8,128)}, f32[896,128]{1,0:T(8,128)S(1)}, u32[]{:S(2)}, u32[]{:S(2)}) collective-permute-start(f32[896,128]{1,0:T(8,128)} %get-tuple-element.37), channel_id=1, source_target_pairs={{0,1},{1,2},{2,3},{3,4},{4,5},{5,6},{6,7},{7,8},{8,9},{9,10},{10,1... | collective-permute-start | bytes 1376264 | tf_op jit(solution)/shard_map/ppermute | solution.py:618
  97.0 1.9 %collective-permute-start.4 = (f32[896,128]{1,0:T(8,128)}, f32[896,128]{1,0:T(8,128)}, u32[]{:S(2)}, u32[]{:S(2)}) collective-permute-start(f32[896,128]{1,0:T(8,128)} %get-tuple-element.38), channel_id=1, source_target_pairs={{1,0},{2,1},{3,2},{4,3},{5,4},{6,5},{7,6},{8,7},{9,8},{10,9},{11,1... | collective-permute-start | bytes 1376264 | tf_op jit(solution)/shard_map/ppermute | solution.py:619
  98.9 6.8 %all-to-all-done.2 = f32[64,3,4,128]{3,2,1,0:T(4,128)S(1)} async-done(((f32[64,3,4,128]{3,2,1,0:T(4,128)}), f32[64,3,4,128]{3,2,1,0:T(4,128)S(1)}, u32[]{:S(2)}, u32[]{:S(2)}) %all-to-all-start.2) | async-done | bytes 393248 | tf_op jit(solution)/shard_map/all_to_all | solution.py:660
  105.8 7.5 %collective-permute-start.2 = (f32[768,128]{1,0:T(8,128)S(1)}, f32[768,128]{1,0:T(8,128)S(1)}, u32[]{:S(2)}, u32[]{:S(2)}) collective-permute-start(f32[768,128]{1,0:T(8,128)S(1)} %bitcast.32), channel_id=1, source_target_pairs={{0,1},{1,0},{2,3},{3,2},{4,5},{5,4},{6,7},{7,6},{8,9},{9,8},{10,11... | collective-permute-start | bytes 1179656 | tf_op jit(solution)/shard_map/ppermute | solution.py:662
  113.2 1.6 %collective-permute-done.1.refs_6_ = f32[384,128]{1,0:T(8,128)S(1)} collective-permute-done((f32[384,128]{1,0:T(8,128)}, f32[384,128]{1,0:T(8,128)S(1)}, u32[]{:S(2)}, u32[]{:S(2)}) %collective-permute-start.1) | collective-permute-done | bytes 196640 | tf_op jit(solution)/shard_map/ppermute | solution.py:647
  114.9 1.4 copy-done.4
  116.3 1.2 copy-done.5
  117.6 0.9 copy-done.14
  118.5 3.9 %shard_map.170 = (f32[1568,128]{1,0:T(8,128)S(1)}, f32[3,1024,128]{2,1,0:T(8,128)}, f32[3,16,8,128]{3,2,1,0:T(8,128)}, f32[3,16,128]{2,1,0:T(8,128)}) custom-call(s32[1]{0:T(128)} %bitcast.refs_0_, s32[1]{0:T(128)} %bitcast.1.refs_1_, s32[1]{0:T(128)} %bitcast.2.refs_2_, s32[1]{0:T(128)} %bitcast.3.refs_3_, f32[3,4,256,128]{3,2,1,0:T(8,128)S(1)} %copy-done.4, ...), custom_call_target="tpu_custom_call" | custom-call | tf_op jit(solution)/shard_map/pallas_call | solution.py:520
  122.4 17.9 %all_to_all.21 = f32[32,49,1,128]{3,2,1,0:T(1,128)S(1)} all-to-all(f32[32,49,1,128]{3,2,1,0:T(1,128)S(1)} %bitcast.34), channel_id=1, replica_groups=mesh['grp'=2,'y'=4,'z'=4,'x'=4,'core'=2] {'y','x','core'}, dimensions={0} | all-to-all | bytes 1605632 | tf_op jit(solution)/shard_map/all_to_all | solution.py:694
  140.3 1.3 collective-permute-start.5
  141.6 1.3 collective-permute-start.6
  142.9 1.3 collective-permute-start.7
  144.2 1.3 collective-permute-start.8
  145.5 3.3 %collective-permute-done.5.refs_8_ = f32[48,128]{1,0:T(8,128)S(1)} collective-permute-done((f32[48,128]{1,0:T(8,128)S(1)}, f32[48,128]{1,0:T(8,128)S(1)}, u32[]{:S(2)}, u32[]{:S(2)}) %collective-permute-start.5) | collective-permute-done | bytes 24608 | tf_op jit(solution)/shard_map/ppermute | solution.py:705
  148.8 1.3 collective-permute-done.6.refs_9_
  150.1 1.1 collective-permute-done.7.refs_10_
  151.3 1.5 collective-permute-done.8.refs_11_
  152.7 0.9 shard_map.172
  (40 shorter events, 0.1 us)
Async XLA Ops:
  4.3 57.7 %all-to-all-start = ((f32[256,13,1,128]{3,2,1,0:T(1,128)}), f32[256,13,1,128]{3,2,1,0:T(1,128)S(1)}, u32[]{:S(2)}, u32[]{:S(2)}) async-start(f32[256,13,1,128]{3,2,1,0:T(1,128)} %bitcast.36), calls=%async_computation | async-start | bytes 3407872 | tf_op jit(solution)/shard_map/all_to_all | solution.py:598
  17.4 44.7 %copy-start.1 = (f32[256,128]{1,0:T(8,128)S(1)}, f32[256,128]{1,0:T(8,128)}, u32[]{:S(2)}) copy-start(f32[256,128]{1,0:T(8,128)} %constant.45.clone.refs_6_.refs_9_.refs_14_) | copy-start | bytes 393220
  62.1 1.1 copy-start.3
  63.2 23.0 %copy-start.10 = (f32[512,1]{1,0:T(8,128)S(1)}, f32[512,1]{1,0:T(8,128)}, u32[]{:S(2)}) copy-start(f32[512,1]{1,0:T(8,128)} %constant.51.clone.refs_8_) | copy-start | bytes 6148
  63.2 23.0 %copy-start.11 = (bf16[512,192]{1,0:T(8,128)(2,1)S(1)}, bf16[512,192]{1,0:T(8,128)(2,1)}, u32[]{:S(2)}) copy-start(bf16[512,192]{1,0:T(8,128)(2,1)} %constant.48.clone.refs_5_) | copy-start | bytes 589828
  63.2 23.0 %copy-start.15 = (bf16[64,512]{1,0:T(8,128)(2,1)S(1)}, bf16[64,512]{1,0:T(8,128)(2,1)}, u32[]{:S(2)}) copy-start(bf16[64,512]{1,0:T(8,128)(2,1)} %constant.50.clone.refs_7_) | copy-start | bytes 196612
  63.2 23.0 %copy-start.16 = (bf16[64,512]{1,0:T(8,128)(2,1)S(1)}, bf16[64,512]{1,0:T(8,128)(2,1)}, u32[]{:S(2)}) copy-start(bf16[64,512]{1,0:T(8,128)(2,1)} %constant.49.clone.refs_6_) | copy-start | bytes 196612
  63.2 2.5 %collective-permute-start = (f32[768,128]{1,0:T(8,128)S(1)}, f32[768,128]{1,0:T(8,128)S(1)}, u32[]{:S(2)}, u32[]{:S(2)}) collective-permute-start(f32[768,128]{1,0:T(8,128)S(1)} %get-tuple-element.31), channel_id=1, source_target_pairs={{0,1},{1,0},{2,3},{3,2},{4,5},{5,4},{6,7},{7,6},{8,9},{9,8},{10,11... | collective-permute-start | bytes 1179656 | tf_op jit(solution)/shard_map/ppermute | solution.py:638
  65.8 21.2 %copy-start.13 = (f32[384,128]{1,0:T(8,128)}, f32[384,128]{1,0:T(8,128)S(1)}, u32[]{:S(2)}) copy-start(f32[384,128]{1,0:T(8,128)S(1)} %get-tuple-element.33.refs_5_) | copy-start | bytes 589828
  65.8 49.1 %copy-start = (f32[1,3,131072]{2,0,1:T(1,128)S(1)}, f32[1,3,131072]{2,0,1:T(1,128)}, u32[]{:S(2)}) copy-start(f32[1,3,131072]{2,0,1:T(1,128)} %param.17) | copy-start | bytes 4718596
  65.8 49.1 %copy-start.2 = (f32[131072]{0:T(1024)S(1)}, f32[131072]{0:T(1024)}, u32[]{:S(2)}) copy-start(f32[131072]{0:T(1024)} %param.18) | copy-start | bytes 1572868
  65.8 49.1 %copy-start.6 = (bf16[256,256]{1,0:T(8,128)(2,1)S(1)}, bf16[256,256]{1,0:T(8,128)(2,1)}, u32[]{:S(2)}) copy-start(bf16[256,256]{1,0:T(8,128)(2,1)} %constant.44.clone.refs_6_.refs_11_) | copy-start | bytes 393220
  65.8 49.1 %copy-start.7 = (bf16[256,256]{1,0:T(8,128)(2,1)S(1)}, bf16[256,256]{1,0:T(8,128)(2,1)}, u32[]{:S(2)}) copy-start(bf16[256,256]{1,0:T(8,128)(2,1)} %constant.47.clone.refs_8_.refs_13_) | copy-start | bytes 393220
  65.8 49.1 %copy-start.8 = (bf16[256,256]{1,0:T(8,128)(2,1)S(1)}, bf16[256,256]{1,0:T(8,128)(2,1)}, u32[]{:S(2)}) copy-start(bf16[256,256]{1,0:T(8,128)(2,1)} %constant.46.clone.refs_7_.refs_12_) | copy-start | bytes 393220
  65.8 49.1 %copy-start.18 = (f32[32,128]{1,0:T(8,128)S(1)}, f32[32,128]{1,0:T(8,128)}, u32[]{:S(2)}) copy-start(f32[32,128]{1,0:T(8,128)} %get-tuple-element.36.refs_10_) | copy-start | bytes 49156
  87.0 18.8 %all-to-all-start.2 = ((f32[64,3,4,128]{3,2,1,0:T(4,128)}), f32[64,3,4,128]{3,2,1,0:T(4,128)S(1)}, u32[]{:S(2)}, u32[]{:S(2)}) async-start(f32[64,3,4,128]{3,2,1,0:T(4,128)} %bitcast.17), calls=%async_computation.2 | async-start | bytes 786432 | tf_op jit(solution)/shard_map/all_to_all | solution.py:660
  92.3 20.9 %collective-permute-start.3 = (f32[896,128]{1,0:T(8,128)}, f32[896,128]{1,0:T(8,128)S(1)}, u32[]{:S(2)}, u32[]{:S(2)}) collective-permute-start(f32[896,128]{1,0:T(8,128)} %get-tuple-element.37), channel_id=1, source_target_pairs={{0,1},{1,2},{2,3},{3,4},{4,5},{5,6},{6,7},{7,8},{8,9},{9,10},{10,1... | collective-permute-start | bytes 1376264 | tf_op jit(solution)/shard_map/ppermute | solution.py:618
  97.0 16.2 %collective-permute-start.4 = (f32[896,128]{1,0:T(8,128)}, f32[896,128]{1,0:T(8,128)}, u32[]{:S(2)}, u32[]{:S(2)}) collective-permute-start(f32[896,128]{1,0:T(8,128)} %get-tuple-element.38), channel_id=1, source_target_pairs={{1,0},{2,1},{3,2},{4,3},{5,4},{6,5},{7,6},{8,7},{9,8},{10,9},{11,1... | collective-permute-start | bytes 1376264 | tf_op jit(solution)/shard_map/ppermute | solution.py:619
  105.8 9.1 %collective-permute-start.2 = (f32[768,128]{1,0:T(8,128)S(1)}, f32[768,128]{1,0:T(8,128)S(1)}, u32[]{:S(2)}, u32[]{:S(2)}) collective-permute-start(f32[768,128]{1,0:T(8,128)S(1)} %bitcast.32), channel_id=1, source_target_pairs={{0,1},{1,0},{2,3},{3,2},{4,5},{5,4},{6,7},{7,6},{8,9},{9,8},{10,11... | collective-permute-start | bytes 1179656 | tf_op jit(solution)/shard_map/ppermute | solution.py:662
  113.2 1.7 %collective-permute-start.1 = (f32[384,128]{1,0:T(8,128)}, f32[384,128]{1,0:T(8,128)S(1)}, u32[]{:S(2)}, u32[]{:S(2)}) collective-permute-start(f32[384,128]{1,0:T(8,128)} %copy-done.13), channel_id=1, source_target_pairs={{0,1},{1,0},{2,3},{3,2},{4,5},{5,4},{6,7},{7,6},{8,9},{9,8},{10,11... | collective-permute-start | bytes 589832 | tf_op jit(solution)/shard_map/ppermute | solution.py:647
  114.9 1.4 copy-start.4
  116.3 1.2 copy-start.5
  117.6 0.9 copy-start.14
  122.4 30.3 %copy-start.9 = (f32[128,128]{1,0:T(8,128)S(1)}, f32[128,128]{1,0:T(8,128)}, u32[]{:S(2)}) copy-start(f32[128,128]{1,0:T(8,128)} %refs_7_.4) | copy-start | bytes 196612
  122.4 30.3 %copy-start.12 = (f32[3,16,8,128]{3,2,1,0:T(8,128)S(1)}, f32[3,16,8,128]{3,2,1,0:T(8,128)}, u32[]{:S(2)}) copy-start(f32[3,16,8,128]{3,2,1,0:T(8,128)} %get-tuple-element.40.refs_5_) | copy-start | bytes 589828
  122.4 30.3 %copy-start.17 = (f32[3,16,128]{2,1,0:T(8,128)S(1)}, f32[3,16,128]{2,1,0:T(8,128)}, u32[]{:S(2)}) copy-start(f32[3,16,128]{2,1,0:T(8,128)} %get-tuple-element.41.refs_6_) | copy-start | bytes 73732
  140.3 8.5 %collective-permute-start.5 = (f32[48,128]{1,0:T(8,128)S(1)}, f32[48,128]{1,0:T(8,128)S(1)}, u32[]{:S(2)}, u32[]{:S(2)}) collective-permute-start(f32[48,128]{1,0:T(8,128)S(1)} %get-tuple-element.43), channel_id=1, source_target_pairs={{128,0},{129,1},{130,2},{131,3},{132,4},{133,5},{134,6},{135,7},{1... | collective-permute-start | bytes 73736 | tf_op jit(solution)/shard_map/ppermute | solution.py:705
  141.6 8.5 %collective-permute-start.6 = (f32[48,128]{1,0:T(8,128)S(1)}, f32[48,128]{1,0:T(8,128)S(1)}, u32[]{:S(2)}, u32[]{:S(2)}) collective-permute-start(f32[48,128]{1,0:T(8,128)S(1)} %get-tuple-element.44), channel_id=1, source_target_pairs={{128,8},{129,9},{130,10},{131,11},{132,12},{133,13},{134,14},{135,... | collective-permute-start | bytes 73736 | tf_op jit(solution)/shard_map/ppermute | solution.py:705
  142.9 8.3 %collective-permute-start.7 = (f32[48,128]{1,0:T(8,128)S(1)}, f32[48,128]{1,0:T(8,128)S(1)}, u32[]{:S(2)}, u32[]{:S(2)}) collective-permute-start(f32[48,128]{1,0:T(8,128)S(1)} %get-tuple-element.45), channel_id=1, source_target_pairs={{128,24},{129,25},{130,26},{131,27},{132,28},{133,29},{134,30},{13... | collective-permute-start | bytes 73736 | tf_op jit(solution)/shard_map/ppermute | solution.py:705
  144.2 8.5 %collective-permute-start.8 = (f32[48,128]{1,0:T(8,128)S(1)}, f32[48,128]{1,0:T(8,128)S(1)}, u32[]{:S(2)}, u32[]{:S(2)}) collective-permute-start(f32[48,128]{1,0:T(8,128)S(1)} %get-tuple-element.46), channel_id=1, source_target_pairs={{128,16},{129,17},{130,18},{131,19},{132,20},{133,21},{134,22},{13... | collective-permute-start | bytes 73736 | tf_op jit(solution)/shard_map/ppermute | solution.py:705
